TPU v7x, 512 devices: a whole 4x4x16 slice. The times are simulated.
512 devices in a mesh: az: 8 (over z_lo), rz: 64 (over x, z_hi, y, core).
Axes of the slice: x: 4, y: 4, z: 16 (z_hi: 2, z_lo: 8; z = z_hi * 8 + z_lo), core: 2. Of those that a mesh axis runs over, the one named last changes fastest.
Arguments:
- positions: float32 [3, 2097152], P(None, ('az', 'rz')), may hold values from -32 to 72, as said below
- velocities: float32 [3, 2097152], P(None, ('az', 'rz')), may hold values from -6 to 6
- masses: bfloat16 [2097152], P(('az', 'rz')), may hold values from 0.5 to 2
- cells: int32 [2097152], P(('az', 'rz')), may hold values from 0 to 16383
- active: int32 [2097152], P(('az', 'rz')), may hold values 0 or 1
- send_lists: int32 [2, 131072], P(None, ('az', 'rz')), may hold values from 0 to 4095, as said below
- send_counts: int32 [2, 512], P(None, ('az', 'rz')), may hold values from 1 to 256, as said below
Outputs:
- potential: float32 [64, 64, 2048], P(None, 'rz', 'az')
- star_state: float32 [6, 2097152], P(None, ('az', 'rz'))
- arrivals: float32 [2, 7, 131072], P(None, None, ('az', 'rz'))
Inputs may be any that keep to these rules, and one draw needn't show every extreme that they name: `positions`: row 0 is a radius between 8 and 72, row 1 an angle between 0 and 2 pi, row 2 a height between -32 and 32. `send_lists`: the two lists of a block name 512 different stars of that block, as indices within the block. `send_counts`: in each list row some block uses all 256 entries.
All inputs are finite; a program needn't handle non-finite values. No bound on the sum of `active` on one device may be relied on, other than what follows from the above.
Results may differ from a plain program's by a relative error of at most 0.0003.
Values sent between devices are 32-bit elements; how exact they have to be, the bound alone decides.
No kernel may reach another device: no remote copies, remote signals or barrier semaphores. Data moves between devices by JAX's collectives and lax.ppermute only.
A program may use at most 128 MiB of HBM per device.

v0:
```python
import math

import jax
import jax.numpy as jnp
from jax import lax
from jax.sharding import PartitionSpec as P

HEIGHTS = 64
AZIM = 2048
R_DEV = 1


two_pi = 2.0 * math.pi
inner_radius = 8.0
gravity = 1.0
time_step = 1.0


def prefix_2(value, axis, combine, identity, reverse):
    count, place = (lax.axis_size(axis), lax.axis_index(axis))
    everything = jax.tree.map(lambda part: lax.all_gather(part, axis), value)
    start = jax.tree.map(
        lambda part, zero: jnp.broadcast_to(jnp.asarray(zero, part.dtype), part.shape),
        value,
        identity,
    )

    def lap(k, before):
        at = count - 1 - k if reverse else k
        reached = at > place if reverse else at < place
        new = combine(before, jax.tree.map(lambda part: part[at], everything))
        return jax.tree.map(lambda a, b: jnp.where(reached, a, b), new, before)

    return lax.fori_loop(0, count, lap, start)


def with_halo(cells, sides, width):
    for axis, dim in sides:
        count = lax.axis_size(axis)
        head = lax.slice_in_dim(cells, 0, width, axis=dim)
        tail = lax.slice_in_dim(cells, cells.shape[dim] - width, cells.shape[dim], axis=dim)
        cells = jnp.concatenate(
            [
                lax.ppermute(tail, axis, [(i, (i + 1) % count) for i in range(count)]),
                cells,
                lax.ppermute(head, axis, [((i + 1) % count, i) for i in range(count)]),
            ],
            axis=dim,
        )
    return cells


def cas_table(first, second, total):
    turns = first[:, None] * second[None, :] % total
    theta = turns.astype(jnp.float32) * (two_pi / total)
    return jnp.cos(theta) + jnp.sin(theta)


def slope_table(modes, angles, total):
    turns = modes[:, None] * angles[None, :] % total
    theta = turns.astype(jnp.float32) * (two_pi / total)
    signed = jnp.where(2 * modes < total, modes, modes - total)
    signed = jnp.where(2 * modes == total, 0, signed).astype(jnp.float32)
    return signed[:, None] * (jnp.cos(theta) - jnp.sin(theta))


def sine_table(count):
    levels = jnp.arange(count, dtype=jnp.int32) + 1
    turns = levels[:, None] * levels[None, :] % (2 * (count + 1))
    return math.sqrt(2.0 / (count + 1)) * jnp.sin(
        turns.astype(jnp.float32) * (math.pi / (count + 1))
    )


def vertical_eigen(count):
    levels = jnp.arange(count, dtype=jnp.int32).astype(jnp.float32) + 1.0
    return (2.0 * jnp.sin(levels * (math.pi / (2 * (count + 1))))) ** 2


def compose(first, second):
    return jnp.sum(first[:, :, None] * second[None, :, :], axis=1)


def normalize(matrix):
    return matrix / jnp.max(jnp.abs(matrix), axis=(0, 1), keepdims=True)


def chain_forward(earlier, later):
    return normalize(compose(later, earlier))


def chain_backward(earlier, later):
    return (later[0] + later[1] * earlier[0], later[1] * earlier[1])


def radial_solve(source, radii, modes, eigen):
    plane_shape = (source.shape[0], source.shape[2])
    zeros_plane = jnp.zeros(plane_shape, jnp.float32)
    ones_plane = jnp.ones(plane_shape, jnp.float32)
    mapping = None
    level = 0
    radius = radii[level]
    lower = -(radius - 0.5) / radius
    upper = -(radius + 0.5) / radius
    diagonal = 2.0 + (modes * modes)[None, :] / (radius * radius) + eigen[:, None]
    lowers = [lower]
    uppers = [upper]
    diagonals = [diagonal]
    matrix = jnp.stack(
        [
            jnp.stack([-lower * ones_plane, zeros_plane, source[:, level]]),
            jnp.stack([zeros_plane, zeros_plane, upper * ones_plane]),
            jnp.stack([zeros_plane, -lower * ones_plane, diagonal]),
        ]
    )
    mapping = normalize(matrix)
    identity = jnp.broadcast_to(jnp.eye(3, dtype=jnp.float32)[:, :, None, None], mapping.shape)
    prefix = prefix_2(mapping, "rz", chain_forward, identity, False)
    factor_in = prefix[1, 2] / prefix[2, 2]
    value_in = prefix[0, 2] / prefix[2, 2]
    factor_prev = factor_in
    value_prev = value_in
    level = 0
    denom = diagonals[level] - lowers[level] * factor_prev
    factor_prev = uppers[level] / denom
    value_prev = (source[:, level] - lowers[level] * value_prev) / denom
    factors = [factor_prev]
    values = [value_prev]
    offset_map = zeros_plane
    scale_map = ones_plane
    level = 0
    offset_map = values[level] - factors[level] * offset_map
    scale_map = -factors[level] * scale_map
    beyond = prefix_2(
        (offset_map, scale_map), "rz", chain_backward, (zeros_plane, ones_plane), True
    )
    next_first = beyond[0]
    solved = [None] * R_DEV
    later_value = next_first
    level = 0
    later_value = values[level] - factors[level] * later_value
    solved[level] = later_value
    spectral = jnp.stack(solved, axis=1)
    previous_last = value_in - factor_in * solved[0]
    return (spectral, previous_last, next_first)


def per_device(positions, velocities, masses, cells, active, send_lists, send_counts):
    highest = lax.Precision.HIGHEST
    sector = AZIM // lax.axis_size("az")
    stack_rows = HEIGHTS * R_DEV
    stars = masses.shape[0]
    group_size = min(stars, 2048)
    groups = stars // group_size
    layer_of = cells // sector
    angle_of = cells % sector
    layer_ids = jnp.arange(stack_rows, dtype=jnp.int32)
    angle_ids = jnp.arange(sector, dtype=jnp.int32)

    def deposit(running, bundle):
        layer_rows, angle_rows, weights = bundle
        left_hot = (layer_rows[:, None] == layer_ids[None, :]).astype(jnp.bfloat16)
        right_hot = jnp.where(angle_rows[:, None] == angle_ids[None, :], weights[:, None], 0)
        added = lax.dot_general(
            left_hot, right_hot, (((0,), (0,)), ((), ())), preferred_element_type=jnp.float32
        )
        return (running + added, None)

    density, ignored = lax.scan(
        deposit,
        jnp.zeros((stack_rows, sector), jnp.float32),
        (
            layer_of.reshape(groups, group_size),
            angle_of.reshape(groups, group_size),
            masses.reshape(groups, group_size),
        ),
    )
    sine = sine_table(HEIGHTS)
    layered = jnp.dot(sine, density, precision=highest).reshape(HEIGHTS, R_DEV, sector)
    own_angles = lax.axis_index("az") * sector + angle_ids
    radii = (
        inner_radius
        + (lax.axis_index("rz") * R_DEV + jnp.arange(R_DEV, dtype=jnp.int32)).astype(jnp.float32)
        + 0.5
    )
    empty_field = jnp.zeros((HEIGHTS, R_DEV, sector), jnp.float32)
    portion = lax.all_gather(layered, "az", axis=2, tiled=True)
    count = portion.shape[2]
    table = cas_table(jnp.arange(count, dtype=jnp.int32), own_angles, AZIM)
    added = jnp.dot(portion.reshape(stack_rows, count), table, precision=highest)
    spectrum = added.reshape(empty_field.shape)
    modes = jnp.minimum(own_angles, AZIM - own_angles).astype(jnp.float32)
    eigen = vertical_eigen(HEIGHTS)
    spectral, previous_last, next_first = radial_solve(-gravity * spectrum, radii, modes, eigen)
    potential_layers = jnp.dot(
        sine, spectral.reshape(HEIGHTS, R_DEV * sector), precision=highest
    ).reshape(HEIGHTS, R_DEV, sector)
    extended = jnp.concatenate([previous_last[:, None], spectral, next_first[:, None]], axis=1)
    slope_modes = (extended[:, 2:] - extended[:, :-2]) * 0.5
    slope_layers = jnp.dot(
        sine, slope_modes.reshape(HEIGHTS, R_DEV * sector), precision=highest
    ).reshape(HEIGHTS, R_DEV, sector)
    running = (empty_field, empty_field, empty_field)
    portions = (
        lax.all_gather(potential_layers, "az", axis=2, tiled=True),
        lax.all_gather(slope_layers, "az", axis=2, tiled=True),
    )
    count = portions[0].shape[2]
    mode_ids = jnp.arange(count, dtype=jnp.int32)
    cas_part = cas_table(mode_ids, own_angles, AZIM)
    slope_part = slope_table(mode_ids, own_angles, AZIM)
    flat_potential = portions[0].reshape(stack_rows, count)
    flat_slope = portions[1].reshape(stack_rows, count)
    potential = (
        running[0] + jnp.dot(flat_potential, cas_part, precision=highest).reshape(running[0].shape)
    ) / AZIM
    radial = (
        running[1] + jnp.dot(flat_slope, cas_part, precision=highest).reshape(running[1].shape)
    ) / AZIM
    angular = (
        running[2]
        + jnp.dot(flat_potential, slope_part, precision=highest).reshape(running[2].shape)
    ) / AZIM
    padded = jnp.pad(potential, ((1, 1), (0, 0), (0, 0)))
    vertical = (padded[2:] - padded[:-2]) * 0.5
    fields = jnp.stack([radial, angular, vertical]).reshape(3, stack_rows * sector)
    sampled = jnp.take(fields, cells, axis=1)
    radius_now = positions[0]
    accel = jnp.stack([-sampled[0], -sampled[1] / radius_now, -sampled[2]])
    live = active.astype(jnp.float32)
    new_velocities = velocities + time_step * live[None, :] * accel
    motion = jnp.stack([new_velocities[0], new_velocities[1] / radius_now, new_velocities[2]])
    new_positions = positions + time_step * live[None, :] * motion
    star_state = jnp.concatenate([new_positions, new_velocities], axis=0)
    moving = jnp.concatenate([star_state, masses.astype(jnp.float32)[None, :]], axis=0)
    picked = moving[:, send_lists]
    slots = send_lists.shape[1]
    keep = (jnp.arange(slots, dtype=jnp.int32)[None, :] < send_counts).astype(jnp.float32)
    parcels = jnp.transpose(picked, (1, 0, 2)) * keep[:, None, :]
    arrived = with_halo(parcels, (("az", 0),), 1)
    arrivals = jnp.stack([arrived[0], arrived[3]])
    return (potential, star_state, arrivals)


def solution(mesh):
    return jax.shard_map(
        per_device,
        mesh=mesh,
        in_specs=(
            P(None, ("az", "rz")),
            P(None, ("az", "rz")),
            P(("az", "rz")),
            P(("az", "rz")),
            P(("az", "rz")),
            P(None, ("az", "rz")),
            P(None, ("az", "rz")),
        ),
        out_specs=(P(None, "rz", "az"), P(None, ("az", "rz")), P(None, None, ("az", "rz"))),
        check_vma=False,
    )
```

profile of v0, /device:TPU:8, one launch (start us, length us, event | category | flops | bytes accessed | tf_op | source)
XLA Modules:
  0.0 1121.8 jit_solution(6455352156629829451)
XLA Ops:
  8.9 2.9 while.43
  8.9 1.4 convolution_add_fusion.2
  10.4 1.4 convolution_add_fusion.2
  12.1 50.4 %all-gather = f32[64,2048]{1,0:T(8,128)S(1)} all-gather(f32[64,256]{1,0:T(8,128)S(1)} %fusion.73), channel_id=2, replica_groups=mesh['az'=8,'rz'=64] {'az'}, dimensions={1}, use_global_device_ids=true | all-gather | bytes 589824 | tf_op jit(solution)/shard_map/all_gather | solution.py:187
  62.7 9.5 convolution_multiply_fusion.2
  73.9 452.8 %all-gather.8.cloned.1.call-done = f32[64,3,3,64,256]{4,3,2,1,0:T(8,128)} async-done(((f32[1,3,3,64,256]{4,3,2,1,0:T(8,128)}), f32[64,3,3,64,256]{4,3,2,1,0:T(8,128)}) %all-gather.8.cloned.1.call-update) | async-done | bytes 37748752 | tf_op jit(solution)/shard_map/all_gather | solution.py:21
  526.9 94.1 %while.42 = (s32[]{:T(128)}, f32[3,3,64,256]{3,2,1,0:T(8,128)S(1)}, s32[]{:T(128)}, f32[64,3,3,64,256]{4,3,2,1,0:T(8,128)}, s32[]{:T(128)}) while((s32[]{:T(128)}, f32[3,3,64,256]{3,2,1,0:T(8,128)S(1)}, s32[]{:T(128)}, f32[64,3,3,64,256]{4,3,2,1,0:T(8,128)}, s32[]{:T(128)}) %tuple.116), condition=%wide.region_6.7_spmd, body=%wide.region_3.6_spmd.sunk | while | flops 1310723 | bytes 5439563 | solution.py:34
  526.9 1.1 dynamic-slice_bitcast_fusion.2
  528.4 1.1 dynamic-slice_bitcast_fusion.2
  529.9 1.1 dynamic-slice_bitcast_fusion.2
  531.3 1.1 dynamic-slice_bitcast_fusion.2
  532.8 1.1 dynamic-slice_bitcast_fusion.2
  534.3 1.1 dynamic-slice_bitcast_fusion.2
  535.7 1.1 dynamic-slice_bitcast_fusion.2
  537.2 1.1 dynamic-slice_bitcast_fusion.2
  538.7 1.1 dynamic-slice_bitcast_fusion.2
  540.1 1.1 dynamic-slice_bitcast_fusion.2
  541.6 1.1 dynamic-slice_bitcast_fusion.2
  543.1 1.1 dynamic-slice_bitcast_fusion.2
  544.6 1.1 dynamic-slice_bitcast_fusion.2
  546.0 1.1 dynamic-slice_bitcast_fusion.2
  547.5 1.1 dynamic-slice_bitcast_fusion.2
  549.0 1.1 dynamic-slice_bitcast_fusion.2
  550.4 1.1 dynamic-slice_bitcast_fusion.2
  551.9 1.1 dynamic-slice_bitcast_fusion.2
  553.4 1.1 dynamic-slice_bitcast_fusion.2
  554.8 1.1 dynamic-slice_bitcast_fusion.2
  556.3 1.1 dynamic-slice_bitcast_fusion.2
  557.8 1.1 dynamic-slice_bitcast_fusion.2
  559.3 1.1 dynamic-slice_bitcast_fusion.2
  560.7 1.1 dynamic-slice_bitcast_fusion.2
  562.2 1.1 dynamic-slice_bitcast_fusion.2
  563.7 1.1 dynamic-slice_bitcast_fusion.2
  565.1 1.1 dynamic-slice_bitcast_fusion.2
  566.6 1.1 dynamic-slice_bitcast_fusion.2
  568.1 1.1 dynamic-slice_bitcast_fusion.2
  623.4 140.8 %all-gather.12.cloned.1.call-done = f32[4096,256]{1,0:T(8,128)} async-done(((f32[64,256]{1,0:T(8,128)}), f32[4096,256]{1,0:T(8,128)}) %all-gather.12.cloned.1.call-update) | async-done | bytes 4194320 | tf_op jit(solution)/shard_map/all_gather | solution.py:21
  764.3 127.7 %all-gather.10.cloned.1.call-done = f32[64,64,256]{2,1,0:T(8,128)} async-done(((f32[1,64,256]{2,1,0:T(8,128)}), f32[64,64,256]{2,1,0:T(8,128)}) %all-gather.10.cloned.1.call-update) | async-done | bytes 4194320 | tf_op jit(solution)/shard_map/all_gather | solution.py:21
  891.9 60.4 %while.44 = (s32[]{:T(128)}, f32[64,256]{1,0:T(8,128)S(1)}, s32[]{:T(128)}, f32[64,64,256]{2,1,0:T(8,128)}, f32[64,64,256]{2,1,0:T(8,128)}, /*index=5*/s32[]{:T(128)}, s32[]{:T(128)}, s32[]{:T(128)}, s32[]{:T(128)}) while((s32[]{:T(128)}, f32[64,256]{1,0:T(8,128)S(1)}, s32[]{:T(128)}, f32[64,64,256]{2,1,0:T(8,128)}, ...), condition=%wide.region_8.9_spmd.clone, body=%wide.region_7.8_spmd.clone.sunk | while | flops 65544 | bytes 262307 | solution.py:34
  953.1 47.9 %all-gather.3 = f32[64,2048]{1,0:T(8,128)S(1)} all-gather(f32[64,256]{1,0:T(8,128)S(1)} %fusion.55), channel_id=5, replica_groups=mesh['az'=8,'rz'=64] {'az'}, dimensions={1}, use_global_device_ids=true | all-gather | bytes 589824 | tf_op jit(solution)/shard_map/all_gather | solution.py:206
  1001.1 9.5 fusion.28
  1010.6 48.2 %all-gather.2 = f32[64,2048]{1,0:T(8,128)S(1)} all-gather(f32[64,256]{1,0:T(8,128)S(1)} %fusion.69), channel_id=4, replica_groups=mesh['az'=8,'rz'=64] {'az'}, dimensions={1}, use_global_device_ids=true | all-gather | bytes 589824 | tf_op jit(solution)/shard_map/all_gather | solution.py:205
  1058.8 9.5 fusion.29
  1068.4 9.8 fusion.25
  1078.5 5.1 copy.73
  1083.6 14.2 %gather_fusion = f32[4096,3]{1,0:T(8,128)S(1)} fusion(f32[3,16384]{0,1:T(8,128)} %copy.73, s32[4096]{0:T(1024)S(1)} %get-tuple-element.407), kind=kCustom, calls=%fused_computation | custom fusion | bytes 114688 | tf_op jit(solution)/shard_map/jit(_take)/gather | solution.py:227
  1100.6 1.9 collective-permute-start
  1102.5 10.5 collective-permute-start.1
  (372 shorter events, 130.2 us)
Async XLA Ops:
  7.2 519.6 %all-gather.8.cloned.1.call-start = ((), (), s32[]{:S(2)}) async-start(), calls=%async_computation | async-start | bytes 38338560 | tf_op jit(solution)/shard_map/all_gather | solution.py:21
  73.4 690.8 %all-gather.12.cloned.1.call-start = ((), (), s32[]{:S(2)}) async-start(), calls=%async_computation.2 | async-start | bytes 4259840 | tf_op jit(solution)/shard_map/all_gather | solution.py:21
  526.8 96.4 %copy-start.3 = (bf16[4096]{0:T(1024)(128)(2,1)S(1)}, bf16[4096]{0:T(1024)(128)(2,1)}, u32[]{:S(2)}) copy-start(bf16[4096]{0:T(1024)(128)(2,1)} %param.15) | copy-start | bytes 24580
  526.8 96.4 %copy-start.4 = (s32[4096]{0:T(1024)S(1)}, s32[4096]{0:T(1024)}, u32[]{:S(2)}) copy-start(s32[4096]{0:T(1024)} %param.17) | copy-start | bytes 49156
  526.9 96.4 %copy-start.5 = (s32[2,256]{1,0:T(2,128)S(1)}, s32[2,256]{1,0:T(2,128)}, u32[]{:S(2)}) copy-start(s32[2,256]{1,0:T(2,128)} %param.18) | copy-start | bytes 6148
  526.9 96.4 %copy-start.6 = (s32[2,1]{0,1:T(1,128)S(1)}, s32[2,1]{0,1:T(1,128)}, u32[]{:S(2)}) copy-start(s32[2,1]{0,1:T(1,128)} %param.19) | copy-start | bytes 28
  526.9 96.5 %copy-start.2 = (s32[4096]{0:T(1024)S(1)}, s32[4096]{0:T(1024)}, u32[]{:S(2)}) copy-start(s32[4096]{0:T(1024)} %param.16) | copy-start | bytes 49156
  622.5 269.5 %all-gather.10.cloned.1.call-start = ((), (), s32[]{:S(2)}) async-start(), calls=%async_computation.1 | async-start | bytes 4259840 | tf_op jit(solution)/shard_map/all_gather | solution.py:21
  1083.6 14.9 %copy-start = (f32[3,4096]{1,0:T(4,128)S(1)}, f32[3,4096]{1,0:T(4,128)}, u32[]{:S(2)}) copy-start(f32[3,4096]{1,0:T(4,128)} %param.13) | copy-start | bytes 147460
  1083.6 14.9 %copy-start.1 = (f32[3,4096]{1,0:T(4,128)S(1)}, f32[3,4096]{1,0:T(4,128)}, u32[]{:S(2)}) copy-start(f32[3,4096]{1,0:T(4,128)} %param.14) | copy-start | bytes 147460
  1100.6 13.8 %collective-permute-start = (f32[1,7,256]{2,0,1:T(1,128)S(1)}, f32[1,7,256]{2,0,1:T(1,128)S(1)}, u32[]{:S(2)}, u32[]{:S(2)}) collective-permute-start(f32[1,7,256]{2,0,1:T(1,128)S(1)} %get-tuple-element.410), channel_id=1, source_target_pairs={{0,64},{64,128},{128,192},{192,256},{256,320},{320,384},{384,448},... | collective-permute-start | bytes 21512 | tf_op jit(solution)/shard_map/ppermute | solution.py:44
  1102.5 11.9 %collective-permute-start.1 = (f32[1,7,256]{2,0,1:T(1,128)S(1)}, f32[1,7,256]{2,0,1:T(1,128)S(1)}, u32[]{:S(2)}, u32[]{:S(2)}) collective-permute-start(f32[1,7,256]{2,0,1:T(1,128)S(1)} %get-tuple-element.411), channel_id=1, source_target_pairs={{64,0},{128,64},{192,128},{256,192},{320,256},{384,320},{448,384},... | collective-permute-start | bytes 21512 | tf_op jit(solution)/shard_map/ppermute | solution.py:46
Sparse Core Ops, SparseCore 0:
  73.5 453.1 all-gather.7
  622.6 141.6 all-gather.11
  769.4 122.4 all-gather.9
where the time goes:
time: 1140 us; the launch traced here: 1120 us
  waiting for transfers between devices  722 us (63%)
  blocking collectives  147 us (13%)
  local copies, waits for them, and re-layouts  94.6 us (8%)
  other arithmetic  84.4 us (7%)
  matrix products  42.2 us (4%)
  between operations  14.5 us (1%)
  starting transfers between devices  13 us (1%)
    all_gather x3, waiting for transfers between devices, prefix_2(): everything = jax.tree.map(lambda part: lax.all_gather(part, axis), value)  721 us
    mul x64, local copies, waits for them, and re-layouts, compose(): return jnp.sum(first[:, :, None] * second[None, :, :], axis=1)  70.8 us
    select_n x128, other arithmetic, lap(): return jax.tree.map(lambda a, b: jnp.where(reached, a, b), new, before)  67 us
    all_gather x1, blocking collectives, per_device(): portion = lax.all_gather(layered, 'az', axis=2, tiled=True)  50.4 us
    all_gather x1, blocking collectives, per_device(): lax.all_gather(potential_layers, 'az', axis=2, tiled=True)  48.2 us
    all_gather x1, blocking collectives, per_device(): lax.all_gather(slope_layers, 'az', axis=2, tiled=True)  47.9 us
  transfers between devices with their start and end apart: 5, of which 3 were waited for; matrix products, arithmetic and copies ran while one was open for 0% of the time, Pallas kernels for 0%

commit v1 on v0

v1 whole, which is shorter than its diff:
```python
import functools
import math

import jax
import jax.numpy as jnp
import numpy as np
from jax import lax
from jax.experimental import pallas as pl
from jax.experimental.pallas import tpu as pltpu
from jax.sharding import Mesh
from jax.sharding import PartitionSpec as P

HEIGHTS = 64
RADII = 64
AZIM = 2048
SECTOR = 256
STARS = 4096
CAP = 256
CHUNK = 512
INNER = 8.0

F32 = jnp.float32
BF16 = jnp.bfloat16


def _split_np(table):
    high = np.asarray(table, np.float32).astype(jnp.bfloat16)
    low = (np.asarray(table, np.float64) - high.astype(np.float64)).astype(np.float32).astype(jnp.bfloat16)
    return high, low


def _sine():
    levels = np.arange(HEIGHTS) + 1
    turns = levels[:, None] * levels[None, :] % (2 * (HEIGHTS + 1))
    return math.sqrt(2.0 / (HEIGHTS + 1)) * np.sin(turns * (math.pi / (HEIGHTS + 1)))


def _trig():
    ids = np.arange(SECTOR)
    theta = (ids[:, None] * ids[None, :] % SECTOR) * (2.0 * math.pi / SECTOR)
    return np.cos(theta), np.sin(theta)


def _twist():
    residues = np.arange(8)
    angles = np.arange(AZIM)
    theta = (residues[:, None] * angles[None, :] % AZIM) * (2.0 * math.pi / AZIM)
    plus = np.cos(theta) + np.sin(theta)
    minus = np.cos(theta) - np.sin(theta)
    return plus.reshape(64, SECTOR).astype(np.float32), minus.reshape(64, SECTOR).astype(np.float32)


def _field_table():
    sine = _sine()
    shifted = np.zeros((HEIGHTS, HEIGHTS))
    shifted[:-1] += sine[1:]
    shifted[1:] -= sine[:-1]
    vertical = 0.5 * shifted
    table = np.zeros((4, HEIGHTS, 16, 3, 4))
    by_group = sine.reshape(HEIGHTS, 16, 4)
    table[0, :, :, 0, :] = by_group
    table[1, :, :, 1, :] = -by_group
    table[2, :, :, 2, :] = -by_group
    table[3, :, :, 0, :] = -vertical.reshape(HEIGHTS, 16, 4)
    return table.reshape(4 * HEIGHTS, 192) / AZIM


def _eigen():
    levels = np.arange(HEIGHTS) + 1.0
    return ((2.0 * np.sin(levels * (math.pi / (2 * (HEIGHTS + 1))))) ** 2).astype(np.float32)


def _row_of(radius):
    x, zh, y, c = radius >> 4, (radius >> 3) & 1, (radius >> 1) & 3, radius & 1
    return (((x * 4 + y) * 2 + c) * 2) + zh


def _split(value):
    high = value.astype(BF16)
    low = (value - high.astype(F32)).astype(BF16)
    return high, low


def _dot(a, b):
    return jnp.dot(a, b, preferred_element_type=F32)


def _dot3(a, b):
    (a_high, a_low), (b_high, b_low) = a, b
    return _dot(a_high, b_high) + (_dot(a_low, b_high) + _dot(a_high, b_low))


def _one_hot(ids, rows):
    lanes = ids.shape[1]
    here = lax.broadcasted_iota(jnp.int32, (rows, lanes), 0) == ids
    return jnp.where(here, 1.0, 0.0).astype(BF16)


def deposit_kernel(cells_ref, mass_ref, sine_high_ref, sine_low_ref, out_ref):
    total = jnp.zeros((HEIGHTS, SECTOR), F32)
    for start in range(0, STARS, CHUNK):
        cell = cells_ref[:, start : start + CHUNK]
        mass = mass_ref[:, start : start + CHUNK]
        layer = lax.shift_right_logical(cell, 8)
        angle = cell & 255
        here = lax.broadcasted_iota(jnp.int32, (HEIGHTS, CHUNK), 0) == layer
        left = jnp.where(here, mass, 0.0).astype(BF16)
        right = _one_hot(angle, SECTOR)
        total += lax.dot_general(
            left, right, (((1,), (1,)), ((), ())), preferred_element_type=F32
        )
    out_ref[...] = _dot3((sine_high_ref[...], sine_low_ref[...]), _split(total))


def forward_kernel(x_ref, plus_ref, minus_ref, high_ref, low_ref, out_ref):
    tiles = [x_ref[8 * a : 8 * a + 8, :] for a in range(8)]
    rows = []
    for n2 in range(8):
        even = tiles[0] * plus_ref[8 * n2 : 8 * n2 + 1, :]
        odd = tiles[0] * minus_ref[8 * n2 : 8 * n2 + 1, :]
        for a in range(1, 8):
            at = 8 * n2 + a
            even += tiles[a] * plus_ref[at : at + 1, :]
            odd += tiles[a] * minus_ref[at : at + 1, :]
        rows.append(jnp.concatenate([even, odd], axis=1))
    left = _split(jnp.concatenate(rows, axis=0))
    result = _dot3(left, (high_ref[...], low_ref[...]))
    for n2 in range(8):
        for k in range(4):
            for zh in range(2):
                at = n2 * 8 + zh * 4 + k
                spot = n2 * 8 + k * 2 + zh
                out_ref[spot : spot + 1, :] = result[at : at + 1, :]


def factor_kernel(eigen_ref, inverse_ref, carry_ref, factor_ref, joint_ref):
    group = lax.axis_index("az") * 2 + lax.axis_index("zh")
    place = (lax.axis_index("x") * 4 + lax.axis_index("y")) * 2 + lax.axis_index("c")
    level = group * 4 + lax.rem(place, 4)
    residue = lax.div(place, 4)
    eigen = eigen_ref[level]
    mode = lax.broadcasted_iota(jnp.int32, (1, SECTOR), 1) * 8 + residue
    mode = jnp.minimum(mode, AZIM - mode).astype(F32)
    square = mode * mode
    top = None
    bottom = None
    for step in range(RADII // 2):
        i = step
        radius = INNER + i + 0.5
        lower = -(radius - 0.5) / radius
        upper = -(radius + 0.5) / radius
        denom = (2.0 + eigen) + square * (1.0 / (radius * radius))
        if top is not None:
            denom = denom - lower * top
        inverse = 1.0 / denom
        top = upper * inverse
        row = _row_of(i)
        inverse_ref[row : row + 1, :] = -inverse
        carry_ref[row : row + 1, :] = -lower * inverse
        factor_ref[row : row + 1, :] = -top
        i = RADII - 1 - step
        radius = INNER + i + 0.5
        lower = -(radius - 0.5) / radius
        upper = -(radius + 0.5) / radius
        denom = (2.0 + eigen) + square * (1.0 / (radius * radius))
        if bottom is not None:
            denom = denom - upper * bottom
        inverse = 1.0 / denom
        bottom = lower * inverse
        row = _row_of(i)
        inverse_ref[row : row + 1, :] = -inverse
        carry_ref[row : row + 1, :] = -upper * inverse
        factor_ref[row : row + 1, :] = -bottom
    joint_ref[...] = jnp.broadcast_to(1.0 / (1.0 - top * bottom), (8, SECTOR))


def solve_kernel(source_ref, inverse_ref, carry_ref, factor_ref, joint_ref, out_ref, scaled_ref):
    half = RADII // 2
    scaled_ref[...] = source_ref[...] * inverse_ref[...]

    def at(ref, i):
        row = _row_of(i)
        return ref[row : row + 1, :]

    values = [None] * RADII
    values[0] = at(scaled_ref, 0)
    values[RADII - 1] = at(scaled_ref, RADII - 1)
    for step in range(1, half):
        i = step
        values[i] = at(scaled_ref, i) + at(carry_ref, i) * values[i - 1]
        i = RADII - 1 - step
        values[i] = at(scaled_ref, i) + at(carry_ref, i) * values[i + 1]
    solved = [None] * RADII
    solved[half - 1] = (values[half - 1] + at(factor_ref, half - 1) * values[half]) * joint_ref[0:1, :]
    solved[half] = values[half] + at(factor_ref, half) * solved[half - 1]
    for step in range(1, half):
        i = half - 1 - step
        solved[i] = values[i] + at(factor_ref, i) * solved[i + 1]
        i = half + step
        solved[i] = values[i] + at(factor_ref, i) * solved[i - 1]
    for i in range(RADII):
        row = _row_of(i)
        spot = (row >> 1) * 4 + (row & 1)
        out_ref[spot : spot + 1, :] = solved[i]
        if i == 0:
            slope = solved[1] * 0.5
        elif i == RADII - 1:
            slope = solved[RADII - 2] * -0.5
        else:
            slope = (solved[i + 1] - solved[i - 1]) * 0.5
        out_ref[spot + 2 : spot + 3, :] = slope


def inverse_kernel(x_ref, plus_ref, minus_ref, high_ref, low_ref, out_ref):
    fields = [[], [], []]
    for n2 in range(8):
        pair = []
        for field in range(2):
            spots = [n2 * 16 + k * 4 + field * 2 + zh for zh in range(2) for k in range(4)]
            pair.append(jnp.concatenate([x_ref[at : at + 1, :] for at in spots], axis=0))
        mode = lax.broadcasted_iota(jnp.int32, (8, SECTOR), 1) * 8 + n2
        signed = jnp.where(2 * mode < AZIM, mode, mode - AZIM)
        signed = jnp.where(2 * mode == AZIM, 0, signed).astype(F32)
        fields[0].append(pair[0])
        fields[1].append(pair[1])
        fields[2].append(pair[0] * signed)
    table = (high_ref[...], low_ref[...])
    for field in range(3):
        left = _split(jnp.concatenate(fields[field], axis=0))
        wave = _dot3(left, table)
        for a in range(8):
            total = None
            for n2 in range(8):
                even = wave[8 * n2 : 8 * n2 + 8, :SECTOR]
                odd = wave[8 * n2 : 8 * n2 + 8, SECTOR:]
                plus = plus_ref[8 * n2 + a : 8 * n2 + a + 1, :]
                minus = minus_ref[8 * n2 + a : 8 * n2 + a + 1, :]
                if field < 2:
                    term = even * plus + odd * minus
                else:
                    term = even * minus - odd * plus
                total = term if total is None else total + term
            for zh in range(2):
                spot = (a * 2 + zh) * 12 + field * 4
                out_ref[spot : spot + 4, :] = total[zh * 4 : zh * 4 + 4, :]


def pick_kernel(positions_ref, velocities_ref, mass_ref, cells_ref, active_ref, lists_ref, out_ref):
    wanted = jnp.concatenate([lists_ref[0:1, :], lists_ref[1:2, :]], axis=1)
    total = jnp.zeros((32, 2 * CAP), F32)
    for start in range(0, STARS, CHUNK):
        moving = jnp.concatenate(
            [positions_ref[:, start : start + CHUNK], velocities_ref[:, start : start + CHUNK]], axis=0
        )
        high = moving.astype(BF16).astype(F32)
        rest = moving - high
        middle = rest.astype(BF16).astype(F32)
        low = rest - middle
        cell = cells_ref[:, start : start + CHUNK]
        plain = jnp.concatenate(
            [
                mass_ref[:, start : start + CHUNK],
                lax.shift_right_logical(cell, 8).astype(F32),
                (cell & 255).astype(F32),
                active_ref[:, start : start + CHUNK].astype(F32),
                jnp.zeros((4, CHUNK), F32),
            ],
            axis=0,
        )
        pad = jnp.zeros((2, CHUNK), F32)
        left = jnp.concatenate([high, pad, middle, pad, low, pad, plain], axis=0).astype(BF16)
        ids = lax.broadcasted_iota(jnp.int32, (CHUNK, 2 * CAP), 0) + start
        hot = jnp.where(ids == wanted, 1.0, 0.0).astype(BF16)
        total += _dot(left, hot)
    out_ref[0:8, :] = (total[0:8] + total[8:16]) + total[16:24]
    out_ref[8:16, :] = total[24:32]


def _sample(fields, layer, angle):
    lanes = layer.shape[1]
    hot = _one_hot(angle, SECTOR)
    both = _dot(fields, hot)
    here = lax.broadcasted_iota(jnp.int32, (HEIGHTS, lanes), 0) == layer
    found = []
    for field in range(3):
        block = both[64 * field : 64 * field + 64] + both[192 + 64 * field : 256 + 64 * field]
        found.append(jnp.sum(jnp.where(here, block, 0.0), axis=0, keepdims=True))
    return found


def _advance(position, velocity, accel, live):
    radius = position[0]
    speed = [
        velocity[0] + live * accel[0],
        velocity[1] + live * (accel[1] / radius),
        velocity[2] + live * accel[2],
    ]
    place = [
        position[0] + live * speed[0],
        position[1] + live * (speed[1] / radius),
        position[2] + live * speed[2],
    ]
    return place + speed


def parcel_kernel(modes_ref, high_ref, low_ref, picked_ref, counts_ref, pot_ref, fields_ref, zero_ref, one_ref):
    result = _dot3((high_ref[...], low_ref[...]), _split(modes_ref[...]))
    pot_ref[...] = result[0:64]
    field_high, field_low = _split(result[64:256])
    fields = jnp.concatenate([field_high, field_low], axis=0)
    fields_ref[...] = fields
    picked = picked_ref[...]
    layer = picked[9:10].astype(jnp.int32)
    angle = picked[10:11].astype(jnp.int32)
    accel = _sample(fields, layer, angle)
    state = _advance(
        [picked[i : i + 1] for i in range(3)],
        [picked[i : i + 1] for i in range(3, 6)],
        accel,
        picked[11:12],
    )
    rows = jnp.concatenate(state + [picked[8:9]], axis=0)
    slots = lax.broadcasted_iota(jnp.int32, (7, CAP), 1)
    zero_ref[...] = jnp.where(slots < counts_ref[0:1, :], rows[:, :CAP], 0.0)
    one_ref[...] = jnp.where(slots < counts_ref[1:2, :], rows[:, CAP:], 0.0)


def stars_kernel(fields_ref, positions_ref, velocities_ref, cells_ref, active_ref, out_ref):
    fields = fields_ref[...]
    for start in range(0, STARS, CHUNK):
        lanes = slice(start, start + CHUNK)
        cell = cells_ref[:, lanes]
        accel = _sample(fields, lax.shift_right_logical(cell, 8), cell & 255)
        state = _advance(
            [positions_ref[i : i + 1, lanes] for i in range(3)],
            [velocities_ref[i : i + 1, lanes] for i in range(3)],
            accel,
            active_ref[:, lanes].astype(F32),
        )
        for row in range(6):
            out_ref[row : row + 1, lanes] = state[row]


def _call(kernel, out_shape, name, flops, in_smem=(), count=0, scratch=()):
    vmem = pl.BlockSpec(memory_space=pltpu.VMEM)
    smem = pl.BlockSpec(memory_space=pltpu.SMEM)
    outs = jax.tree.map(lambda _: vmem, out_shape)
    return pl.pallas_call(
        kernel,
        out_shape=out_shape,
        in_specs=[smem if i in in_smem else vmem for i in range(count)],
        out_specs=outs,
        scratch_shapes=list(scratch),
        name=name,
        cost_estimate=pl.CostEstimate(flops=flops, bytes_accessed=1 << 20, transcendentals=0),
        compiler_params=pltpu.CompilerParams(vmem_limit_bytes=48 << 20),
    )


def per_device(positions, velocities, masses, cells, active, send_lists, send_counts):
    shape = functools.partial(jax.ShapeDtypeStruct, dtype=F32)
    sine_high, sine_low = _split_np(_sine())
    cosine, sine = _trig()
    down_high, down_low = _split_np(np.concatenate([cosine, sine], axis=0))
    up_high, up_low = _split_np(np.concatenate([cosine, sine], axis=1))
    plus, minus = _twist()
    out_high, out_low = _split_np(_field_table())

    mass = masses.astype(F32).reshape(1, STARS)
    cell = cells.reshape(1, STARS)
    live = active.reshape(1, STARS)

    layered = _call(deposit_kernel, shape((64, SECTOR)), "deposit", 10**9, count=4)(
        cell, mass, sine_high, sine_low
    )
    sectors = lax.all_to_all(layered, ("az", "zh"), 0, 0, tiled=True)
    factors = _call(
        factor_kernel,
        (shape((64, SECTOR)), shape((64, SECTOR)), shape((64, SECTOR)), shape((8, SECTOR))),
        "factor",
        10**9,
        in_smem=(0,),
        count=1,
    )(_eigen())
    picked = _call(pick_kernel, shape((16, 2 * CAP)), "pick", 10**9, count=6)(
        positions, velocities, mass, cell, live, send_lists
    )
    spectrum = _call(forward_kernel, shape((64, SECTOR)), "forward", 10**9, count=5)(
        sectors, plus, minus, down_high, down_low
    )
    columns = lax.all_to_all(spectrum, ("x", "y", "c"), 0, 0, tiled=True)
    solved = _call(
        solve_kernel,
        shape((128, SECTOR)),
        "solve",
        10**9,
        count=5,
        scratch=[pltpu.VMEM((64, SECTOR), F32)],
    )(columns, *factors)
    waves = lax.all_to_all(solved, ("x", "y", "c"), 0, 0, tiled=True)
    angles = _call(inverse_kernel, shape((192, SECTOR)), "inverse", 10**9, count=5)(
        waves, plus, minus, up_high, up_low
    )
    modes = lax.all_to_all(angles, ("az", "zh"), 0, 0, tiled=True)
    potential, fields, zero, one = _call(
        parcel_kernel,
        (
            shape((64, SECTOR)),
            jax.ShapeDtypeStruct((384, SECTOR), BF16),
            shape((7, CAP)),
            shape((7, CAP)),
        ),
        "parcel",
        10**9,
        count=5,
    )(modes, out_high, out_low, picked, send_counts)
    from_lower = lax.ppermute(one, "az", [(i, (i + 1) % 8) for i in range(8)])
    from_upper = lax.ppermute(zero, "az", [((i + 1) % 8, i) for i in range(8)])
    state = _call(stars_kernel, shape((6, STARS)), "stars", 10**9, count=5)(
        fields, positions, velocities, cell, live
    )
    return potential.reshape(64, 1, SECTOR), state, jnp.stack([from_lower, from_upper])


def solution(mesh):
    fine = Mesh(mesh.devices.reshape(8, 4, 2, 4, 2), ("az", "x", "zh", "y", "c"))
    rz = ("x", "zh", "y", "c")
    every = ("az",) + rz
    return jax.shard_map(
        per_device,
        mesh=fine,
        in_specs=(
            P(None, every),
            P(None, every),
            P(every),
            P(every),
            P(every),
            P(None, every),
            P(None, every),
        ),
        out_specs=(P(None, rz, "az"), P(None, every), P(None, None, every)),
        check_vma=False,
    )
```

time: 1140 us -> 101 us (0.09)
  the two profiles are of different devices: /device:TPU:8 before, /device:TPU:2 now
where the time goes in v1:
time: 101 us; the launch traced here: 100 us
  blocking collectives  39.7 us (39%)
  starting transfers between devices  23.9 us (24%)
  waiting for transfers between devices  23.7 us (23%)
  Pallas kernels  6.21 us (6%)
  local copies, waits for them, and re-layouts  5.18 us (5%)
    all_to_all x1, blocking collectives, per_device(): sectors = lax.all_to_all(layered, ('az', 'zh'), 0, 0, tiled=True)  28.4 us
    all_to_all x1, waiting for transfers between devices, per_device(): modes = lax.all_to_all(angles, ('az', 'zh'), 0, 0, tiled=True)  18.2 us
    all_to_all x1, blocking collectives, per_device(): waves = lax.all_to_all(solved, ('x', 'y', 'c'), 0, 0, tiled=True)  11.3 us
    all_to_all x1, starting transfers between devices, per_device(): columns = lax.all_to_all(spectrum, ('x', 'y', 'c'), 0, 0, tiled=True)  7.75 us
    ppermute x1, starting transfers between devices, per_device(): from_upper = lax.ppermute(zero, 'az', [((i + 1) % 8, i) for i in range(8)])  7.08 us
    all_to_all x1, waiting for transfers between devices, per_device(): columns = lax.all_to_all(spectrum, ('x', 'y', 'c'), 0, 0, tiled=True)  5.43 us
    ppermute x1, starting transfers between devices, per_device(): from_lower = lax.ppermute(one, 'az', [(i, (i + 1) % 8) for i in range(8)])  5.37 us
    all_to_all x1, starting transfers between devices, per_device(): modes = lax.all_to_all(angles, ('az', 'zh'), 0, 0, tiled=True)  3.67 us
  transfers between devices with their start and end apart: 4, of which 2 were waited for; matrix products, arithmetic and copies ran while one was open for 1% of the time, Pallas kernels for 4%

profile of v1, /device:TPU:2, one launch (start us, length us, event | category | flops | bytes accessed | tf_op | source)
XLA Modules:
  0.0 100.2 jit_solution(14269363058899789057)
XLA Ops:
  0.6 0.0 copy-start.13
  0.6 0.0 copy-start.2
  0.7 0.7 reshape.33
  1.4 0.0 copy-done.13
  1.4 0.0 copy-done.2
  1.4 0.7 copy-done.14
  2.1 0.9 deposit.1
  3.0 0.0 copy-start.7
  3.1 28.4 %all_to_all.44 = f32[16,4,256]{2,1,0:T(4,128)S(1)} all-to-all(f32[16,4,256]{2,1,0:T(4,128)S(1)} %all_to_all.28), channel_id=1, replica_groups=mesh['az'=8,'x'=4,'zh'=2,'y'=4,'c'=2] {'az','zh'}, dimensions={0} | all-to-all | bytes 131072 | tf_op jit(solution)/shard_map/all_to_all | solution.py:376
  31.5 0.0 copy-done.8
  31.5 0.0 copy-done.7
  31.5 0.8 copy-done.11
  32.3 0.0 copy-done.12
  32.3 0.3 forward.1
  32.6 0.7 all_to_all.31
  33.3 7.8 %all-to-all-start.1 = ((f32[32,2,256]{2,1,0:T(2,128)}), f32[32,2,256]{2,1,0:T(2,128)S(1)}, u32[]{:S(2)}, u32[]{:S(2)}) async-start(f32[32,2,256]{2,1,0:T(2,128)} %all_to_all.31), calls=%async_computation.1 | async-start | bytes 131072 | tf_op jit(solution)/shard_map/all_to_all | solution.py:391
  41.1 0.0 copy-done.15
  41.1 0.9 factor.1
  42.0 5.4 %all-to-all-done.1 = f32[32,2,256]{2,1,0:T(2,128)S(1)} async-done(((f32[32,2,256]{2,1,0:T(2,128)}), f32[32,2,256]{2,1,0:T(2,128)S(1)}, u32[]{:S(2)}, u32[]{:S(2)}) %all-to-all-start.1) | async-done | bytes 65568 | tf_op jit(solution)/shard_map/all_to_all | solution.py:391
  47.5 0.2 solve.1
  47.7 0.0 copy-start.5
  47.7 0.0 copy-start.6
  47.7 11.3 %all_to_all.45 = f32[32,4,256]{2,1,0:T(4,128)S(1)} all-to-all(f32[32,4,256]{2,1,0:T(4,128)S(1)} %all_to_all.34), channel_id=1, replica_groups=mesh['az'=8,'x'=4,'zh'=2,'y'=4,'c'=2] {'x','y','c'}, dimensions={0} | all-to-all | bytes 262144 | tf_op jit(solution)/shard_map/all_to_all | solution.py:400
  59.0 0.0 copy-done.5
  59.1 0.0 copy-done.6
  59.1 0.6 inverse.1
  59.7 0.7 all_to_all.37
  60.5 3.7 %all-to-all-start.3 = ((f32[16,12,256]{2,1,0:T(8,128)}), f32[16,12,256]{2,1,0:T(8,128)S(1)}, u32[]{:S(2)}, u32[]{:S(2)}) async-start(f32[16,12,256]{2,1,0:T(8,128)} %all_to_all.37), calls=%async_computation.3 | async-start | bytes 524288 | tf_op jit(solution)/shard_map/all_to_all | solution.py:404
  64.1 0.0 copy-done.16
  64.2 0.0 copy-start.4
  64.2 0.1 copy.24.counts_ref
  64.3 0.0 copy-done
  64.3 0.0 copy-done.1
  64.3 0.0 copy-done.3
  64.3 0.6 copy-done.4
  64.8 0.8 pick.1.picked_ref
  65.7 0.0 copy-start.10
  65.7 18.2 %all-to-all-done.3 = f32[16,12,256]{2,1,0:T(8,128)S(1)} async-done(((f32[16,12,256]{2,1,0:T(8,128)}), f32[16,12,256]{2,1,0:T(8,128)S(1)}, u32[]{:S(2)}, u32[]{:S(2)}) %all-to-all-start.3) | async-done | bytes 196640 | tf_op jit(solution)/shard_map/all_to_all | solution.py:404
  83.9 0.0 copy-done.9
  83.9 0.0 copy-done.10
  83.9 0.6 parcel.1
  84.6 5.4 %collective-permute-start = (f32[7,256]{1,0:T(8,128)S(1)}, f32[7,256]{1,0:T(8,128)S(1)}, u32[]{:S(2)}, u32[]{:S(2)}) collective-permute-start(f32[7,256]{1,0:T(8,128)S(1)} %get-tuple-element.17), channel_id=1, source_target_pairs={{0,64},{64,128},{128,192},{192,256},{256,320},{320,384},{384,448},... | collective-permute-start | bytes 21512 | tf_op jit(solution)/shard_map/ppermute | solution.py:417
  90.0 7.1 %collective-permute-start.1 = (f32[7,256]{1,0:T(8,128)S(1)}, f32[7,256]{1,0:T(8,128)S(1)}, u32[]{:S(2)}, u32[]{:S(2)}) collective-permute-start(f32[7,256]{1,0:T(8,128)S(1)} %get-tuple-element.18), channel_id=1, source_target_pairs={{64,0},{128,64},{192,128},{256,192},{320,256},{384,320},{448,384},... | collective-permute-start | bytes 21512 | tf_op jit(solution)/shard_map/ppermute | solution.py:418
  97.1 1.8 %stars.1 = f32[6,4096]{1,0:T(8,128)} custom-call(bf16[384,256]{1,0:T(8,128)(2,1)S(1)} %get-tuple-element.16.fields_ref, f32[3,4096]{1,0:T(4,128)S(1)} %copy-done, f32[3,4096]{1,0:T(4,128)S(1)} %copy-done.1, s32[1,4096]{1,0:T(1,128)S(1)} %bitcast.11, s32[1,4096]{1,0:T(1,128)S(1)} %bitcast.13), custom_call_target="tpu_custom_call" | custom-call | flops 1000000000 | bytes 1048576 | tf_op jit(solution)/shard_map/stars/pallas_call | solution.py:419
  98.9 0.7 copy.25
  99.6 0.0 collective-permute-done
  99.6 0.0 collective-permute-done.1
  99.6 0.6 copy.26
  (17 shorter events, 0.2 us)
Async XLA Ops:
  0.6 0.7 copy-start.13
  0.6 0.7 copy-start.2
  1.4 0.7 copy-start.14
  2.1 29.4 %copy-start.8 = (bf16[512,256]{1,0:T(8,128)(2,1)S(1)}, bf16[512,256]{1,0:T(8,128)(2,1)}, u32[]{:S(2)}) copy-start(bf16[512,256]{1,0:T(8,128)(2,1)} %constant.28.clone.low_ref) | copy-start | bytes 786436
  3.0 28.5 %copy-start.7 = (bf16[512,256]{1,0:T(8,128)(2,1)S(1)}, bf16[512,256]{1,0:T(8,128)(2,1)}, u32[]{:S(2)}) copy-start(bf16[512,256]{1,0:T(8,128)(2,1)} %constant.27.clone.high_ref) | copy-start | bytes 786436
  31.5 0.8 copy-start.11
  31.5 0.9 copy-start.12
  33.3 7.8 %copy-start.15 = (f32[64]{0:T(128)S(1)}, f32[64]{0:T(128)}, u32[]{:S(2)}) copy-start(f32[64]{0:T(128)} %constant.24.clone.eigen_ref) | copy-start | bytes 772
  33.3 14.1 %all-to-all-start.1 = ((f32[32,2,256]{2,1,0:T(2,128)}), f32[32,2,256]{2,1,0:T(2,128)S(1)}, u32[]{:S(2)}, u32[]{:S(2)}) async-start(f32[32,2,256]{2,1,0:T(2,128)} %all_to_all.31), calls=%async_computation.1 | async-start | bytes 131072 | tf_op jit(solution)/shard_map/all_to_all | solution.py:391
  47.7 11.4 %copy-start.5 = (bf16[256,512]{1,0:T(8,128)(2,1)S(1)}, bf16[256,512]{1,0:T(8,128)(2,1)}, u32[]{:S(2)}) copy-start(bf16[256,512]{1,0:T(8,128)(2,1)} %constant.29.clone.high_ref) | copy-start | bytes 786436
  47.7 11.4 %copy-start.6 = (bf16[256,512]{1,0:T(8,128)(2,1)S(1)}, bf16[256,512]{1,0:T(8,128)(2,1)}, u32[]{:S(2)}) copy-start(bf16[256,512]{1,0:T(8,128)(2,1)} %constant.30.clone.low_ref) | copy-start | bytes 786436
  60.5 3.7 %copy-start.16 = (s32[2,1]{0,1:T(1,128)S(1)}, s32[2,1]{0,1:T(1,128)}, u32[]{:S(2)}) copy-start(s32[2,1]{0,1:T(1,128)} %param.24) | copy-start | bytes 28
  60.5 3.8 %copy-start = (f32[3,4096]{1,0:T(4,128)S(1)}, f32[3,4096]{1,0:T(4,128)}, u32[]{:S(2)}) copy-start(f32[3,4096]{1,0:T(4,128)} %positions_ref.3) | copy-start | bytes 147460
  60.5 3.8 %copy-start.1 = (f32[3,4096]{1,0:T(4,128)S(1)}, f32[3,4096]{1,0:T(4,128)}, u32[]{:S(2)}) copy-start(f32[3,4096]{1,0:T(4,128)} %velocities_ref.3) | copy-start | bytes 147460
  60.5 3.8 %copy-start.3 = (s32[4096]{0:T(1024)S(1)}, s32[4096]{0:T(1024)}, u32[]{:S(2)}) copy-start(s32[4096]{0:T(1024)} %param.22) | copy-start | bytes 49156
  60.5 23.4 %all-to-all-start.3 = ((f32[16,12,256]{2,1,0:T(8,128)}), f32[16,12,256]{2,1,0:T(8,128)S(1)}, u32[]{:S(2)}, u32[]{:S(2)}) async-start(f32[16,12,256]{2,1,0:T(8,128)} %all_to_all.37), calls=%async_computation.3 | async-start | bytes 524288 | tf_op jit(solution)/shard_map/all_to_all | solution.py:404
  64.2 0.7 copy-start.4
  65.7 18.3 %copy-start.9 = (bf16[256,192]{1,0:T(8,128)(2,1)S(1)}, bf16[256,192]{1,0:T(8,128)(2,1)}, u32[]{:S(2)}) copy-start(bf16[256,192]{1,0:T(8,128)(2,1)} %constant.31.clone.high_ref) | copy-start | bytes 294916
  65.7 18.3 %copy-start.10 = (bf16[256,192]{1,0:T(8,128)(2,1)S(1)}, bf16[256,192]{1,0:T(8,128)(2,1)}, u32[]{:S(2)}) copy-start(bf16[256,192]{1,0:T(8,128)(2,1)} %constant.32.clone.low_ref) | copy-start | bytes 294916
  84.6 15.0 %collective-permute-start = (f32[7,256]{1,0:T(8,128)S(1)}, f32[7,256]{1,0:T(8,128)S(1)}, u32[]{:S(2)}, u32[]{:S(2)}) collective-permute-start(f32[7,256]{1,0:T(8,128)S(1)} %get-tuple-element.17), channel_id=1, source_target_pairs={{0,64},{64,128},{128,192},{192,256},{256,320},{320,384},{384,448},... | collective-permute-start | bytes 21512 | tf_op jit(solution)/shard_map/ppermute | solution.py:417
  90.0 9.6 %collective-permute-start.1 = (f32[7,256]{1,0:T(8,128)S(1)}, f32[7,256]{1,0:T(8,128)S(1)}, u32[]{:S(2)}, u32[]{:S(2)}) collective-permute-start(f32[7,256]{1,0:T(8,128)S(1)} %get-tuple-element.18), channel_id=1, source_target_pairs={{64,0},{128,64},{192,128},{256,192},{320,256},{384,320},{448,384},... | collective-permute-start | bytes 21512 | tf_op jit(solution)/shard_map/ppermute | solution.py:418

commit v2 on v1

--- a/solution.py
+++ b/solution.py
@@ -24,9 +24,10 @@
 
 
 def _split_np(table):
-    high = np.asarray(table, np.float32).astype(jnp.bfloat16)
-    low = (np.asarray(table, np.float64) - high.astype(np.float64)).astype(np.float32).astype(jnp.bfloat16)
-    return high, low
+    exact = np.asarray(table, np.float64)
+    high = exact.astype(np.float32).astype(jnp.bfloat16)
+    low = (exact - high.astype(np.float64)).astype(np.float32).astype(jnp.bfloat16)
+    return np.concatenate([high, low], axis=0)
 
 
 def _sine():
@@ -38,7 +39,7 @@
 def _trig():
     ids = np.arange(SECTOR)
     theta = (ids[:, None] * ids[None, :] % SECTOR) * (2.0 * math.pi / SECTOR)
-    return np.cos(theta), np.sin(theta)
+    return np.concatenate([np.cos(theta), np.sin(theta)], axis=0)
 
 
 def _twist():
@@ -47,7 +48,7 @@
     theta = (residues[:, None] * angles[None, :] % AZIM) * (2.0 * math.pi / AZIM)
     plus = np.cos(theta) + np.sin(theta)
     minus = np.cos(theta) - np.sin(theta)
-    return plus.reshape(64, SECTOR).astype(np.float32), minus.reshape(64, SECTOR).astype(np.float32)
+    return np.concatenate([plus, minus], axis=0).reshape(128, SECTOR).astype(np.float32)
 
 
 def _field_table():
@@ -96,11 +97,36 @@
     return jnp.where(here, 1.0, 0.0).astype(BF16)
 
 
-def deposit_kernel(cells_ref, mass_ref, sine_high_ref, sine_low_ref, out_ref):
+def _sine_in_kernel():
+    shape = (HEIGHTS, HEIGHTS)
+    first = lax.broadcasted_iota(jnp.int32, shape, 0) + 1
+    second = lax.broadcasted_iota(jnp.int32, shape, 1) + 1
+    turns = lax.rem(first * second, 2 * (HEIGHTS + 1))
+    negative = turns > HEIGHTS + 1
+    turns = jnp.where(negative, turns - (HEIGHTS + 1), turns)
+    turns = jnp.minimum(turns, HEIGHTS + 1 - turns).astype(F32)
+    angle = turns * (math.pi / (HEIGHTS + 1))
+    square = angle * angle
+    series = jnp.full(shape, 1.0 / math.factorial(13), F32)
+    for power in (11, 9, 7, 5, 3, 1):
+        sign = -1.0 if power % 4 == 3 else 1.0
+        series = series * square + sign / math.factorial(power)
+    value = series * angle * math.sqrt(2.0 / (HEIGHTS + 1))
+    return jnp.where(negative, -value, value)
+
+
+def deposit_kernel(cells_hbm, mass_hbm, out_ref, cells_ref, mass_ref, sems):
+    cells_copy = pltpu.make_async_copy(cells_hbm, cells_ref, sems.at[0])
+    mass_copy = pltpu.make_async_copy(mass_hbm, mass_ref, sems.at[1])
+    cells_copy.start()
+    mass_copy.start()
+    sine = _split(_sine_in_kernel())
+    cells_copy.wait()
+    mass_copy.wait()
     total = jnp.zeros((HEIGHTS, SECTOR), F32)
     for start in range(0, STARS, CHUNK):
         cell = cells_ref[:, start : start + CHUNK]
-        mass = mass_ref[:, start : start + CHUNK]
+        mass = mass_ref[start : start + CHUNK].astype(F32).reshape(1, CHUNK)
         layer = lax.shift_right_logical(cell, 8)
         angle = cell & 255
         here = lax.broadcasted_iota(jnp.int32, (HEIGHTS, CHUNK), 0) == layer
@@ -109,28 +135,33 @@
         total += lax.dot_general(
             left, right, (((1,), (1,)), ((), ())), preferred_element_type=F32
         )
-    out_ref[...] = _dot3((sine_high_ref[...], sine_low_ref[...]), _split(total))
-
-
-def forward_kernel(x_ref, plus_ref, minus_ref, high_ref, low_ref, out_ref):
-    tiles = [x_ref[8 * a : 8 * a + 8, :] for a in range(8)]
+    layered = _dot3(sine, _split(total))
+    for group in range(16):
+        out_ref[group] = layered[4 * group : 4 * group + 4, :]
+
+
+def forward_kernel(x_ref, twist_ref, table_ref, out_ref):
+    tiles = []
+    for a in range(8):
+        tiles.append(jnp.concatenate([x_ref[2 * a], x_ref[2 * a + 1]], axis=0))
     rows = []
     for n2 in range(8):
-        even = tiles[0] * plus_ref[8 * n2 : 8 * n2 + 1, :]
-        odd = tiles[0] * minus_ref[8 * n2 : 8 * n2 + 1, :]
-        for a in range(1, 8):
+        even = None
+        odd = None
+        for a in range(8):
             at = 8 * n2 + a
-            even += tiles[a] * plus_ref[at : at + 1, :]
-            odd += tiles[a] * minus_ref[at : at + 1, :]
+            plus = tiles[a] * twist_ref[at : at + 1, :]
+            minus = tiles[a] * twist_ref[64 + at : 65 + at, :]
+            even = plus if even is None else even + plus
+            odd = minus if odd is None else odd + minus
         rows.append(jnp.concatenate([even, odd], axis=1))
     left = _split(jnp.concatenate(rows, axis=0))
-    result = _dot3(left, (high_ref[...], low_ref[...]))
+    result = _dot3(left, (table_ref[0:512, :], table_ref[512:1024, :]))
     for n2 in range(8):
         for k in range(4):
             for zh in range(2):
                 at = n2 * 8 + zh * 4 + k
-                spot = n2 * 8 + k * 2 + zh
-                out_ref[spot : spot + 1, :] = result[at : at + 1, :]
+                out_ref[n2 * 4 + k, zh : zh + 1, :] = result[at : at + 1, :]
 
 
 def factor_kernel(eigen_ref, inverse_ref, carry_ref, factor_ref, joint_ref):
@@ -176,7 +207,9 @@
 
 def solve_kernel(source_ref, inverse_ref, carry_ref, factor_ref, joint_ref, out_ref, scaled_ref):
     half = RADII // 2
-    scaled_ref[...] = source_ref[...] * inverse_ref[...]
+    for place in range(32):
+        rows = slice(2 * place, 2 * place + 2)
+        scaled_ref[rows, :] = source_ref[place] * inverse_ref[rows, :]
 
     def at(ref, i):
         row = _row_of(i)
@@ -200,52 +233,53 @@
         solved[i] = values[i] + at(factor_ref, i) * solved[i - 1]
     for i in range(RADII):
         row = _row_of(i)
-        spot = (row >> 1) * 4 + (row & 1)
-        out_ref[spot : spot + 1, :] = solved[i]
+        place, zh = row >> 1, row & 1
+        out_ref[place, zh : zh + 1, :] = solved[i]
         if i == 0:
             slope = solved[1] * 0.5
         elif i == RADII - 1:
             slope = solved[RADII - 2] * -0.5
         else:
             slope = (solved[i + 1] - solved[i - 1]) * 0.5
-        out_ref[spot + 2 : spot + 3, :] = slope
-
-
-def inverse_kernel(x_ref, plus_ref, minus_ref, high_ref, low_ref, out_ref):
+        out_ref[place, zh + 2 : zh + 3, :] = slope
+
+
+def inverse_kernel(x_ref, twist_ref, table_ref, out_ref):
     fields = [[], [], []]
     for n2 in range(8):
         pair = []
         for field in range(2):
-            spots = [n2 * 16 + k * 4 + field * 2 + zh for zh in range(2) for k in range(4)]
-            pair.append(jnp.concatenate([x_ref[at : at + 1, :] for at in spots], axis=0))
+            spots = [(n2 * 4 + k, field * 2 + zh) for zh in range(2) for k in range(4)]
+            pair.append(jnp.concatenate([x_ref[at, row : row + 1, :] for at, row in spots], axis=0))
         mode = lax.broadcasted_iota(jnp.int32, (8, SECTOR), 1) * 8 + n2
         signed = jnp.where(2 * mode < AZIM, mode, mode - AZIM)
         signed = jnp.where(2 * mode == AZIM, 0, signed).astype(F32)
         fields[0].append(pair[0])
         fields[1].append(pair[1])
         fields[2].append(pair[0] * signed)
-    table = (high_ref[...], low_ref[...])
+    cosine = (table_ref[0:256, :], table_ref[512:768, :])
+    sine = (table_ref[256:512, :], table_ref[768:1024, :])
     for field in range(3):
         left = _split(jnp.concatenate(fields[field], axis=0))
-        wave = _dot3(left, table)
+        evens = _dot3(left, cosine)
+        odds = _dot3(left, sine)
         for a in range(8):
             total = None
             for n2 in range(8):
-                even = wave[8 * n2 : 8 * n2 + 8, :SECTOR]
-                odd = wave[8 * n2 : 8 * n2 + 8, SECTOR:]
-                plus = plus_ref[8 * n2 + a : 8 * n2 + a + 1, :]
-                minus = minus_ref[8 * n2 + a : 8 * n2 + a + 1, :]
+                even = evens[8 * n2 : 8 * n2 + 8, :]
+                odd = odds[8 * n2 : 8 * n2 + 8, :]
+                plus = twist_ref[8 * n2 + a : 8 * n2 + a + 1, :]
+                minus = twist_ref[64 + 8 * n2 + a : 65 + 8 * n2 + a, :]
                 if field < 2:
                     term = even * plus + odd * minus
                 else:
                     term = even * minus - odd * plus
                 total = term if total is None else total + term
             for zh in range(2):
-                spot = (a * 2 + zh) * 12 + field * 4
-                out_ref[spot : spot + 4, :] = total[zh * 4 : zh * 4 + 4, :]
-
-
-def pick_kernel(positions_ref, velocities_ref, mass_ref, cells_ref, active_ref, lists_ref, out_ref):
+                out_ref[a * 2 + zh, field] = total[zh * 4 : zh * 4 + 4, :]
+
+
+def pick_kernel(positions_ref, velocities_ref, mass_ref, cells_ref, active_ref, lists_ref, counts_ref, out_ref):
     wanted = jnp.concatenate([lists_ref[0:1, :], lists_ref[1:2, :]], axis=1)
     total = jnp.zeros((32, 2 * CAP), F32)
     for start in range(0, STARS, CHUNK):
@@ -259,7 +293,7 @@
         cell = cells_ref[:, start : start + CHUNK]
         plain = jnp.concatenate(
             [
-                mass_ref[:, start : start + CHUNK],
+                mass_ref[start : start + CHUNK].astype(F32).reshape(1, CHUNK),
                 lax.shift_right_logical(cell, 8).astype(F32),
                 (cell & 255).astype(F32),
                 active_ref[:, start : start + CHUNK].astype(F32),
@@ -273,7 +307,10 @@
         hot = jnp.where(ids == wanted, 1.0, 0.0).astype(BF16)
         total += _dot(left, hot)
     out_ref[0:8, :] = (total[0:8] + total[8:16]) + total[16:24]
-    out_ref[8:16, :] = total[24:32]
+    slots = lax.broadcasted_iota(jnp.int32, (1, CAP), 1)
+    keep = [jnp.where(slots < counts_ref[:, i : i + 1], 1.0, 0.0) for i in range(2)]
+    out_ref[8:12, :] = total[24:28]
+    out_ref[12:13, :] = jnp.concatenate(keep, axis=1)
 
 
 def _sample(fields, layer, angle):
@@ -303,8 +340,9 @@
     return place + speed
 
 
-def parcel_kernel(modes_ref, high_ref, low_ref, picked_ref, counts_ref, pot_ref, fields_ref, zero_ref, one_ref):
-    result = _dot3((high_ref[...], low_ref[...]), _split(modes_ref[...]))
+def parcel_kernel(modes_ref, table_ref, picked_ref, pot_ref, fields_ref, wrap_ref, near_ref):
+    modes = jnp.concatenate([modes_ref[group, field] for group in range(16) for field in range(3)], axis=0)
+    result = _dot3((table_ref[0:256, :], table_ref[256:512, :]), _split(modes))
     pot_ref[...] = result[0:64]
     field_high, field_low = _split(result[64:256])
     fields = jnp.concatenate([field_high, field_low], axis=0)
@@ -320,12 +358,17 @@
         picked[11:12],
     )
     rows = jnp.concatenate(state + [picked[8:9]], axis=0)
-    slots = lax.broadcasted_iota(jnp.int32, (7, CAP), 1)
-    zero_ref[...] = jnp.where(slots < counts_ref[0:1, :], rows[:, :CAP], 0.0)
-    one_ref[...] = jnp.where(slots < counts_ref[1:2, :], rows[:, CAP:], 0.0)
-
-
-def stars_kernel(fields_ref, positions_ref, velocities_ref, cells_ref, active_ref, out_ref):
+    rows = jnp.where(picked[12:13] > 0.5, rows, 0.0)
+    down = rows[:, :CAP]
+    up = rows[:, CAP:]
+    odd = lax.rem(lax.axis_index("az"), 2) == 1
+    wrap_ref[...] = jnp.where(odd, up, down)
+    near_ref[...] = jnp.where(odd, down, up)
+
+
+def stars_kernel(pot_ref, fields_ref, positions_ref, velocities_ref, cells_ref, active_ref, grid_ref, out_ref):
+    for h in range(HEIGHTS):
+        grid_ref[h] = pot_ref[h : h + 1, :]
     fields = fields_ref[...]
     for start in range(0, STARS, CHUNK):
         lanes = slice(start, start + CHUNK)
@@ -341,39 +384,63 @@
             out_ref[row : row + 1, lanes] = state[row]
 
 
-def _call(kernel, out_shape, name, flops, in_smem=(), count=0, scratch=()):
+def arrive_kernel(far_ref, close_ref, out_ref):
+    odd = lax.rem(lax.axis_index("az"), 2) == 1
+    far = far_ref[...]
+    close = close_ref[...]
+    lower = jnp.where(odd, close, far)
+    upper = jnp.where(odd, far, close)
+    for row in range(7):
+        out_ref[row, 0:1, :] = lower[row : row + 1]
+        out_ref[row, 1:2, :] = upper[row : row + 1]
+
+
+def _call(kernel, out_shape, name, flops, in_smem=(), in_hbm=(), count=0, scratch=(), limit=48 << 20):
     vmem = pl.BlockSpec(memory_space=pltpu.VMEM)
     smem = pl.BlockSpec(memory_space=pltpu.SMEM)
+    hbm = pl.BlockSpec(memory_space=pltpu.HBM)
     outs = jax.tree.map(lambda _: vmem, out_shape)
     return pl.pallas_call(
         kernel,
         out_shape=out_shape,
-        in_specs=[smem if i in in_smem else vmem for i in range(count)],
+        in_specs=[smem if i in in_smem else hbm if i in in_hbm else vmem for i in range(count)],
         out_specs=outs,
         scratch_shapes=list(scratch),
         name=name,
         cost_estimate=pl.CostEstimate(flops=flops, bytes_accessed=1 << 20, transcendentals=0),
-        compiler_params=pltpu.CompilerParams(vmem_limit_bytes=48 << 20),
+        compiler_params=pltpu.CompilerParams(vmem_limit_bytes=limit),
     )
 
 
 def per_device(positions, velocities, masses, cells, active, send_lists, send_counts):
     shape = functools.partial(jax.ShapeDtypeStruct, dtype=F32)
-    sine_high, sine_low = _split_np(_sine())
-    cosine, sine = _trig()
-    down_high, down_low = _split_np(np.concatenate([cosine, sine], axis=0))
-    up_high, up_low = _split_np(np.concatenate([cosine, sine], axis=1))
-    plus, minus = _twist()
-    out_high, out_low = _split_np(_field_table())
-
-    mass = masses.astype(F32).reshape(1, STARS)
+    z_axes, plane_axes = ("az", "zh"), ("x", "y", "c")
+    exchange = functools.partial(lax.all_to_all, split_axis=0, concat_axis=0, tiled=True)
+    table = _split_np(_trig())
+    twist = _twist()
     cell = cells.reshape(1, STARS)
     live = active.reshape(1, STARS)
 
-    layered = _call(deposit_kernel, shape((64, SECTOR)), "deposit", 10**9, count=4)(
-        cell, mass, sine_high, sine_low
+    layered = _call(
+        deposit_kernel,
+        shape((16, 4, SECTOR)),
+        "deposit",
+        10**9,
+        in_hbm=(0, 1),
+        limit=None,
+        count=2,
+        scratch=[
+            pltpu.VMEM((1, STARS), jnp.int32),
+            pltpu.VMEM((STARS,), BF16),
+            pltpu.SemaphoreType.DMA((2,)),
+        ],
+    )(cell, masses)
+    sectors = exchange(layered, z_axes)
+    spectrum = _call(forward_kernel, shape((32, 2, SECTOR)), "forward", 10**9, count=3)(
+        sectors, twist, table
     )
-    sectors = lax.all_to_all(layered, ("az", "zh"), 0, 0, tiled=True)
+    spectrum, eigen, send_lists = lax.optimization_barrier((spectrum, jnp.asarray(_eigen()), send_lists))
+    columns = exchange(spectrum, plane_axes)
     factors = _call(
         factor_kernel,
         (shape((64, SECTOR)), shape((64, SECTOR)), shape((64, SECTOR)), shape((8, SECTOR))),
@@ -381,28 +448,25 @@
         10**9,
         in_smem=(0,),
         count=1,
-    )(_eigen())
-    picked = _call(pick_kernel, shape((16, 2 * CAP)), "pick", 10**9, count=6)(
-        positions, velocities, mass, cell, live, send_lists
+    )(eigen)
+    picked = _call(pick_kernel, shape((16, 2 * CAP)), "pick", 10**9, count=7)(
+        positions, velocities, masses, cell, live, send_lists, send_counts.reshape(1, 2)
     )
-    spectrum = _call(forward_kernel, shape((64, SECTOR)), "forward", 10**9, count=5)(
-        sectors, plus, minus, down_high, down_low
-    )
-    columns = lax.all_to_all(spectrum, ("x", "y", "c"), 0, 0, tiled=True)
+    columns, factors, picked = lax.optimization_barrier((columns, factors, picked))
     solved = _call(
         solve_kernel,
-        shape((128, SECTOR)),
+        shape((32, 4, SECTOR)),
         "solve",
         10**9,
         count=5,
         scratch=[pltpu.VMEM((64, SECTOR), F32)],
     )(columns, *factors)
-    waves = lax.all_to_all(solved, ("x", "y", "c"), 0, 0, tiled=True)
-    angles = _call(inverse_kernel, shape((192, SECTOR)), "inverse", 10**9, count=5)(
-        waves, plus, minus, up_high, up_low
+    waves = exchange(solved, plane_axes)
+    angles = _call(inverse_kernel, shape((16, 3, 4, SECTOR)), "inverse", 10**9, count=3)(
+        waves, twist, table
     )
-    modes = lax.all_to_all(angles, ("az", "zh"), 0, 0, tiled=True)
-    potential, fields, zero, one = _call(
+    modes = exchange(angles, z_axes)
+    grid, fields, wrap, near = _call(
         parcel_kernel,
         (
             shape((64, SECTOR)),
@@ -412,14 +476,15 @@
         ),
         "parcel",
         10**9,
-        count=5,
-    )(modes, out_high, out_low, picked, send_counts)
-    from_lower = lax.ppermute(one, "az", [(i, (i + 1) % 8) for i in range(8)])
-    from_upper = lax.ppermute(zero, "az", [((i + 1) % 8, i) for i in range(8)])
-    state = _call(stars_kernel, shape((6, STARS)), "stars", 10**9, count=5)(
-        fields, positions, velocities, cell, live
-    )
-    return potential.reshape(64, 1, SECTOR), state, jnp.stack([from_lower, from_upper])
+        count=3,
+    )(modes, _split_np(_field_table()), picked)
+    far = lax.ppermute(wrap, "az", [(i, (i + 1) % 8 if i % 2 else (i + 7) % 8) for i in range(8)])
+    close = lax.ppermute(near, "az", [(i, i ^ 1) for i in range(8)])
+    potential, state = _call(
+        stars_kernel, (shape((64, 1, SECTOR)), shape((6, STARS))), "stars", 10**9, count=6
+    )(grid, fields, positions, velocities, cell, live)
+    arrivals = _call(arrive_kernel, shape((7, 2, CAP)), "arrive", 10**6, count=2)(far, close)
+    return potential, state, arrivals.transpose(1, 0, 2)
 
 
 def solution(mesh):

time: 101 us -> 93.1 us (0.922)
  blocking collectives: 39.7 us -> 60.3 us
  waiting for transfers between devices: 23.7 us -> 7.69 us
  starting transfers between devices: 23.9 us -> 14.2 us
  local copies, waits for them, and re-layouts: 5.18 us -> 0.68 us
  Pallas kernels: 6.21 us -> 8.93 us
    all_to_all x2 -> x3, blocking collectives: 39.7 us -> 60.3 us  [the longest x1 28.6 us: per_device(): sectors = exchange(layered, z_axes)]
    all_to_all x2 -> x1, waiting for transfers between devices: 23.7 us -> 3.86 us  [per_device(): columns = exchange(spectrum, plane_axes)]
    ppermute x2, starting transfers between devices: 12.4 us -> 6.46 us  [the longest x1 4.29 us: per_device(): lax.ppermute(wrap, 'az', [(i, (i + 1) % 8 if i % 2 else (i + 7) % 8) for...]
    ppermute x2, waiting for transfers between devices: 0.01 us -> 3.83 us  [the longest x1 3.82 us: per_device(): lax.ppermute(wrap, 'az', [(i, (i + 1) % 8 if i % 2 else (i + 7) % 8) for...]
    all_to_all x2 -> x1, starting transfers between devices: 11.4 us -> 7.75 us  [per_device(): columns = exchange(spectrum, plane_axes)]
    unnamed x37 -> x22, local copies, waits for them, and re-layouts: 3.58 us -> 0.68 us
    pallas_call x6 -> x7, Pallas kernels: 4.69 us -> 7.41 us  [the longest x1 2.35 us: per_device(): _call(deposit_kernel, shape((16, 4, SECTOR)), 'deposit', 10 ** 9, in_hbm=...]
    all_to_all x8 -> x0, local copies, waits for them, and re-layouts: 1.6 us -> none  [the longest x2 0.76 us: per_device(): modes = lax.all_to_all(angles, ('az', 'zh'), 0, 0, tiled=True)]
  transfers between devices with their start and end apart: 4 -> 3, of which waited for: 2 -> 2; matrix products, arithmetic and copies ran while one was open for 1% -> 0% of each run, Pallas kernels for 4% -> 4%
where the time goes in v2:
time: 93.1 us; the launch traced here: 92.7 us
  blocking collectives  60.3 us (65%)
  starting transfers between devices  14.2 us (15%)
  Pallas kernels  8.93 us (10%)
  waiting for transfers between devices  7.69 us (8%)
    all_to_all x1, blocking collectives, per_device(): sectors = exchange(layered, z_axes)  28.6 us
    all_to_all x1, blocking collectives, per_device(): modes = exchange(angles, z_axes)  20.5 us
    all_to_all x1, blocking collectives, per_device(): waves = exchange(solved, plane_axes)  11.2 us
    all_to_all x1, starting transfers between devices, per_device(): columns = exchange(spectrum, plane_axes)  7.75 us
    ppermute x1, starting transfers between devices, per_device(): lax.ppermute(wrap, 'az', [(i, (i + 1) % 8 if i % 2 else (i + 7) % 8) for...  4.29 us
    all_to_all x1, waiting for transfers between devices, per_device(): columns = exchange(spectrum, plane_axes)  3.86 us
    ppermute x1, waiting for transfers between devices, per_device(): lax.ppermute(wrap, 'az', [(i, (i + 1) % 8 if i % 2 else (i + 7) % 8) for...  3.82 us
    pallas_call x1, Pallas kernels, per_device(): _call(deposit_kernel, shape((16, 4, SECTOR)), 'deposit', 10 ** 9, in_hbm=...  2.35 us
  transfers between devices with their start and end apart: 3, of which 2 were waited for; matrix products, arithmetic and copies ran while one was open for 0% of the time, Pallas kernels for 4%

profile of v2, /device:TPU:2, one launch (start us, length us, event | category | flops | bytes accessed | tf_op | source)
XLA Modules:
  0.0 92.7 jit_solution(4337337897212808065)
XLA Ops:
  0.6 0.0 copy-start.7
  0.6 2.4 %deposit.1 = f32[16,4,256]{2,1,0:T(4,128)} custom-call(s32[1,4096]{1,0:T(1,128)} %bitcast.4, bf16[4096]{0:T(1024)(128)(2,1)} %mass_ref.1), custom_call_target="tpu_custom_call" | custom-call | flops 1000000000 | bytes 1048576 | tf_op jit(solution)/shard_map/deposit/pallas_call | solution.py:424
  3.0 0.0 copy-start.9
  3.0 28.6 %all_to_all.20.x_ref = f32[16,4,256]{2,1,0:T(4,128)S(1)} all-to-all(f32[16,4,256]{2,1,0:T(4,128)} %deposit.1), channel_id=1, replica_groups=mesh['az'=8,'x'=4,'zh'=2,'y'=4,'c'=2] {'az','zh'}, dimensions={0} | all-to-all | bytes 131072 | tf_op jit(solution)/shard_map/all_to_all | solution.py:438
  31.6 0.0 copy-done.7
  31.6 0.0 copy-done.9
  31.6 0.9 %forward.1 = f32[32,2,256]{2,1,0:T(2,128)} custom-call(f32[16,4,256]{2,1,0:T(4,128)S(1)} %all_to_all.20.x_ref, f32[128,256]{1,0:T(8,128)S(1)} %copy-done.9, bf16[1024,256]{1,0:T(8,128)(2,1)S(1)} %copy-done.7), custom_call_target="tpu_custom_call" | custom-call | flops 1000000000 | bytes 1048576 | tf_op jit(solution)/shard_map/forward/pallas_call | solution.py:439
  32.6 0.0 copy-start.10
  32.6 7.8 %all-to-all-start.1 = ((f32[32,2,256]{2,1,0:T(2,128)}), f32[32,2,256]{2,1,0:T(2,128)S(1)}, u32[]{:S(2)}, u32[]{:S(2)}) async-start(f32[32,2,256]{2,1,0:T(2,128)} %forward.1), calls=%async_computation.1 | async-start | bytes 131072 | tf_op jit(solution)/shard_map/all_to_all | solution.py:443
  40.3 0.0 copy-done.10
  40.3 0.0 copy-start
  40.4 0.0 copy-start.1
  40.4 0.0 copy-start.2
  40.4 0.0 copy-start.3
  40.4 0.0 copy-start.4
  40.4 0.9 factor.1
  41.3 0.0 copy-start.5
  41.3 0.0 copy-start.6
  41.3 0.0 copy-done
  41.3 0.0 copy-done.1
  41.3 0.0 copy-done.2
  41.3 0.0 copy-done.3
  41.3 0.0 copy-done.4
  41.4 0.6 copy-done.5
  42.0 0.0 copy-done.6
  42.0 0.8 pick.1.picked_ref
  42.8 3.9 %all-to-all-done.1.source_ref = f32[32,2,256]{2,1,0:T(2,128)S(1)} async-done(((f32[32,2,256]{2,1,0:T(2,128)}), f32[32,2,256]{2,1,0:T(2,128)S(1)}, u32[]{:S(2)}, u32[]{:S(2)}) %all-to-all-start.1) | async-done | bytes 65568 | tf_op jit(solution)/shard_map/all_to_all | solution.py:443
  46.7 0.2 solve.1
  46.8 11.2 %all_to_all.21.x_ref = f32[32,4,256]{2,1,0:T(4,128)S(1)} all-to-all(f32[32,4,256]{2,1,0:T(4,128)S(1)} %solve.1), channel_id=1, replica_groups=mesh['az'=8,'x'=4,'zh'=2,'y'=4,'c'=2] {'x','y','c'}, dimensions={0} | all-to-all | bytes 262144 | tf_op jit(solution)/shard_map/all_to_all | solution.py:464
  58.0 0.6 inverse.1
  58.7 0.0 copy-start.8
  58.7 20.5 %all_to_all.22.modes_ref = f32[16,3,4,256]{3,2,1,0:T(4,128)S(1)} all-to-all(f32[16,3,4,256]{3,2,1,0:T(4,128)S(1)} %inverse.1), channel_id=1, replica_groups=mesh['az'=8,'x'=4,'zh'=2,'y'=4,'c'=2] {'az','zh'}, dimensions={0} | all-to-all | bytes 393216 | tf_op jit(solution)/shard_map/all_to_all | solution.py:468
  79.2 0.0 copy-done.8
  79.2 0.6 parcel.1
  79.9 4.3 %collective-permute-start = (f32[7,256]{1,0:T(8,128)S(1)}, f32[7,256]{1,0:T(8,128)S(1)}, u32[]{:S(2)}, u32[]{:S(2)}) collective-permute-start(f32[7,256]{1,0:T(8,128)S(1)} %get-tuple-element.39), channel_id=1, source_target_pairs={{0,448},{64,128},{128,64},{192,256},{256,192},{320,384},{384,320},... | collective-permute-start | bytes 21512 | tf_op jit(solution)/shard_map/ppermute | solution.py:481
  84.2 2.2 %collective-permute-start.1 = (f32[7,256]{1,0:T(8,128)S(1)}, f32[7,256]{1,0:T(8,128)S(1)}, u32[]{:S(2)}, u32[]{:S(2)}) collective-permute-start(f32[7,256]{1,0:T(8,128)S(1)} %get-tuple-element.40), channel_id=1, source_target_pairs={{0,64},{64,0},{128,192},{192,128},{256,320},{320,256},{384,448},{4... | collective-permute-start | bytes 21512 | tf_op jit(solution)/shard_map/ppermute | solution.py:482
  86.4 1.9 %stars.1 = (f32[64,1,256]{2,1,0:T(1,128)}, f32[6,4096]{1,0:T(8,128)}) custom-call(f32[64,256]{1,0:T(8,128)S(1)} %get-tuple-element.35.pot_ref, bf16[384,256]{1,0:T(8,128)(2,1)S(1)} %get-tuple-element.36.fields_ref, f32[3,4096]{1,0:T(4,128)S(1)} %copy-done, f32[3,4096]{1,0:T(4,128)S(1)} %copy-done.1, s32[1,4096]{1,0:T(1,128)S(1)} %bitcast.6, ...), custom_call_target="tpu_custom_call" | custom-call | flops 1000000000 | bytes 1048576 | tf_op jit(solution)/shard_map/stars/pallas_call | solution.py:483
  88.2 3.8 %collective-permute-done.far_ref = f32[7,256]{1,0:T(8,128)S(1)} collective-permute-done((f32[7,256]{1,0:T(8,128)S(1)}, f32[7,256]{1,0:T(8,128)S(1)}, u32[]{:S(2)}, u32[]{:S(2)}) %collective-permute-start) | collective-permute-done | bytes 7200 | tf_op jit(solution)/shard_map/ppermute | solution.py:481
  92.0 0.0 collective-permute-done.1.close_ref
  92.0 0.6 arrive.1
Async XLA Ops:
  0.6 31.0 %copy-start.7 = (bf16[1024,256]{1,0:T(8,128)(2,1)S(1)}, bf16[1024,256]{1,0:T(8,128)(2,1)}, u32[]{:S(2)}) copy-start(bf16[1024,256]{1,0:T(8,128)(2,1)} %constant.9.clone.table_ref) | copy-start | bytes 1572868
  3.0 28.6 %copy-start.9 = (f32[128,256]{1,0:T(8,128)S(1)}, f32[128,256]{1,0:T(8,128)}, u32[]{:S(2)}) copy-start(f32[128,256]{1,0:T(8,128)} %constant.8.clone.twist_ref) | copy-start | bytes 393220
  32.6 7.8 %copy-start.10 = (f32[64]{0:T(128)S(1)}, f32[64]{0:T(128)}, u32[]{:S(2)}) copy-start(f32[64]{0:T(128)} %constant.10.clone.eigen_ref) | copy-start | bytes 772
  32.6 14.1 %all-to-all-start.1 = ((f32[32,2,256]{2,1,0:T(2,128)}), f32[32,2,256]{2,1,0:T(2,128)S(1)}, u32[]{:S(2)}, u32[]{:S(2)}) async-start(f32[32,2,256]{2,1,0:T(2,128)} %forward.1), calls=%async_computation.1 | async-start | bytes 131072 | tf_op jit(solution)/shard_map/all_to_all | solution.py:443
  40.3 1.0 %copy-start = (f32[3,4096]{1,0:T(4,128)S(1)}, f32[3,4096]{1,0:T(4,128)}, u32[]{:S(2)}) copy-start(f32[3,4096]{1,0:T(4,128)} %positions_ref.3) | copy-start | bytes 147460
  40.4 1.0 %copy-start.1 = (f32[3,4096]{1,0:T(4,128)S(1)}, f32[3,4096]{1,0:T(4,128)}, u32[]{:S(2)}) copy-start(f32[3,4096]{1,0:T(4,128)} %velocities_ref.3) | copy-start | bytes 147460
  40.4 1.0 %copy-start.2 = (s32[4096]{0:T(1024)S(1)}, s32[4096]{0:T(1024)}, u32[]{:S(2)}) copy-start(s32[4096]{0:T(1024)} %param.14) | copy-start | bytes 49156
  40.4 1.0 %copy-start.3 = (s32[4096]{0:T(1024)S(1)}, s32[4096]{0:T(1024)}, u32[]{:S(2)}) copy-start(s32[4096]{0:T(1024)} %param.15) | copy-start | bytes 49156
  40.4 1.0 %copy-start.4 = (bf16[4096]{0:T(1024)(128)(2,1)S(1)}, bf16[4096]{0:T(1024)(128)(2,1)}, u32[]{:S(2)}) copy-start(bf16[4096]{0:T(1024)(128)(2,1)} %mass_ref.1) | copy-start | bytes 24580
  41.3 0.7 copy-start.5
  41.3 0.7 copy-start.6
  58.7 20.6 %copy-start.8 = (bf16[512,192]{1,0:T(8,128)(2,1)S(1)}, bf16[512,192]{1,0:T(8,128)(2,1)}, u32[]{:S(2)}) copy-start(bf16[512,192]{1,0:T(8,128)(2,1)} %constant.11.clone.table_ref) | copy-start | bytes 589828
  79.9 12.1 %collective-permute-start = (f32[7,256]{1,0:T(8,128)S(1)}, f32[7,256]{1,0:T(8,128)S(1)}, u32[]{:S(2)}, u32[]{:S(2)}) collective-permute-start(f32[7,256]{1,0:T(8,128)S(1)} %get-tuple-element.39), channel_id=1, source_target_pairs={{0,448},{64,128},{128,64},{192,256},{256,192},{320,384},{384,320},... | collective-permute-start | bytes 21512 | tf_op jit(solution)/shard_map/ppermute | solution.py:481
  84.2 7.9 %collective-permute-start.1 = (f32[7,256]{1,0:T(8,128)S(1)}, f32[7,256]{1,0:T(8,128)S(1)}, u32[]{:S(2)}, u32[]{:S(2)}) collective-permute-start(f32[7,256]{1,0:T(8,128)S(1)} %get-tuple-element.40), channel_id=1, source_target_pairs={{0,64},{64,0},{128,192},{192,128},{256,320},{320,256},{384,448},{4... | collective-permute-start | bytes 21512 | tf_op jit(solution)/shard_map/ppermute | solution.py:482

commit v3 on v2

--- a/solution.py
+++ b/solution.py
@@ -435,12 +435,8 @@
             pltpu.SemaphoreType.DMA((2,)),
         ],
     )(cell, masses)
+    layered, eigen, send_lists = lax.optimization_barrier((layered, jnp.asarray(_eigen()), send_lists))
     sectors = exchange(layered, z_axes)
-    spectrum = _call(forward_kernel, shape((32, 2, SECTOR)), "forward", 10**9, count=3)(
-        sectors, twist, table
-    )
-    spectrum, eigen, send_lists = lax.optimization_barrier((spectrum, jnp.asarray(_eigen()), send_lists))
-    columns = exchange(spectrum, plane_axes)
     factors = _call(
         factor_kernel,
         (shape((64, SECTOR)), shape((64, SECTOR)), shape((64, SECTOR)), shape((8, SECTOR))),
@@ -452,7 +448,11 @@
     picked = _call(pick_kernel, shape((16, 2 * CAP)), "pick", 10**9, count=7)(
         positions, velocities, masses, cell, live, send_lists, send_counts.reshape(1, 2)
     )
-    columns, factors, picked = lax.optimization_barrier((columns, factors, picked))
+    sectors, factors, picked = lax.optimization_barrier((sectors, factors, picked))
+    spectrum = _call(forward_kernel, shape((32, 2, SECTOR)), "forward", 10**9, count=3)(
+        sectors, twist, table
+    )
+    columns = exchange(spectrum, plane_axes)
     solved = _call(
         solve_kernel,
         shape((32, 4, SECTOR)),

time: 93.1 us -> 92 us (0.988)
  blocking collectives: 60.3 us -> 45.5 us
  starting transfers between devices: 14.2 us -> 21.7 us
  waiting for transfers between devices: 7.69 us -> 14.6 us
    all_to_all x1, blocking collectives: 28.6 us -> 13.8 us  [per_device(): columns = exchange(spectrum, plane_axes)]
    all_to_all x1, starting transfers between devices: 7.75 us -> 15.2 us  [per_device(): sectors = exchange(layered, z_axes)]
    all_to_all x1, waiting for transfers between devices: 3.86 us -> 10.8 us  [per_device(): sectors = exchange(layered, z_axes)]
where the time goes in v3:
time: 92 us; the launch traced here: 91.5 us
  blocking collectives  45.5 us (49%)
  starting transfers between devices  21.7 us (24%)
  waiting for transfers between devices  14.6 us (16%)
  Pallas kernels  8.26 us (9%)
    all_to_all x1, blocking collectives, per_device(): modes = exchange(angles, z_axes)  20.5 us
    all_to_all x1, starting transfers between devices, per_device(): sectors = exchange(layered, z_axes)  15.2 us
    all_to_all x1, blocking collectives, per_device(): columns = exchange(spectrum, plane_axes)  13.8 us
    all_to_all x1, blocking collectives, per_device(): waves = exchange(solved, plane_axes)  11.2 us
    all_to_all x1, waiting for transfers between devices, per_device(): sectors = exchange(layered, z_axes)  10.8 us
    ppermute x1, starting transfers between devices, per_device(): lax.ppermute(wrap, 'az', [(i, (i + 1) % 8 if i % 2 else (i + 7) % 8) for...  4.29 us
    ppermute x1, waiting for transfers between devices, per_device(): lax.ppermute(wrap, 'az', [(i, (i + 1) % 8 if i % 2 else (i + 7) % 8) for...  3.83 us
    pallas_call x1, Pallas kernels, per_device(): _call(deposit_kernel, shape((16, 4, SECTOR)), 'deposit', 10 ** 9, in_hbm=...  2.3 us
  transfers between devices with their start and end apart: 3, of which 2 were waited for; matrix products, arithmetic and copies ran while one was open for 0% of the time, Pallas kernels for 4%

profile of v3, /device:TPU:2, one launch (start us, length us, event | category | flops | bytes accessed | tf_op | source)
XLA Modules:
  0.0 91.5 jit_solution(12697596674385839035)
XLA Ops:
  0.6 2.3 %deposit.1 = f32[16,4,256]{2,1,0:T(4,128)} custom-call(s32[1,4096]{1,0:T(1,128)} %bitcast.4, bf16[4096]{0:T(1024)(128)(2,1)} %mass_ref.1), custom_call_target="tpu_custom_call" | custom-call | flops 1000000000 | bytes 1048576 | tf_op jit(solution)/shard_map/deposit/pallas_call | solution.py:424
  2.9 0.0 copy-start.10
  2.9 15.2 %all-to-all-start = ((f32[16,4,256]{2,1,0:T(4,128)}), f32[16,4,256]{2,1,0:T(4,128)S(1)}, u32[]{:S(2)}, u32[]{:S(2)}) async-start(f32[16,4,256]{2,1,0:T(4,128)} %deposit.1), calls=%async_computation | async-start | bytes 131072 | tf_op jit(solution)/shard_map/all_to_all | solution.py:439
  18.2 0.0 copy-done.10
  18.2 0.0 copy-start
  18.2 0.0 copy-start.1
  18.2 0.0 copy-start.2
  18.2 0.0 copy-start.3
  18.2 0.0 copy-start.4
  18.2 0.9 factor.1
  19.1 0.0 copy-start.5
  19.1 0.0 copy-start.6
  19.1 0.0 copy-done
  19.1 0.0 copy-done.1
  19.2 0.0 copy-done.2
  19.2 0.0 copy-done.3
  19.2 0.0 copy-done.4
  19.2 0.6 copy-done.5
  19.8 0.0 copy-done.6
  19.8 0.0 copy-start.7
  19.8 0.0 copy-start.9
  19.8 0.8 pick.1.picked_ref
  20.6 10.8 %all-to-all-done.x_ref = f32[16,4,256]{2,1,0:T(4,128)S(1)} async-done(((f32[16,4,256]{2,1,0:T(4,128)}), f32[16,4,256]{2,1,0:T(4,128)S(1)}, u32[]{:S(2)}, u32[]{:S(2)}) %all-to-all-start) | async-done | bytes 65568 | tf_op jit(solution)/shard_map/all_to_all | solution.py:439
  31.4 0.0 copy-done.7
  31.4 0.0 copy-done.9
  31.4 0.3 forward.1
  31.7 13.8 %all_to_all.20.source_ref = f32[32,2,256]{2,1,0:T(2,128)S(1)} all-to-all(f32[32,2,256]{2,1,0:T(2,128)S(1)} %forward.1), channel_id=1, replica_groups=mesh['az'=8,'x'=4,'zh'=2,'y'=4,'c'=2] {'x','y','c'}, dimensions={0} | all-to-all | bytes 131072 | tf_op jit(solution)/shard_map/all_to_all | solution.py:455
  45.5 0.2 solve.1
  45.7 11.2 %all_to_all.21.x_ref = f32[32,4,256]{2,1,0:T(4,128)S(1)} all-to-all(f32[32,4,256]{2,1,0:T(4,128)S(1)} %solve.1), channel_id=1, replica_groups=mesh['az'=8,'x'=4,'zh'=2,'y'=4,'c'=2] {'x','y','c'}, dimensions={0} | all-to-all | bytes 262144 | tf_op jit(solution)/shard_map/all_to_all | solution.py:464
  56.9 0.7 inverse.1
  57.5 0.0 copy-start.8
  57.6 20.5 %all_to_all.22.modes_ref = f32[16,3,4,256]{3,2,1,0:T(4,128)S(1)} all-to-all(f32[16,3,4,256]{3,2,1,0:T(4,128)S(1)} %inverse.1), channel_id=1, replica_groups=mesh['az'=8,'x'=4,'zh'=2,'y'=4,'c'=2] {'az','zh'}, dimensions={0} | all-to-all | bytes 393216 | tf_op jit(solution)/shard_map/all_to_all | solution.py:468
  78.1 0.0 copy-done.8
  78.1 0.6 parcel.1
  78.8 4.3 %collective-permute-start = (f32[7,256]{1,0:T(8,128)S(1)}, f32[7,256]{1,0:T(8,128)S(1)}, u32[]{:S(2)}, u32[]{:S(2)}) collective-permute-start(f32[7,256]{1,0:T(8,128)S(1)} %get-tuple-element.39), channel_id=1, source_target_pairs={{0,448},{64,128},{128,64},{192,256},{256,192},{320,384},{384,320},... | collective-permute-start | bytes 21512 | tf_op jit(solution)/shard_map/ppermute | solution.py:481
  83.0 2.2 %collective-permute-start.1 = (f32[7,256]{1,0:T(8,128)S(1)}, f32[7,256]{1,0:T(8,128)S(1)}, u32[]{:S(2)}, u32[]{:S(2)}) collective-permute-start(f32[7,256]{1,0:T(8,128)S(1)} %get-tuple-element.40), channel_id=1, source_target_pairs={{0,64},{64,0},{128,192},{192,128},{256,320},{320,256},{384,448},{4... | collective-permute-start | bytes 21512 | tf_op jit(solution)/shard_map/ppermute | solution.py:482
  85.2 1.9 %stars.1 = (f32[64,1,256]{2,1,0:T(1,128)}, f32[6,4096]{1,0:T(8,128)}) custom-call(f32[64,256]{1,0:T(8,128)S(1)} %get-tuple-element.35.pot_ref, bf16[384,256]{1,0:T(8,128)(2,1)S(1)} %get-tuple-element.36.fields_ref, f32[3,4096]{1,0:T(4,128)S(1)} %copy-done, f32[3,4096]{1,0:T(4,128)S(1)} %copy-done.1, s32[1,4096]{1,0:T(1,128)S(1)} %bitcast.6, ...), custom_call_target="tpu_custom_call" | custom-call | flops 1000000000 | bytes 1048576 | tf_op jit(solution)/shard_map/stars/pallas_call | solution.py:483
  87.1 3.8 %collective-permute-done.far_ref = f32[7,256]{1,0:T(8,128)S(1)} collective-permute-done((f32[7,256]{1,0:T(8,128)S(1)}, f32[7,256]{1,0:T(8,128)S(1)}, u32[]{:S(2)}, u32[]{:S(2)}) %collective-permute-start) | collective-permute-done | bytes 7200 | tf_op jit(solution)/shard_map/ppermute | solution.py:481
  90.9 0.0 collective-permute-done.1.close_ref
  90.9 0.6 arrive.1
Async XLA Ops:
  2.9 15.2 %copy-start.10 = (f32[64]{0:T(128)S(1)}, f32[64]{0:T(128)}, u32[]{:S(2)}) copy-start(f32[64]{0:T(128)} %constant.8.clone.eigen_ref) | copy-start | bytes 772
  2.9 28.5 %all-to-all-start = ((f32[16,4,256]{2,1,0:T(4,128)}), f32[16,4,256]{2,1,0:T(4,128)S(1)}, u32[]{:S(2)}, u32[]{:S(2)}) async-start(f32[16,4,256]{2,1,0:T(4,128)} %deposit.1), calls=%async_computation | async-start | bytes 131072 | tf_op jit(solution)/shard_map/all_to_all | solution.py:439
  18.2 1.0 %copy-start = (f32[3,4096]{1,0:T(4,128)S(1)}, f32[3,4096]{1,0:T(4,128)}, u32[]{:S(2)}) copy-start(f32[3,4096]{1,0:T(4,128)} %positions_ref.3) | copy-start | bytes 147460
  18.2 1.0 %copy-start.1 = (f32[3,4096]{1,0:T(4,128)S(1)}, f32[3,4096]{1,0:T(4,128)}, u32[]{:S(2)}) copy-start(f32[3,4096]{1,0:T(4,128)} %velocities_ref.3) | copy-start | bytes 147460
  18.2 1.0 %copy-start.2 = (s32[4096]{0:T(1024)S(1)}, s32[4096]{0:T(1024)}, u32[]{:S(2)}) copy-start(s32[4096]{0:T(1024)} %param.14) | copy-start | bytes 49156
  18.2 1.0 %copy-start.3 = (s32[4096]{0:T(1024)S(1)}, s32[4096]{0:T(1024)}, u32[]{:S(2)}) copy-start(s32[4096]{0:T(1024)} %param.15) | copy-start | bytes 49156
  18.2 1.0 %copy-start.4 = (bf16[4096]{0:T(1024)(128)(2,1)S(1)}, bf16[4096]{0:T(1024)(128)(2,1)}, u32[]{:S(2)}) copy-start(bf16[4096]{0:T(1024)(128)(2,1)} %mass_ref.1) | copy-start | bytes 24580
  19.1 0.7 copy-start.5
  19.1 0.7 copy-start.6
  19.8 11.6 %copy-start.7 = (bf16[1024,256]{1,0:T(8,128)(2,1)S(1)}, bf16[1024,256]{1,0:T(8,128)(2,1)}, u32[]{:S(2)}) copy-start(bf16[1024,256]{1,0:T(8,128)(2,1)} %constant.10.clone.table_ref) | copy-start | bytes 1572868
  19.8 11.6 %copy-start.9 = (f32[128,256]{1,0:T(8,128)S(1)}, f32[128,256]{1,0:T(8,128)}, u32[]{:S(2)}) copy-start(f32[128,256]{1,0:T(8,128)} %constant.9.clone.twist_ref) | copy-start | bytes 393220
  57.5 20.6 %copy-start.8 = (bf16[512,192]{1,0:T(8,128)(2,1)S(1)}, bf16[512,192]{1,0:T(8,128)(2,1)}, u32[]{:S(2)}) copy-start(bf16[512,192]{1,0:T(8,128)(2,1)} %constant.11.clone.table_ref) | copy-start | bytes 589828
  78.8 12.1 %collective-permute-start = (f32[7,256]{1,0:T(8,128)S(1)}, f32[7,256]{1,0:T(8,128)S(1)}, u32[]{:S(2)}, u32[]{:S(2)}) collective-permute-start(f32[7,256]{1,0:T(8,128)S(1)} %get-tuple-element.39), channel_id=1, source_target_pairs={{0,448},{64,128},{128,64},{192,256},{256,192},{320,384},{384,320},... | collective-permute-start | bytes 21512 | tf_op jit(solution)/shard_map/ppermute | solution.py:481
  83.0 7.9 %collective-permute-start.1 = (f32[7,256]{1,0:T(8,128)S(1)}, f32[7,256]{1,0:T(8,128)S(1)}, u32[]{:S(2)}, u32[]{:S(2)}) collective-permute-start(f32[7,256]{1,0:T(8,128)S(1)} %get-tuple-element.40), channel_id=1, source_target_pairs={{0,64},{64,0},{128,192},{192,128},{256,320},{320,256},{384,448},{4... | collective-permute-start | bytes 21512 | tf_op jit(solution)/shard_map/ppermute | solution.py:482

commit v4 on v3

--- a/solution.py
+++ b/solution.py
@@ -64,6 +64,19 @@
     table[2, :, :, 2, :] = -by_group
     table[3, :, :, 0, :] = -vertical.reshape(HEIGHTS, 16, 4)
     return table.reshape(4 * HEIGHTS, 192) / AZIM
+
+
+def _weight_table():
+    table = _field_table().reshape(4, HEIGHTS, 16, 3, 4)
+    sine = table[1, :, :, 1, :]
+    vertical = table[3, :, :, 0, :]
+    exact = np.zeros((16, 2, 2, 2, 4, HEIGHTS))
+    for zh in range(2):
+        exact[:, zh, 0, zh] = sine.transpose(1, 2, 0)
+        exact[:, zh, 1, zh] = vertical.transpose(1, 2, 0)
+    exact = exact.reshape(16 * 2 * 16, HEIGHTS)
+    both = _split_np(exact).reshape(2, 16, 2, 16, HEIGHTS)
+    return both.transpose(1, 2, 0, 3, 4).reshape(16, 2, 32, HEIGHTS)
 
 
 def _eigen():
@@ -115,20 +128,29 @@
     return jnp.where(negative, -value, value)
 
 
-def deposit_kernel(cells_hbm, mass_hbm, out_ref, cells_ref, mass_ref, sems):
+def deposit_kernel(cells_hbm, mass_hbm, lists_hbm, out_ref, cells_ref, mass_ref, lists_ref, sems):
     cells_copy = pltpu.make_async_copy(cells_hbm, cells_ref, sems.at[0])
     mass_copy = pltpu.make_async_copy(mass_hbm, mass_ref, sems.at[1])
+    lists_copy = pltpu.make_async_copy(lists_hbm, lists_ref, sems.at[2])
     cells_copy.start()
+    lists_copy.start()
     mass_copy.start()
     sine = _split(_sine_in_kernel())
     cells_copy.wait()
+    lists_copy.wait()
     mass_copy.wait()
+    wanted = jnp.concatenate([lists_ref[0:1, :], lists_ref[1:2, :]], axis=1)
+    sent = jnp.zeros((16, 2 * CAP), F32)
     total = jnp.zeros((HEIGHTS, SECTOR), F32)
     for start in range(0, STARS, CHUNK):
         cell = cells_ref[:, start : start + CHUNK]
         mass = mass_ref[start : start + CHUNK].astype(F32).reshape(1, CHUNK)
         layer = lax.shift_right_logical(cell, 8)
         angle = cell & 255
+        pair = jnp.concatenate([layer, angle, jnp.zeros((14, CHUNK), jnp.int32)], axis=0)
+        ids = lax.broadcasted_iota(jnp.int32, (CHUNK, 2 * CAP), 0) + start
+        hot = jnp.where(ids == wanted, 1.0, 0.0).astype(BF16)
+        sent += _dot(pair.astype(F32).astype(BF16), hot)
         here = lax.broadcasted_iota(jnp.int32, (HEIGHTS, CHUNK), 0) == layer
         left = jnp.where(here, mass, 0.0).astype(BF16)
         right = _one_hot(angle, SECTOR)
@@ -136,14 +158,19 @@
             left, right, (((1,), (1,)), ((), ())), preferred_element_type=F32
         )
     layered = _dot3(sine, _split(total))
+    sent_cell = sent[0:1] * 256.0 + sent[1:2]
     for group in range(16):
-        out_ref[group] = layered[4 * group : 4 * group + 4, :]
+        out_ref[group, 0] = layered[4 * group : 4 * group + 2, :]
+        out_ref[group, 1] = layered[4 * group + 2 : 4 * group + 4, :]
+        out_ref[group, 2, 0:1, :] = sent_cell[:, :CAP]
+        out_ref[group, 2, 1:2, :] = sent_cell[:, CAP:]
 
 
 def forward_kernel(x_ref, twist_ref, table_ref, out_ref):
     tiles = []
     for a in range(8):
-        tiles.append(jnp.concatenate([x_ref[2 * a], x_ref[2 * a + 1]], axis=0))
+        parts = [x_ref[2 * a + zh, half] for zh in range(2) for half in range(2)]
+        tiles.append(jnp.concatenate(parts, axis=0))
     rows = []
     for n2 in range(8):
         even = None
@@ -244,7 +271,8 @@
         out_ref[place, zh + 2 : zh + 3, :] = slope
 
 
-def inverse_kernel(x_ref, twist_ref, table_ref, out_ref):
+def inverse_kernel(x_ref, twist_ref, table_ref, cells_ref, weight_ref, out_ref):
+    group = lax.axis_index("az") * 2 + lax.axis_index("zh")
     fields = [[], [], []]
     for n2 in range(8):
         pair = []
@@ -259,15 +287,17 @@
         fields[2].append(pair[0] * signed)
     cosine = (table_ref[0:256, :], table_ref[512:768, :])
     sine = (table_ref[256:512, :], table_ref[768:1024, :])
+    waves = []
     for field in range(3):
         left = _split(jnp.concatenate(fields[field], axis=0))
-        evens = _dot3(left, cosine)
-        odds = _dot3(left, sine)
-        for a in range(8):
+        waves.append((_dot3(left, cosine), _dot3(left, sine)))
+    for a in range(8):
+        tiles = []
+        for field in range(3):
             total = None
             for n2 in range(8):
-                even = evens[8 * n2 : 8 * n2 + 8, :]
-                odd = odds[8 * n2 : 8 * n2 + 8, :]
+                even = waves[field][0][8 * n2 : 8 * n2 + 8, :]
+                odd = waves[field][1][8 * n2 : 8 * n2 + 8, :]
                 plus = twist_ref[8 * n2 + a : 8 * n2 + a + 1, :]
                 minus = twist_ref[64 + 8 * n2 + a : 65 + 8 * n2 + a, :]
                 if field < 2:
@@ -276,10 +306,32 @@
                     term = even * minus - odd * plus
                 total = term if total is None else total + term
             for zh in range(2):
-                out_ref[a * 2 + zh, field] = total[zh * 4 : zh * 4 + 4, :]
-
-
-def pick_kernel(positions_ref, velocities_ref, mass_ref, cells_ref, active_ref, lists_ref, counts_ref, out_ref):
+                for half in range(2):
+                    row = zh * 4 + half * 2
+                    out_ref[a * 2 + zh, field * 2 + half] = total[row : row + 2, :]
+            tiles.append(total)
+        high, low = _split(jnp.concatenate(tiles, axis=0))
+        both = jnp.concatenate([high, low], axis=0)
+        for zh in range(2):
+            cell = cells_ref[a * 2 + zh, 2]
+            cell = jnp.concatenate([cell[0:1], cell[1:2]], axis=1).astype(jnp.int32)
+            found = _dot(both, _one_hot(cell & 255, SECTOR))
+            found = found[0:24] + found[24:48]
+            weight = _dot(weight_ref[group, zh], _one_hot(lax.shift_right_logical(cell, 8), HEIGHTS))
+            weight = weight[0:16] + weight[16:32]
+            accel = [
+                jnp.sum(weight[0:8] * found[8:16], axis=0, keepdims=True),
+                jnp.sum(weight[0:8] * found[16:24], axis=0, keepdims=True),
+                jnp.sum(weight[8:16] * found[0:8], axis=0, keepdims=True),
+            ]
+            for slot, dest in ((1, (a + 7) % 8), (0, (a + 1) % 8)):
+                lanes = slice(0, CAP) if slot == 1 else slice(CAP, 2 * CAP)
+                for field in range(3):
+                    row = slot * 3 + field
+                    out_ref[dest * 2 + zh, 6 + row // 2, row % 2 : row % 2 + 1, :] = accel[field][:, lanes]
+
+
+def pick_kernel(positions_ref, velocities_ref, mass_ref, active_ref, lists_ref, counts_ref, wrap_ref, near_ref):
     wanted = jnp.concatenate([lists_ref[0:1, :], lists_ref[1:2, :]], axis=1)
     total = jnp.zeros((32, 2 * CAP), F32)
     for start in range(0, STARS, CHUNK):
@@ -290,14 +342,11 @@
         rest = moving - high
         middle = rest.astype(BF16).astype(F32)
         low = rest - middle
-        cell = cells_ref[:, start : start + CHUNK]
         plain = jnp.concatenate(
             [
                 mass_ref[start : start + CHUNK].astype(F32).reshape(1, CHUNK),
-                lax.shift_right_logical(cell, 8).astype(F32),
-                (cell & 255).astype(F32),
                 active_ref[:, start : start + CHUNK].astype(F32),
-                jnp.zeros((4, CHUNK), F32),
+                jnp.zeros((6, CHUNK), F32),
             ],
             axis=0,
         )
@@ -306,11 +355,17 @@
         ids = lax.broadcasted_iota(jnp.int32, (CHUNK, 2 * CAP), 0) + start
         hot = jnp.where(ids == wanted, 1.0, 0.0).astype(BF16)
         total += _dot(left, hot)
-    out_ref[0:8, :] = (total[0:8] + total[8:16]) + total[16:24]
+    moving = (total[0:6] + total[8:14]) + total[16:22]
     slots = lax.broadcasted_iota(jnp.int32, (1, CAP), 1)
     keep = [jnp.where(slots < counts_ref[:, i : i + 1], 1.0, 0.0) for i in range(2)]
-    out_ref[8:12, :] = total[24:28]
-    out_ref[12:13, :] = jnp.concatenate(keep, axis=1)
+    rows = jnp.concatenate(
+        [moving, total[24:26], jnp.concatenate(keep, axis=1), jnp.zeros((7, 2 * CAP), F32)], axis=0
+    )
+    down = rows[:, :CAP]
+    up = rows[:, CAP:]
+    odd = lax.rem(lax.axis_index("az"), 2) == 1
+    wrap_ref[...] = jnp.where(odd, up, down)
+    near_ref[...] = jnp.where(odd, down, up)
 
 
 def _sample(fields, layer, angle):
@@ -340,36 +395,39 @@
     return place + speed
 
 
-def parcel_kernel(modes_ref, table_ref, picked_ref, pot_ref, fields_ref, wrap_ref, near_ref):
-    modes = jnp.concatenate([modes_ref[group, field] for group in range(16) for field in range(3)], axis=0)
+def final_kernel(
+    modes_ref, table_ref, far_ref, close_ref, positions_ref, velocities_ref, cells_ref, active_ref,
+    grid_ref, state_ref, arrive_ref,
+):
+    pieces = [modes_ref[group, part] for group in range(16) for part in range(6)]
+    modes = jnp.concatenate(pieces, axis=0)
     result = _dot3((table_ref[0:256, :], table_ref[256:512, :]), _split(modes))
-    pot_ref[...] = result[0:64]
+    for h in range(HEIGHTS):
+        grid_ref[h] = result[h : h + 1, :]
     field_high, field_low = _split(result[64:256])
     fields = jnp.concatenate([field_high, field_low], axis=0)
-    fields_ref[...] = fields
-    picked = picked_ref[...]
-    layer = picked[9:10].astype(jnp.int32)
-    angle = picked[10:11].astype(jnp.int32)
-    accel = _sample(fields, layer, angle)
-    state = _advance(
-        [picked[i : i + 1] for i in range(3)],
-        [picked[i : i + 1] for i in range(3, 6)],
-        accel,
-        picked[11:12],
-    )
-    rows = jnp.concatenate(state + [picked[8:9]], axis=0)
-    rows = jnp.where(picked[12:13] > 0.5, rows, 0.0)
-    down = rows[:, :CAP]
-    up = rows[:, CAP:]
+
+    sums = []
+    for part in range(6, 9):
+        total = modes_ref[0, part]
+        for group in range(1, 16):
+            total = total + modes_ref[group, part]
+        sums += [total[0:1], total[1:2]]
     odd = lax.rem(lax.axis_index("az"), 2) == 1
-    wrap_ref[...] = jnp.where(odd, up, down)
-    near_ref[...] = jnp.where(odd, down, up)
-
-
-def stars_kernel(pot_ref, fields_ref, positions_ref, velocities_ref, cells_ref, active_ref, grid_ref, out_ref):
-    for h in range(HEIGHTS):
-        grid_ref[h] = pot_ref[h : h + 1, :]
-    fields = fields_ref[...]
+    far = far_ref[...]
+    close = close_ref[...]
+    for slot in range(2):
+        picked = jnp.where(odd, far, close) if slot else jnp.where(odd, close, far)
+        state = _advance(
+            [picked[i : i + 1] for i in range(3)],
+            [picked[i : i + 1] for i in range(3, 6)],
+            sums[slot * 3 : slot * 3 + 3],
+            picked[7:8],
+        )
+        keep = picked[8:9] > 0.5
+        for row, value in enumerate(state + [picked[6:7]]):
+            arrive_ref[row, slot : slot + 1, :] = jnp.where(keep, value, 0.0)
+
     for start in range(0, STARS, CHUNK):
         lanes = slice(start, start + CHUNK)
         cell = cells_ref[:, lanes]
@@ -381,18 +439,7 @@
             active_ref[:, lanes].astype(F32),
         )
         for row in range(6):
-            out_ref[row : row + 1, lanes] = state[row]
-
-
-def arrive_kernel(far_ref, close_ref, out_ref):
-    odd = lax.rem(lax.axis_index("az"), 2) == 1
-    far = far_ref[...]
-    close = close_ref[...]
-    lower = jnp.where(odd, close, far)
-    upper = jnp.where(odd, far, close)
-    for row in range(7):
-        out_ref[row, 0:1, :] = lower[row : row + 1]
-        out_ref[row, 1:2, :] = upper[row : row + 1]
+            state_ref[row : row + 1, lanes] = state[row]
 
 
 def _call(kernel, out_shape, name, flops, in_smem=(), in_hbm=(), count=0, scratch=(), limit=48 << 20):
@@ -423,19 +470,20 @@
 
     layered = _call(
         deposit_kernel,
-        shape((16, 4, SECTOR)),
+        shape((16, 3, 2, SECTOR)),
         "deposit",
         10**9,
-        in_hbm=(0, 1),
+        in_hbm=(0, 1, 2),
         limit=None,
-        count=2,
+        count=3,
         scratch=[
             pltpu.VMEM((1, STARS), jnp.int32),
             pltpu.VMEM((STARS,), BF16),
-            pltpu.SemaphoreType.DMA((2,)),
+            pltpu.VMEM((2, CAP), jnp.int32),
+            pltpu.SemaphoreType.DMA((3,)),
         ],
-    )(cell, masses)
-    layered, eigen, send_lists = lax.optimization_barrier((layered, jnp.asarray(_eigen()), send_lists))
+    )(cell, masses, send_lists)
+    layered, eigen, late_lists = lax.optimization_barrier((layered, jnp.asarray(_eigen()), send_lists))
     sectors = exchange(layered, z_axes)
     factors = _call(
         factor_kernel,
@@ -445,10 +493,10 @@
         in_smem=(0,),
         count=1,
     )(eigen)
-    picked = _call(pick_kernel, shape((16, 2 * CAP)), "pick", 10**9, count=7)(
-        positions, velocities, masses, cell, live, send_lists, send_counts.reshape(1, 2)
+    wrap, near = _call(pick_kernel, (shape((16, CAP)), shape((16, CAP))), "pick", 10**9, count=6)(
+        positions, velocities, masses, live, late_lists, send_counts.reshape(1, 2)
     )
-    sectors, factors, picked = lax.optimization_barrier((sectors, factors, picked))
+    sectors, factors, wrap, near = lax.optimization_barrier((sectors, factors, wrap, near))
     spectrum = _call(forward_kernel, shape((32, 2, SECTOR)), "forward", 10**9, count=3)(
         sectors, twist, table
     )
@@ -462,28 +510,20 @@
         scratch=[pltpu.VMEM((64, SECTOR), F32)],
     )(columns, *factors)
     waves = exchange(solved, plane_axes)
-    angles = _call(inverse_kernel, shape((16, 3, 4, SECTOR)), "inverse", 10**9, count=3)(
-        waves, twist, table
+    angles = _call(inverse_kernel, shape((16, 9, 2, SECTOR)), "inverse", 10**9, count=5)(
+        waves, twist, table, sectors, _weight_table()
     )
+    angles, wrap, near = lax.optimization_barrier((angles, wrap, near))
     modes = exchange(angles, z_axes)
-    grid, fields, wrap, near = _call(
-        parcel_kernel,
-        (
-            shape((64, SECTOR)),
-            jax.ShapeDtypeStruct((384, SECTOR), BF16),
-            shape((7, CAP)),
-            shape((7, CAP)),
-        ),
-        "parcel",
-        10**9,
-        count=3,
-    )(modes, _split_np(_field_table()), picked)
     far = lax.ppermute(wrap, "az", [(i, (i + 1) % 8 if i % 2 else (i + 7) % 8) for i in range(8)])
     close = lax.ppermute(near, "az", [(i, i ^ 1) for i in range(8)])
-    potential, state = _call(
-        stars_kernel, (shape((64, 1, SECTOR)), shape((6, STARS))), "stars", 10**9, count=6
-    )(grid, fields, positions, velocities, cell, live)
-    arrivals = _call(arrive_kernel, shape((7, 2, CAP)), "arrive", 10**6, count=2)(far, close)
+    potential, state, arrivals = _call(
+        final_kernel,
+        (shape((64, 1, SECTOR)), shape((6, STARS)), shape((7, 2, CAP))),
+        "final",
+        10**9,
+        count=8,
+    )(modes, _split_np(_field_table()), far, close, positions, velocities, cell, live)
     return potential, state, arrivals.transpose(1, 0, 2)
 
 

time: 92 us -> 92 us (level)
  the two profiles are of different devices: /device:TPU:2 before, /device:TPU:32 now
where the time goes in v4:
time: 92 us; the launch traced here: 91.5 us
  starting transfers between devices  31.4 us (34%)
  blocking collectives  26 us (28%)
  waiting for transfers between devices  22.2 us (24%)
  Pallas kernels  10.5 us (11%)
    all_to_all x1, starting transfers between devices, per_device(): sectors = exchange(layered, z_axes)  15.2 us
    all_to_all x1, blocking collectives, per_device(): columns = exchange(spectrum, plane_axes)  14.6 us
    all_to_all x1, waiting for transfers between devices, per_device(): sectors = exchange(layered, z_axes)  11.4 us
    all_to_all x1, blocking collectives, per_device(): waves = exchange(solved, plane_axes)  11.3 us
    ppermute x1, starting transfers between devices, per_device(): close = lax.ppermute(near, 'az', [(i, i ^ 1) for i in range(8)])  9.14 us
    all_to_all x1, waiting for transfers between devices, per_device(): modes = exchange(angles, z_axes)  8.44 us
    all_to_all x1, starting transfers between devices, per_device(): modes = exchange(angles, z_axes)  3.64 us
    ppermute x1, starting transfers between devices, per_device(): lax.ppermute(wrap, 'az', [(i, (i + 1) % 8 if i % 2 else (i + 7) % 8) for...  3.37 us
  transfers between devices with their start and end apart: 4, of which 3 were waited for; matrix products, arithmetic and copies ran while one was open for 0% of the time, Pallas kernels for 2%

profile of v4, /device:TPU:32, one launch (start us, length us, event | category | flops | bytes accessed | tf_op | source)
XLA Modules:
  0.0 91.5 jit_solution(8312171276489729223)
XLA Ops:
  0.6 3.0 %deposit.1 = f32[16,3,2,256]{3,2,1,0:T(2,128)} custom-call(s32[1,4096]{1,0:T(1,128)} %bitcast.4, bf16[4096]{0:T(1024)(128)(2,1)} %mass_ref.1, s32[2,256]{1,0:T(2,128)} %lists_ref), custom_call_target="tpu_custom_call" | custom-call | flops 1000000000 | bytes 1048576 | tf_op jit(solution)/shard_map/deposit/pallas_call | solution.py:471
  3.6 0.0 copy-start.11
  3.6 15.2 %all-to-all-start = ((f32[16,3,2,256]{3,2,1,0:T(2,128)}), f32[16,3,2,256]{3,2,1,0:T(2,128)S(1)}, u32[]{:S(2)}, u32[]{:S(2)}) async-start(f32[16,3,2,256]{3,2,1,0:T(2,128)} %deposit.1), calls=%async_computation | async-start | bytes 196608 | tf_op jit(solution)/shard_map/all_to_all | solution.py:487
  18.8 0.0 copy-done.11
  18.8 0.0 copy-start
  18.9 0.0 copy-start.1
  18.9 0.0 copy-start.3
  18.9 0.0 copy-start.4
  18.9 0.9 factor.1
  19.8 0.0 copy-start.5
  19.8 0.0 copy-start.6
  19.8 0.0 copy-done
  19.8 0.0 copy-done.1
  19.8 0.0 copy-done.3
  19.8 0.0 copy-done.4
  19.8 0.6 copy-done.5
  20.5 0.0 copy-done.6
  20.5 0.0 copy-start.7
  20.5 0.0 copy-start.10
  20.5 0.8 pick.1
  21.3 11.4 %all-to-all-done.x_ref.cells_ref = f32[16,3,2,256]{3,2,1,0:T(2,128)S(1)} async-done(((f32[16,3,2,256]{3,2,1,0:T(2,128)}), f32[16,3,2,256]{3,2,1,0:T(2,128)S(1)}, u32[]{:S(2)}, u32[]{:S(2)}) %all-to-all-start) | async-done | bytes 98336 | tf_op jit(solution)/shard_map/all_to_all | solution.py:487
  32.7 0.0 copy-done.7
  32.7 0.0 copy-done.10
  32.7 0.3 forward.1
  33.0 14.6 %all_to_all.20.source_ref = f32[32,2,256]{2,1,0:T(2,128)S(1)} all-to-all(f32[32,2,256]{2,1,0:T(2,128)S(1)} %forward.1), channel_id=1, replica_groups=mesh['az'=8,'x'=4,'zh'=2,'y'=4,'c'=2] {'x','y','c'}, dimensions={0} | all-to-all | bytes 131072 | tf_op jit(solution)/shard_map/all_to_all | solution.py:503
  47.6 0.2 solve.1
  47.8 0.0 copy-start.9
  47.8 11.3 %all_to_all.21.x_ref = f32[32,4,256]{2,1,0:T(4,128)S(1)} all-to-all(f32[32,4,256]{2,1,0:T(4,128)S(1)} %solve.1), channel_id=1, replica_groups=mesh['az'=8,'x'=4,'zh'=2,'y'=4,'c'=2] {'x','y','c'}, dimensions={0} | all-to-all | bytes 262144 | tf_op jit(solution)/shard_map/all_to_all | solution.py:512
  59.2 0.0 copy-done.9
  59.2 3.2 %inverse.1 = f32[16,9,2,256]{3,2,1,0:T(2,128)} custom-call(f32[32,4,256]{2,1,0:T(4,128)S(1)} %all_to_all.21.x_ref, f32[128,256]{1,0:T(8,128)S(1)} %copy-done.10, bf16[1024,256]{1,0:T(8,128)(2,1)S(1)} %copy-done.7, f32[16,3,2,256]{3,2,1,0:T(2,128)S(1)} %all-to-all-done.x_ref.cells_ref, bf16[16,2,32,64]{3,2,1,0:T(8,128)(2,1)S(1)} %copy-done.9), custom_call_target="tpu_custom_call" | custom-call | flops 1000000000 | bytes 1048576 | tf_op jit(solution)/shard_map/inverse/pallas_call | solution.py:513
  62.3 0.0 copy-start.2
  62.3 0.0 copy-start.8
  62.3 3.6 %all-to-all-start.3 = ((f32[16,9,2,256]{3,2,1,0:T(2,128)}), f32[16,9,2,256]{3,2,1,0:T(2,128)S(1)}, u32[]{:S(2)}, u32[]{:S(2)}) async-start(f32[16,9,2,256]{3,2,1,0:T(2,128)} %inverse.1), calls=%async_computation.3 | async-start | bytes 589824 | tf_op jit(solution)/shard_map/all_to_all | solution.py:517
  66.0 3.4 %collective-permute-start = (f32[16,256]{1,0:T(8,128)S(1)}, f32[16,256]{1,0:T(8,128)S(1)}, u32[]{:S(2)}, u32[]{:S(2)}) collective-permute-start(f32[16,256]{1,0:T(8,128)S(1)} %get-tuple-element.42), channel_id=1, source_target_pairs={{0,448},{64,128},{128,64},{192,256},{256,192},{320,384},{384,320},... | collective-permute-start | bytes 49160 | tf_op jit(solution)/shard_map/ppermute | solution.py:518
  69.4 9.1 %collective-permute-start.1 = (f32[16,256]{1,0:T(8,128)S(1)}, f32[16,256]{1,0:T(8,128)S(1)}, u32[]{:S(2)}, u32[]{:S(2)}) collective-permute-start(f32[16,256]{1,0:T(8,128)S(1)} %get-tuple-element.43), channel_id=1, source_target_pairs={{0,64},{64,0},{128,192},{192,128},{256,320},{320,256},{384,448},{4... | collective-permute-start | bytes 49160 | tf_op jit(solution)/shard_map/ppermute | solution.py:519
  78.5 0.0 collective-permute-done.far_ref
  78.5 2.4 %collective-permute-done.1.close_ref = f32[16,256]{1,0:T(8,128)S(1)} collective-permute-done((f32[16,256]{1,0:T(8,128)S(1)}, f32[16,256]{1,0:T(8,128)S(1)}, u32[]{:S(2)}, u32[]{:S(2)}) %collective-permute-start.1) | collective-permute-done | bytes 16416 | tf_op jit(solution)/shard_map/ppermute | solution.py:519
  80.9 8.4 %all-to-all-done.3.modes_ref = f32[16,9,2,256]{3,2,1,0:T(2,128)S(1)} async-done(((f32[16,9,2,256]{3,2,1,0:T(2,128)}), f32[16,9,2,256]{3,2,1,0:T(2,128)S(1)}, u32[]{:S(2)}, u32[]{:S(2)}) %all-to-all-start.3) | async-done | bytes 294944 | tf_op jit(solution)/shard_map/all_to_all | solution.py:517
  89.3 0.0 copy-done.2
  89.3 0.0 copy-done.8
  89.3 2.2 %final.1 = (f32[64,1,256]{2,1,0:T(1,128)}, f32[6,4096]{1,0:T(8,128)}, f32[7,2,256]{2,1,0:T(2,128)}) custom-call(f32[16,9,2,256]{3,2,1,0:T(2,128)S(1)} %all-to-all-done.3.modes_ref, bf16[512,192]{1,0:T(8,128)(2,1)S(1)} %copy-done.8, f32[16,256]{1,0:T(8,128)S(1)} %collective-permute-done.far_ref, f32[16,256]{1,0:T(8,128)S(1)} %collective-permute-done.1.close_ref, ...), custom_call_target="tpu_custom_call" | custom-call | flops 1000000000 | bytes 1048576 | tf_op jit(solution)/shard_map/final/pallas_call | solution.py:520
Async XLA Ops:
  3.6 15.2 %copy-start.11 = (f32[64]{0:T(128)S(1)}, f32[64]{0:T(128)}, u32[]{:S(2)}) copy-start(f32[64]{0:T(128)} %constant.10.clone.eigen_ref) | copy-start | bytes 772
  3.6 29.0 %all-to-all-start = ((f32[16,3,2,256]{3,2,1,0:T(2,128)}), f32[16,3,2,256]{3,2,1,0:T(2,128)S(1)}, u32[]{:S(2)}, u32[]{:S(2)}) async-start(f32[16,3,2,256]{3,2,1,0:T(2,128)} %deposit.1), calls=%async_computation | async-start | bytes 196608 | tf_op jit(solution)/shard_map/all_to_all | solution.py:487
  18.8 1.0 %copy-start = (f32[3,4096]{1,0:T(4,128)S(1)}, f32[3,4096]{1,0:T(4,128)}, u32[]{:S(2)}) copy-start(f32[3,4096]{1,0:T(4,128)} %positions_ref.3) | copy-start | bytes 147460
  18.9 1.0 %copy-start.1 = (f32[3,4096]{1,0:T(4,128)S(1)}, f32[3,4096]{1,0:T(4,128)}, u32[]{:S(2)}) copy-start(f32[3,4096]{1,0:T(4,128)} %velocities_ref.3) | copy-start | bytes 147460
  18.9 1.0 %copy-start.3 = (s32[4096]{0:T(1024)S(1)}, s32[4096]{0:T(1024)}, u32[]{:S(2)}) copy-start(s32[4096]{0:T(1024)} %param.16) | copy-start | bytes 49156
  18.9 1.0 %copy-start.4 = (bf16[4096]{0:T(1024)(128)(2,1)S(1)}, bf16[4096]{0:T(1024)(128)(2,1)}, u32[]{:S(2)}) copy-start(bf16[4096]{0:T(1024)(128)(2,1)} %mass_ref.1) | copy-start | bytes 24580
  19.8 0.7 copy-start.5
  19.8 0.7 copy-start.6
  20.5 12.2 %copy-start.7 = (bf16[1024,256]{1,0:T(8,128)(2,1)S(1)}, bf16[1024,256]{1,0:T(8,128)(2,1)}, u32[]{:S(2)}) copy-start(bf16[1024,256]{1,0:T(8,128)(2,1)} %constant.12.clone.table_ref) | copy-start | bytes 1572868
  20.5 12.2 %copy-start.10 = (f32[128,256]{1,0:T(8,128)S(1)}, f32[128,256]{1,0:T(8,128)}, u32[]{:S(2)}) copy-start(f32[128,256]{1,0:T(8,128)} %constant.11.clone.twist_ref) | copy-start | bytes 393220
  47.8 11.4 %copy-start.9 = (bf16[16,2,32,64]{3,2,1,0:T(8,128)(2,1)S(1)}, bf16[16,2,32,64]{3,2,1,0:T(8,128)(2,1)}, u32[]{:S(2)}) copy-start(bf16[16,2,32,64]{3,2,1,0:T(8,128)(2,1)} %constant.13.clone.weight_ref) | copy-start | bytes 393220
  62.3 27.0 %copy-start.2 = (s32[4096]{0:T(1024)S(1)}, s32[4096]{0:T(1024)}, u32[]{:S(2)}) copy-start(s32[4096]{0:T(1024)} %param.15) | copy-start | bytes 49156
  62.3 27.0 %copy-start.8 = (bf16[512,192]{1,0:T(8,128)(2,1)S(1)}, bf16[512,192]{1,0:T(8,128)(2,1)}, u32[]{:S(2)}) copy-start(bf16[512,192]{1,0:T(8,128)(2,1)} %constant.14.clone.table_ref) | copy-start | bytes 589828
  62.3 27.0 %all-to-all-start.3 = ((f32[16,9,2,256]{3,2,1,0:T(2,128)}), f32[16,9,2,256]{3,2,1,0:T(2,128)S(1)}, u32[]{:S(2)}, u32[]{:S(2)}) async-start(f32[16,9,2,256]{3,2,1,0:T(2,128)} %inverse.1), calls=%async_computation.3 | async-start | bytes 589824 | tf_op jit(solution)/shard_map/all_to_all | solution.py:517
  66.0 12.5 %collective-permute-start = (f32[16,256]{1,0:T(8,128)S(1)}, f32[16,256]{1,0:T(8,128)S(1)}, u32[]{:S(2)}, u32[]{:S(2)}) collective-permute-start(f32[16,256]{1,0:T(8,128)S(1)} %get-tuple-element.42), channel_id=1, source_target_pairs={{0,448},{64,128},{128,64},{192,256},{256,192},{320,384},{384,320},... | collective-permute-start | bytes 49160 | tf_op jit(solution)/shard_map/ppermute | solution.py:518
  69.4 11.5 %collective-permute-start.1 = (f32[16,256]{1,0:T(8,128)S(1)}, f32[16,256]{1,0:T(8,128)S(1)}, u32[]{:S(2)}, u32[]{:S(2)}) collective-permute-start(f32[16,256]{1,0:T(8,128)S(1)} %get-tuple-element.43), channel_id=1, source_target_pairs={{0,64},{64,0},{128,192},{192,128},{256,320},{320,256},{384,448},{4... | collective-permute-start | bytes 49160 | tf_op jit(solution)/shard_map/ppermute | solution.py:519

commit v5 on v4

--- a/solution.py
+++ b/solution.py
@@ -68,15 +68,10 @@
 
 def _weight_table():
     table = _field_table().reshape(4, HEIGHTS, 16, 3, 4)
-    sine = table[1, :, :, 1, :]
-    vertical = table[3, :, :, 0, :]
-    exact = np.zeros((16, 2, 2, 2, 4, HEIGHTS))
-    for zh in range(2):
-        exact[:, zh, 0, zh] = sine.transpose(1, 2, 0)
-        exact[:, zh, 1, zh] = vertical.transpose(1, 2, 0)
-    exact = exact.reshape(16 * 2 * 16, HEIGHTS)
-    both = _split_np(exact).reshape(2, 16, 2, 16, HEIGHTS)
-    return both.transpose(1, 2, 0, 3, 4).reshape(16, 2, 32, HEIGHTS)
+    exact = np.zeros((16, 2, 2, 4, 128), np.float32)
+    exact[:, 0, :, :, :HEIGHTS] = table[1, :, :, 1, :].transpose(1, 2, 0)[:, None]
+    exact[:, 1, :, :, :HEIGHTS] = table[3, :, :, 0, :].transpose(1, 2, 0)[:, None]
+    return exact.reshape(16, 16, 128)
 
 
 def _eigen():
@@ -104,10 +99,21 @@
     return _dot(a_high, b_high) + (_dot(a_low, b_high) + _dot(a_high, b_low))
 
 
+def _rows(rows, lanes):
+    return lax.broadcasted_iota(jnp.int32, (rows, lanes), 0).astype(F32).astype(BF16)
+
+
 def _one_hot(ids, rows):
     lanes = ids.shape[1]
-    here = lax.broadcasted_iota(jnp.int32, (rows, lanes), 0) == ids
-    return jnp.where(here, 1.0, 0.0).astype(BF16)
+    small = jnp.broadcast_to(ids.astype(F32).astype(BF16), (rows, lanes))
+    here = _rows(rows, lanes) == small
+    return jnp.where(here, jnp.ones((), BF16), jnp.zeros((), BF16))
+
+
+def _star_hot(wanted, start):
+    offset = wanted - start
+    inside = (offset >= 0) & (offset < 256)
+    return _one_hot(jnp.where(inside, offset, -1), 256)
 
 
 def _sine_in_kernel():
@@ -128,29 +134,39 @@
     return jnp.where(negative, -value, value)
 
 
-def deposit_kernel(cells_hbm, mass_hbm, lists_hbm, out_ref, cells_ref, mass_ref, lists_ref, sems):
+def _lanes_of(table, ids):
+    return jnp.take_along_axis(table, ids, axis=1)
+
+
+def deposit_kernel(cells_hbm, mass_hbm, lists_hbm, square_hbm, out_ref, cells_ref, mass_ref, lists_ref, square_ref, sems):
     cells_copy = pltpu.make_async_copy(cells_hbm, cells_ref, sems.at[0])
     mass_copy = pltpu.make_async_copy(mass_hbm, mass_ref, sems.at[1])
     lists_copy = pltpu.make_async_copy(lists_hbm, lists_ref, sems.at[2])
     cells_copy.start()
+    square_copy = pltpu.make_async_copy(square_hbm, square_ref, sems.at[3])
     lists_copy.start()
     mass_copy.start()
+    square_copy.start()
     sine = _split(_sine_in_kernel())
     cells_copy.wait()
     lists_copy.wait()
     mass_copy.wait()
-    wanted = jnp.concatenate([lists_ref[0:1, :], lists_ref[1:2, :]], axis=1)
-    sent = jnp.zeros((16, 2 * CAP), F32)
+    square_copy.wait()
+    wanted = [lists_ref[i : i + 1, half : half + 128] for i in range(2) for half in (0, 128)]
+    wanted = jnp.concatenate(wanted + wanted, axis=0)
+    lane = wanted & 127
+    line = lax.shift_right_logical(wanted, 7)
+    sent = jnp.zeros((8, 128), jnp.int32)
+    for row in range(STARS // 128):
+        found = _lanes_of(jnp.broadcast_to(square_ref[row : row + 1, :], (8, 128)), lane)
+        sent = jnp.where(line == row, found, sent)
+    sent = sent.astype(F32)
     total = jnp.zeros((HEIGHTS, SECTOR), F32)
     for start in range(0, STARS, CHUNK):
         cell = cells_ref[:, start : start + CHUNK]
         mass = mass_ref[start : start + CHUNK].astype(F32).reshape(1, CHUNK)
         layer = lax.shift_right_logical(cell, 8)
         angle = cell & 255
-        pair = jnp.concatenate([layer, angle, jnp.zeros((14, CHUNK), jnp.int32)], axis=0)
-        ids = lax.broadcasted_iota(jnp.int32, (CHUNK, 2 * CAP), 0) + start
-        hot = jnp.where(ids == wanted, 1.0, 0.0).astype(BF16)
-        sent += _dot(pair.astype(F32).astype(BF16), hot)
         here = lax.broadcasted_iota(jnp.int32, (HEIGHTS, CHUNK), 0) == layer
         left = jnp.where(here, mass, 0.0).astype(BF16)
         right = _one_hot(angle, SECTOR)
@@ -158,12 +174,12 @@
             left, right, (((1,), (1,)), ((), ())), preferred_element_type=F32
         )
     layered = _dot3(sine, _split(total))
-    sent_cell = sent[0:1] * 256.0 + sent[1:2]
+    cells_sent = [jnp.concatenate([sent[2 * i : 2 * i + 1], sent[2 * i + 1 : 2 * i + 2]], axis=1) for i in range(2)]
     for group in range(16):
         out_ref[group, 0] = layered[4 * group : 4 * group + 2, :]
         out_ref[group, 1] = layered[4 * group + 2 : 4 * group + 4, :]
-        out_ref[group, 2, 0:1, :] = sent_cell[:, :CAP]
-        out_ref[group, 2, 1:2, :] = sent_cell[:, CAP:]
+        out_ref[group, 2, 0:1, :] = cells_sent[0]
+        out_ref[group, 2, 1:2, :] = cells_sent[1]
 
 
 def forward_kernel(x_ref, twist_ref, table_ref, out_ref):
@@ -310,25 +326,30 @@
                     row = zh * 4 + half * 2
                     out_ref[a * 2 + zh, field * 2 + half] = total[row : row + 2, :]
             tiles.append(total)
-        high, low = _split(jnp.concatenate(tiles, axis=0))
-        both = jnp.concatenate([high, low], axis=0)
-        for zh in range(2):
-            cell = cells_ref[a * 2 + zh, 2]
-            cell = jnp.concatenate([cell[0:1], cell[1:2]], axis=1).astype(jnp.int32)
-            found = _dot(both, _one_hot(cell & 255, SECTOR))
-            found = found[0:24] + found[24:48]
-            weight = _dot(weight_ref[group, zh], _one_hot(lax.shift_right_logical(cell, 8), HEIGHTS))
-            weight = weight[0:16] + weight[16:32]
-            accel = [
-                jnp.sum(weight[0:8] * found[8:16], axis=0, keepdims=True),
-                jnp.sum(weight[0:8] * found[16:24], axis=0, keepdims=True),
-                jnp.sum(weight[8:16] * found[0:8], axis=0, keepdims=True),
+        accel = [[], [], []]
+        for quarter in range(4):
+            at = 128 * (quarter % 2)
+            cell = [cells_ref[a * 2 + zh, 2, quarter // 2 : quarter // 2 + 1, at : at + 128] for zh in range(2)]
+            cell = jnp.concatenate([jnp.broadcast_to(part, (4, 128)) for part in cell], axis=0).astype(jnp.int32)
+            layer = lax.shift_right_logical(cell, 8)
+            lane = cell & 127
+            upper = (cell & 128) == 128
+            found = [
+                jnp.where(upper, _lanes_of(tile[:, 128:], lane), _lanes_of(tile[:, :128], lane))
+                for tile in tiles
             ]
-            for slot, dest in ((1, (a + 7) % 8), (0, (a + 1) % 8)):
-                lanes = slice(0, CAP) if slot == 1 else slice(CAP, 2 * CAP)
-                for field in range(3):
-                    row = slot * 3 + field
-                    out_ref[dest * 2 + zh, 6 + row // 2, row % 2 : row % 2 + 1, :] = accel[field][:, lanes]
+            sine_at = _lanes_of(weight_ref[group, 0:8, :], layer)
+            step_at = _lanes_of(weight_ref[group, 8:16, :], layer)
+            for field, term in enumerate((sine_at * found[1], sine_at * found[2], step_at * found[0])):
+                term = term + pltpu.roll(term, 2, axis=0)
+                accel[field].append(term + pltpu.roll(term, 1, axis=0))
+        for field in range(3):
+            for slot, dest, first in ((1, (a + 7) % 8, 0), (0, (a + 1) % 8, 2)):
+                pair = jnp.concatenate(accel[field][first : first + 2], axis=1)
+                row = slot * 3 + field
+                for zh in range(2):
+                    spot = 4 * zh + 3
+                    out_ref[dest * 2 + zh, 6 + row // 2, row % 2 : row % 2 + 1, :] = pair[spot : spot + 1, :]
 
 
 def pick_kernel(positions_ref, velocities_ref, mass_ref, active_ref, lists_ref, counts_ref, wrap_ref, near_ref):
@@ -352,8 +373,7 @@
         )
         pad = jnp.zeros((2, CHUNK), F32)
         left = jnp.concatenate([high, pad, middle, pad, low, pad, plain], axis=0).astype(BF16)
-        ids = lax.broadcasted_iota(jnp.int32, (CHUNK, 2 * CAP), 0) + start
-        hot = jnp.where(ids == wanted, 1.0, 0.0).astype(BF16)
+        hot = jnp.concatenate([_star_hot(wanted, start), _star_hot(wanted, start + 256)], axis=0)
         total += _dot(left, hot)
     moving = (total[0:6] + total[8:14]) + total[16:22]
     slots = lax.broadcasted_iota(jnp.int32, (1, CAP), 1)
@@ -473,16 +493,17 @@
         shape((16, 3, 2, SECTOR)),
         "deposit",
         10**9,
-        in_hbm=(0, 1, 2),
+        in_hbm=(0, 1, 2, 3),
         limit=None,
-        count=3,
+        count=4,
         scratch=[
             pltpu.VMEM((1, STARS), jnp.int32),
             pltpu.VMEM((STARS,), BF16),
             pltpu.VMEM((2, CAP), jnp.int32),
-            pltpu.SemaphoreType.DMA((3,)),
+            pltpu.VMEM((STARS // 128, 128), jnp.int32),
+            pltpu.SemaphoreType.DMA((4,)),
         ],
-    )(cell, masses, send_lists)
+    )(cell, masses, send_lists, cells.reshape(STARS // 128, 128))
     layered, eigen, late_lists = lax.optimization_barrier((layered, jnp.asarray(_eigen()), send_lists))
     sectors = exchange(layered, z_axes)
     factors = _call(

time: 92 us -> 90 us (0.978)
  Pallas kernels: 10.5 us -> 8.48 us
    pallas_call x1, Pallas kernels: 3.16 us -> 1.79 us  [per_device(): _call(inverse_kernel, shape((16, 9, 2, SECTOR)), 'inverse', 10 ** 9, coun...]
where the time goes in v5:
time: 90 us; the launch traced here: 89.5 us
  starting transfers between devices  31.4 us (35%)
  blocking collectives  26 us (29%)
  waiting for transfers between devices  22.2 us (25%)
  Pallas kernels  8.48 us (9%)
    all_to_all x1, starting transfers between devices, per_device(): sectors = exchange(layered, z_axes)  15.2 us
    all_to_all x1, blocking collectives, per_device(): columns = exchange(spectrum, plane_axes)  14.6 us
    all_to_all x1, waiting for transfers between devices, per_device(): sectors = exchange(layered, z_axes)  11.4 us
    all_to_all x1, blocking collectives, per_device(): waves = exchange(solved, plane_axes)  11.3 us
    ppermute x1, starting transfers between devices, per_device(): close = lax.ppermute(near, 'az', [(i, i ^ 1) for i in range(8)])  9.14 us
    all_to_all x1, waiting for transfers between devices, per_device(): modes = exchange(angles, z_axes)  8.44 us
    all_to_all x1, starting transfers between devices, per_device(): modes = exchange(angles, z_axes)  3.63 us
    ppermute x1, starting transfers between devices, per_device(): lax.ppermute(wrap, 'az', [(i, (i + 1) % 8 if i % 2 else (i + 7) % 8) for...  3.37 us
  transfers between devices with their start and end apart: 4, of which 3 were waited for; matrix products, arithmetic and copies ran while one was open for 0% of the time, Pallas kernels for 2%

profile of v5, /device:TPU:32, one launch (start us, length us, event | category | flops | bytes accessed | tf_op | source)
XLA Modules:
  0.0 89.5 jit_solution(16718109946449731995)
XLA Ops:
  0.6 2.4 %deposit.1 = f32[16,3,2,256]{3,2,1,0:T(2,128)} custom-call(s32[1,4096]{1,0:T(1,128)} %bitcast.5, bf16[4096]{0:T(1024)(128)(2,1)} %mass_ref.1, s32[2,256]{1,0:T(2,128)} %lists_ref, s32[32,128]{1,0:T(8,128)} %bitcast.6), custom_call_target="tpu_custom_call" | custom-call | flops 1000000000 | bytes 1048576 | tf_op jit(solution)/shard_map/deposit/pallas_call | solution.py:491
  3.0 0.0 copy-start.11
  3.0 15.2 %all-to-all-start = ((f32[16,3,2,256]{3,2,1,0:T(2,128)}), f32[16,3,2,256]{3,2,1,0:T(2,128)S(1)}, u32[]{:S(2)}, u32[]{:S(2)}) async-start(f32[16,3,2,256]{3,2,1,0:T(2,128)} %deposit.1), calls=%async_computation | async-start | bytes 196608 | tf_op jit(solution)/shard_map/all_to_all | solution.py:508
  18.3 0.0 copy-done.11
  18.3 0.0 copy-start
  18.3 0.0 copy-start.1
  18.3 0.0 copy-start.3
  18.3 0.0 copy-start.4
  18.3 0.9 factor.1
  19.2 0.0 copy-start.5
  19.2 0.0 copy-start.6
  19.2 0.0 copy-done
  19.2 0.0 copy-done.1
  19.3 0.0 copy-done.3
  19.3 0.0 copy-done.4
  19.3 0.6 copy-done.5
  19.9 0.0 copy-done.6
  19.9 0.0 copy-start.7
  19.9 0.0 copy-start.9
  19.9 0.8 pick.1
  20.7 11.4 %all-to-all-done.x_ref.cells_ref = f32[16,3,2,256]{3,2,1,0:T(2,128)S(1)} async-done(((f32[16,3,2,256]{3,2,1,0:T(2,128)}), f32[16,3,2,256]{3,2,1,0:T(2,128)S(1)}, u32[]{:S(2)}, u32[]{:S(2)}) %all-to-all-start) | async-done | bytes 98336 | tf_op jit(solution)/shard_map/all_to_all | solution.py:508
  32.1 0.0 copy-done.7
  32.1 0.0 copy-done.9
  32.1 0.3 forward.1
  32.4 14.6 %all_to_all.20.source_ref = f32[32,2,256]{2,1,0:T(2,128)S(1)} all-to-all(f32[32,2,256]{2,1,0:T(2,128)S(1)} %forward.1), channel_id=1, replica_groups=mesh['az'=8,'x'=4,'zh'=2,'y'=4,'c'=2] {'x','y','c'}, dimensions={0} | all-to-all | bytes 131072 | tf_op jit(solution)/shard_map/all_to_all | solution.py:524
  47.1 0.2 solve.1
  47.3 0.0 copy-start.10
  47.3 11.3 %all_to_all.21.x_ref = f32[32,4,256]{2,1,0:T(4,128)S(1)} all-to-all(f32[32,4,256]{2,1,0:T(4,128)S(1)} %solve.1), channel_id=1, replica_groups=mesh['az'=8,'x'=4,'zh'=2,'y'=4,'c'=2] {'x','y','c'}, dimensions={0} | all-to-all | bytes 262144 | tf_op jit(solution)/shard_map/all_to_all | solution.py:533
  58.6 0.0 copy-done.10
  58.6 1.8 %inverse.1 = f32[16,9,2,256]{3,2,1,0:T(2,128)} custom-call(f32[32,4,256]{2,1,0:T(4,128)S(1)} %all_to_all.21.x_ref, f32[128,256]{1,0:T(8,128)S(1)} %copy-done.9, bf16[1024,256]{1,0:T(8,128)(2,1)S(1)} %copy-done.7, f32[16,3,2,256]{3,2,1,0:T(2,128)S(1)} %all-to-all-done.x_ref.cells_ref, f32[16,16,128]{2,1,0:T(8,128)S(1)} %copy-done.10), custom_call_target="tpu_custom_call" | custom-call | flops 1000000000 | bytes 1048576 | tf_op jit(solution)/shard_map/inverse/pallas_call | solution.py:534
  60.4 0.0 copy-start.2
  60.4 0.0 copy-start.8
  60.4 3.6 %all-to-all-start.3 = ((f32[16,9,2,256]{3,2,1,0:T(2,128)}), f32[16,9,2,256]{3,2,1,0:T(2,128)S(1)}, u32[]{:S(2)}, u32[]{:S(2)}) async-start(f32[16,9,2,256]{3,2,1,0:T(2,128)} %inverse.1), calls=%async_computation.3 | async-start | bytes 589824 | tf_op jit(solution)/shard_map/all_to_all | solution.py:538
  64.0 3.4 %collective-permute-start = (f32[16,256]{1,0:T(8,128)S(1)}, f32[16,256]{1,0:T(8,128)S(1)}, u32[]{:S(2)}, u32[]{:S(2)}) collective-permute-start(f32[16,256]{1,0:T(8,128)S(1)} %get-tuple-element.42), channel_id=1, source_target_pairs={{0,448},{64,128},{128,64},{192,256},{256,192},{320,384},{384,320},... | collective-permute-start | bytes 49160 | tf_op jit(solution)/shard_map/ppermute | solution.py:539
  67.4 9.1 %collective-permute-start.1 = (f32[16,256]{1,0:T(8,128)S(1)}, f32[16,256]{1,0:T(8,128)S(1)}, u32[]{:S(2)}, u32[]{:S(2)}) collective-permute-start(f32[16,256]{1,0:T(8,128)S(1)} %get-tuple-element.43), channel_id=1, source_target_pairs={{0,64},{64,0},{128,192},{192,128},{256,320},{320,256},{384,448},{4... | collective-permute-start | bytes 49160 | tf_op jit(solution)/shard_map/ppermute | solution.py:540
  76.6 0.0 collective-permute-done.far_ref
  76.6 2.4 %collective-permute-done.1.close_ref = f32[16,256]{1,0:T(8,128)S(1)} collective-permute-done((f32[16,256]{1,0:T(8,128)S(1)}, f32[16,256]{1,0:T(8,128)S(1)}, u32[]{:S(2)}, u32[]{:S(2)}) %collective-permute-start.1) | collective-permute-done | bytes 16416 | tf_op jit(solution)/shard_map/ppermute | solution.py:540
  78.9 8.4 %all-to-all-done.3.modes_ref = f32[16,9,2,256]{3,2,1,0:T(2,128)S(1)} async-done(((f32[16,9,2,256]{3,2,1,0:T(2,128)}), f32[16,9,2,256]{3,2,1,0:T(2,128)S(1)}, u32[]{:S(2)}, u32[]{:S(2)}) %all-to-all-start.3) | async-done | bytes 294944 | tf_op jit(solution)/shard_map/all_to_all | solution.py:538
  87.4 0.0 copy-done.2
  87.4 0.0 copy-done.8
  87.4 2.1 %final.1 = (f32[64,1,256]{2,1,0:T(1,128)}, f32[6,4096]{1,0:T(8,128)}, f32[7,2,256]{2,1,0:T(2,128)}) custom-call(f32[16,9,2,256]{3,2,1,0:T(2,128)S(1)} %all-to-all-done.3.modes_ref, bf16[512,192]{1,0:T(8,128)(2,1)S(1)} %copy-done.8, f32[16,256]{1,0:T(8,128)S(1)} %collective-permute-done.far_ref, f32[16,256]{1,0:T(8,128)S(1)} %collective-permute-done.1.close_ref, ...), custom_call_target="tpu_custom_call" | custom-call | flops 1000000000 | bytes 1048576 | tf_op jit(solution)/shard_map/final/pallas_call | solution.py:541
Async XLA Ops:
  3.0 15.2 %copy-start.11 = (f32[64]{0:T(128)S(1)}, f32[64]{0:T(128)}, u32[]{:S(2)}) copy-start(f32[64]{0:T(128)} %constant.10.clone.eigen_ref) | copy-start | bytes 772
  3.0 29.0 %all-to-all-start = ((f32[16,3,2,256]{3,2,1,0:T(2,128)}), f32[16,3,2,256]{3,2,1,0:T(2,128)S(1)}, u32[]{:S(2)}, u32[]{:S(2)}) async-start(f32[16,3,2,256]{3,2,1,0:T(2,128)} %deposit.1), calls=%async_computation | async-start | bytes 196608 | tf_op jit(solution)/shard_map/all_to_all | solution.py:508
  18.3 1.0 %copy-start = (f32[3,4096]{1,0:T(4,128)S(1)}, f32[3,4096]{1,0:T(4,128)}, u32[]{:S(2)}) copy-start(f32[3,4096]{1,0:T(4,128)} %positions_ref.3) | copy-start | bytes 147460
  18.3 1.0 %copy-start.1 = (f32[3,4096]{1,0:T(4,128)S(1)}, f32[3,4096]{1,0:T(4,128)}, u32[]{:S(2)}) copy-start(f32[3,4096]{1,0:T(4,128)} %velocities_ref.3) | copy-start | bytes 147460
  18.3 1.0 %copy-start.3 = (s32[4096]{0:T(1024)S(1)}, s32[4096]{0:T(1024)}, u32[]{:S(2)}) copy-start(s32[4096]{0:T(1024)} %param.16) | copy-start | bytes 49156
  18.3 1.0 %copy-start.4 = (bf16[4096]{0:T(1024)(128)(2,1)S(1)}, bf16[4096]{0:T(1024)(128)(2,1)}, u32[]{:S(2)}) copy-start(bf16[4096]{0:T(1024)(128)(2,1)} %mass_ref.1) | copy-start | bytes 24580
  19.2 0.7 copy-start.5
  19.2 0.7 copy-start.6
  19.9 12.2 %copy-start.7 = (bf16[1024,256]{1,0:T(8,128)(2,1)S(1)}, bf16[1024,256]{1,0:T(8,128)(2,1)}, u32[]{:S(2)}) copy-start(bf16[1024,256]{1,0:T(8,128)(2,1)} %constant.12.clone.table_ref) | copy-start | bytes 1572868
  19.9 12.2 %copy-start.9 = (f32[128,256]{1,0:T(8,128)S(1)}, f32[128,256]{1,0:T(8,128)}, u32[]{:S(2)}) copy-start(f32[128,256]{1,0:T(8,128)} %constant.11.clone.twist_ref) | copy-start | bytes 393220
  47.3 11.4 %copy-start.10 = (f32[16,16,128]{2,1,0:T(8,128)S(1)}, f32[16,16,128]{2,1,0:T(8,128)}, u32[]{:S(2)}) copy-start(f32[16,16,128]{2,1,0:T(8,128)} %constant.13.clone.weight_ref) | copy-start | bytes 393220
  60.4 27.0 %copy-start.2 = (s32[4096]{0:T(1024)S(1)}, s32[4096]{0:T(1024)}, u32[]{:S(2)}) copy-start(s32[4096]{0:T(1024)} %param.15) | copy-start | bytes 49156
  60.4 27.0 %copy-start.8 = (bf16[512,192]{1,0:T(8,128)(2,1)S(1)}, bf16[512,192]{1,0:T(8,128)(2,1)}, u32[]{:S(2)}) copy-start(bf16[512,192]{1,0:T(8,128)(2,1)} %constant.14.clone.table_ref) | copy-start | bytes 589828
  60.4 27.0 %all-to-all-start.3 = ((f32[16,9,2,256]{3,2,1,0:T(2,128)}), f32[16,9,2,256]{3,2,1,0:T(2,128)S(1)}, u32[]{:S(2)}, u32[]{:S(2)}) async-start(f32[16,9,2,256]{3,2,1,0:T(2,128)} %inverse.1), calls=%async_computation.3 | async-start | bytes 589824 | tf_op jit(solution)/shard_map/all_to_all | solution.py:538
  64.0 12.5 %collective-permute-start = (f32[16,256]{1,0:T(8,128)S(1)}, f32[16,256]{1,0:T(8,128)S(1)}, u32[]{:S(2)}, u32[]{:S(2)}) collective-permute-start(f32[16,256]{1,0:T(8,128)S(1)} %get-tuple-element.42), channel_id=1, source_target_pairs={{0,448},{64,128},{128,64},{192,256},{256,192},{320,384},{384,320},... | collective-permute-start | bytes 49160 | tf_op jit(solution)/shard_map/ppermute | solution.py:539
  67.4 11.5 %collective-permute-start.1 = (f32[16,256]{1,0:T(8,128)S(1)}, f32[16,256]{1,0:T(8,128)S(1)}, u32[]{:S(2)}, u32[]{:S(2)}) collective-permute-start(f32[16,256]{1,0:T(8,128)S(1)} %get-tuple-element.43), channel_id=1, source_target_pairs={{0,64},{64,0},{128,192},{192,128},{256,320},{320,256},{384,448},{4... | collective-permute-start | bytes 49160 | tf_op jit(solution)/shard_map/ppermute | solution.py:540

commit v6 on v5

--- a/solution.py
+++ b/solution.py
@@ -81,7 +81,7 @@
 
 def _row_of(radius):
     x, zh, y, c = radius >> 4, (radius >> 3) & 1, (radius >> 1) & 3, radius & 1
-    return (((x * 4 + y) * 2 + c) * 2) + zh
+    return (((y * 2 + c) * 4 + x) * 2) + zh
 
 
 def _split(value):
@@ -185,7 +185,7 @@
 def forward_kernel(x_ref, twist_ref, table_ref, out_ref):
     tiles = []
     for a in range(8):
-        parts = [x_ref[2 * a + zh, half] for zh in range(2) for half in range(2)]
+        parts = [x_ref[zh * 8 + a, half] for zh in range(2) for half in range(2)]
         tiles.append(jnp.concatenate(parts, axis=0))
     rows = []
     for n2 in range(8):
@@ -208,8 +208,8 @@
 
 
 def factor_kernel(eigen_ref, inverse_ref, carry_ref, factor_ref, joint_ref):
-    group = lax.axis_index("az") * 2 + lax.axis_index("zh")
-    place = (lax.axis_index("x") * 4 + lax.axis_index("y")) * 2 + lax.axis_index("c")
+    group = lax.axis_index("zh") * 8 + lax.axis_index("az")
+    place = (lax.axis_index("y") * 2 + lax.axis_index("c")) * 4 + lax.axis_index("x")
     level = group * 4 + lax.rem(place, 4)
     residue = lax.div(place, 4)
     eigen = eigen_ref[level]
@@ -288,7 +288,7 @@
 
 
 def inverse_kernel(x_ref, twist_ref, table_ref, cells_ref, weight_ref, out_ref):
-    group = lax.axis_index("az") * 2 + lax.axis_index("zh")
+    group = lax.axis_index("zh") * 8 + lax.axis_index("az")
     fields = [[], [], []]
     for n2 in range(8):
         pair = []
@@ -324,12 +324,12 @@
             for zh in range(2):
                 for half in range(2):
                     row = zh * 4 + half * 2
-                    out_ref[a * 2 + zh, field * 2 + half] = total[row : row + 2, :]
+                    out_ref[zh * 8 + a, field * 2 + half] = total[row : row + 2, :]
             tiles.append(total)
         accel = [[], [], []]
         for quarter in range(4):
             at = 128 * (quarter % 2)
-            cell = [cells_ref[a * 2 + zh, 2, quarter // 2 : quarter // 2 + 1, at : at + 128] for zh in range(2)]
+            cell = [cells_ref[zh * 8 + a, 2, quarter // 2 : quarter // 2 + 1, at : at + 128] for zh in range(2)]
             cell = jnp.concatenate([jnp.broadcast_to(part, (4, 128)) for part in cell], axis=0).astype(jnp.int32)
             layer = lax.shift_right_logical(cell, 8)
             lane = cell & 127
@@ -349,7 +349,7 @@
                 row = slot * 3 + field
                 for zh in range(2):
                     spot = 4 * zh + 3
-                    out_ref[dest * 2 + zh, 6 + row // 2, row % 2 : row % 2 + 1, :] = pair[spot : spot + 1, :]
+                    out_ref[zh * 8 + dest, 6 + row // 2, row % 2 : row % 2 + 1, :] = pair[spot : spot + 1, :]
 
 
 def pick_kernel(positions_ref, velocities_ref, mass_ref, active_ref, lists_ref, counts_ref, wrap_ref, near_ref):
@@ -379,7 +379,7 @@
     slots = lax.broadcasted_iota(jnp.int32, (1, CAP), 1)
     keep = [jnp.where(slots < counts_ref[:, i : i + 1], 1.0, 0.0) for i in range(2)]
     rows = jnp.concatenate(
-        [moving, total[24:26], jnp.concatenate(keep, axis=1), jnp.zeros((7, 2 * CAP), F32)], axis=0
+        [moving, total[24:25] * jnp.concatenate(keep, axis=1), total[25:26]], axis=0
     )
     down = rows[:, :CAP]
     up = rows[:, CAP:]
@@ -444,7 +444,7 @@
             sums[slot * 3 : slot * 3 + 3],
             picked[7:8],
         )
-        keep = picked[8:9] > 0.5
+        keep = picked[6:7] > 0.0
         for row, value in enumerate(state + [picked[6:7]]):
             arrive_ref[row, slot : slot + 1, :] = jnp.where(keep, value, 0.0)
 
@@ -481,7 +481,7 @@
 
 def per_device(positions, velocities, masses, cells, active, send_lists, send_counts):
     shape = functools.partial(jax.ShapeDtypeStruct, dtype=F32)
-    z_axes, plane_axes = ("az", "zh"), ("x", "y", "c")
+    z_axes, plane_axes = ("zh", "az"), ("y", "c", "x")
     exchange = functools.partial(lax.all_to_all, split_axis=0, concat_axis=0, tiled=True)
     table = _split_np(_trig())
     twist = _twist()
@@ -514,7 +514,7 @@
         in_smem=(0,),
         count=1,
     )(eigen)
-    wrap, near = _call(pick_kernel, (shape((16, CAP)), shape((16, CAP))), "pick", 10**9, count=6)(
+    wrap, near = _call(pick_kernel, (shape((8, CAP)), shape((8, CAP))), "pick", 10**9, count=6)(
         positions, velocities, masses, live, late_lists, send_counts.reshape(1, 2)
     )
     sectors, factors, wrap, near = lax.optimization_barrier((sectors, factors, wrap, near))

time: 90 us -> 86.2 us (0.958)
  the two profiles are of different devices: /device:TPU:32 before, /device:TPU:2 now
where the time goes in v6:
time: 86.2 us; the launch traced here: 85.7 us
  starting transfers between devices  31.3 us (36%)
  blocking collectives  24.9 us (29%)
  waiting for transfers between devices  19.6 us (23%)
  Pallas kernels  8.48 us (10%)
    all_to_all x1, starting transfers between devices, per_device(): sectors = exchange(layered, z_axes)  15.2 us
    all_to_all x1, blocking collectives, per_device(): columns = exchange(spectrum, plane_axes)  13.6 us
    all_to_all x1, blocking collectives, per_device(): waves = exchange(solved, plane_axes)  11.3 us
    all_to_all x1, waiting for transfers between devices, per_device(): sectors = exchange(layered, z_axes)  11.1 us
    ppermute x1, starting transfers between devices, per_device(): lax.ppermute(wrap, 'az', [(i, (i + 1) % 8 if i % 2 else (i + 7) % 8) for...  10.4 us
    ppermute x1, waiting for transfers between devices, per_device(): lax.ppermute(wrap, 'az', [(i, (i + 1) % 8 if i % 2 else (i + 7) % 8) for...  5.5 us
    all_to_all x1, starting transfers between devices, per_device(): modes = exchange(angles, z_axes)  3.71 us
    all_to_all x1, waiting for transfers between devices, per_device(): modes = exchange(angles, z_axes)  2.95 us
  transfers between devices with their start and end apart: 4, of which 3 were waited for; matrix products, arithmetic and copies ran while one was open for 0% of the time, Pallas kernels for 2%

profile of v6, /device:TPU:2, one launch (start us, length us, event | category | flops | bytes accessed | tf_op | source)
XLA Modules:
  0.0 85.7 jit_solution(2165379576255447664)
XLA Ops:
  0.6 2.4 %deposit.1 = f32[16,3,2,256]{3,2,1,0:T(2,128)} custom-call(s32[1,4096]{1,0:T(1,128)} %bitcast.5, bf16[4096]{0:T(1024)(128)(2,1)} %mass_ref.1, s32[2,256]{1,0:T(2,128)} %lists_ref, s32[32,128]{1,0:T(8,128)} %bitcast.6), custom_call_target="tpu_custom_call" | custom-call | flops 1000000000 | bytes 1048576 | tf_op jit(solution)/shard_map/deposit/pallas_call | solution.py:491
  3.0 0.0 copy-start.11
  3.0 15.2 %all-to-all-start = ((f32[16,3,2,256]{3,2,1,0:T(2,128)}), f32[16,3,2,256]{3,2,1,0:T(2,128)S(1)}, u32[]{:S(2)}, u32[]{:S(2)}) async-start(f32[16,3,2,256]{3,2,1,0:T(2,128)} %deposit.1), calls=%async_computation | async-start | bytes 196608 | tf_op jit(solution)/shard_map/all_to_all | solution.py:508
  18.3 0.0 copy-done.11
  18.3 0.0 copy-start
  18.3 0.0 copy-start.1
  18.3 0.0 copy-start.3
  18.3 0.0 copy-start.4
  18.3 0.9 %factor.1 = (f32[64,256]{1,0:T(8,128)S(1)}, f32[64,256]{1,0:T(8,128)S(1)}, f32[64,256]{1,0:T(8,128)S(1)}, f32[8,256]{1,0:T(8,128)S(1)}) custom-call(f32[64]{0:T(128)S(1)} %copy-done.11), custom_call_target="tpu_custom_call" | custom-call | flops 1000000000 | bytes 1048576 | tf_op jit(solution)/shard_map/factor/pallas_call | solution.py:509
  19.2 0.0 copy-start.5
  19.2 0.0 copy-start.6
  19.2 0.0 copy-done
  19.2 0.0 copy-done.1
  19.3 0.0 copy-done.3
  19.3 0.0 copy-done.4
  19.3 0.6 copy-done.5
  19.9 0.0 copy-done.6
  19.9 0.0 copy-start.7
  19.9 0.0 copy-start.9
  19.9 0.8 pick.1
  20.7 11.1 %all-to-all-done.x_ref.cells_ref = f32[16,3,2,256]{3,2,1,0:T(2,128)S(1)} async-done(((f32[16,3,2,256]{3,2,1,0:T(2,128)}), f32[16,3,2,256]{3,2,1,0:T(2,128)S(1)}, u32[]{:S(2)}, u32[]{:S(2)}) %all-to-all-start) | async-done | bytes 98336 | tf_op jit(solution)/shard_map/all_to_all | solution.py:508
  31.8 0.0 copy-done.7
  31.8 0.0 copy-done.9
  31.8 0.3 forward.1
  32.2 13.6 %all_to_all.20.source_ref = f32[32,2,256]{2,1,0:T(2,128)S(1)} all-to-all(f32[32,2,256]{2,1,0:T(2,128)S(1)} %forward.1), channel_id=1, replica_groups=mesh['az'=8,'x'=4,'zh'=2,'y'=4,'c'=2] {'y','c','x'}, dimensions={0} | all-to-all | bytes 131072 | tf_op jit(solution)/shard_map/all_to_all | solution.py:524
  45.8 0.2 solve.1
  46.0 0.0 copy-start.10
  46.0 11.3 %all_to_all.21.x_ref = f32[32,4,256]{2,1,0:T(4,128)S(1)} all-to-all(f32[32,4,256]{2,1,0:T(4,128)S(1)} %solve.1), channel_id=1, replica_groups=mesh['az'=8,'x'=4,'zh'=2,'y'=4,'c'=2] {'y','c','x'}, dimensions={0} | all-to-all | bytes 262144 | tf_op jit(solution)/shard_map/all_to_all | solution.py:533
  57.3 0.0 copy-done.10
  57.3 1.8 %inverse.1 = f32[16,9,2,256]{3,2,1,0:T(2,128)} custom-call(f32[32,4,256]{2,1,0:T(4,128)S(1)} %all_to_all.21.x_ref, f32[128,256]{1,0:T(8,128)S(1)} %copy-done.9, bf16[1024,256]{1,0:T(8,128)(2,1)S(1)} %copy-done.7, f32[16,3,2,256]{3,2,1,0:T(2,128)S(1)} %all-to-all-done.x_ref.cells_ref, f32[16,16,128]{2,1,0:T(8,128)S(1)} %copy-done.10), custom_call_target="tpu_custom_call" | custom-call | flops 1000000000 | bytes 1048576 | tf_op jit(solution)/shard_map/inverse/pallas_call | solution.py:534
  59.0 0.0 copy-start.2
  59.0 0.0 copy-start.8
  59.1 3.7 %all-to-all-start.3 = ((f32[16,9,2,256]{3,2,1,0:T(2,128)}), f32[16,9,2,256]{3,2,1,0:T(2,128)S(1)}, u32[]{:S(2)}, u32[]{:S(2)}) async-start(f32[16,9,2,256]{3,2,1,0:T(2,128)} %inverse.1), calls=%async_computation.3 | async-start | bytes 589824 | tf_op jit(solution)/shard_map/all_to_all | solution.py:538
  62.8 10.4 %collective-permute-start = (f32[8,256]{1,0:T(8,128)S(1)}, f32[8,256]{1,0:T(8,128)S(1)}, u32[]{:S(2)}, u32[]{:S(2)}) collective-permute-start(f32[8,256]{1,0:T(8,128)S(1)} %get-tuple-element.42), channel_id=1, source_target_pairs={{0,448},{64,128},{128,64},{192,256},{256,192},{320,384},{384,320},... | collective-permute-start | bytes 24584 | tf_op jit(solution)/shard_map/ppermute | solution.py:539
  73.2 1.9 %collective-permute-start.1 = (f32[8,256]{1,0:T(8,128)S(1)}, f32[8,256]{1,0:T(8,128)S(1)}, u32[]{:S(2)}, u32[]{:S(2)}) collective-permute-start(f32[8,256]{1,0:T(8,128)S(1)} %get-tuple-element.43), channel_id=1, source_target_pairs={{0,64},{64,0},{128,192},{192,128},{256,320},{320,256},{384,448},{4... | collective-permute-start | bytes 24584 | tf_op jit(solution)/shard_map/ppermute | solution.py:540
  75.1 5.5 %collective-permute-done.far_ref = f32[8,256]{1,0:T(8,128)S(1)} collective-permute-done((f32[8,256]{1,0:T(8,128)S(1)}, f32[8,256]{1,0:T(8,128)S(1)}, u32[]{:S(2)}, u32[]{:S(2)}) %collective-permute-start) | collective-permute-done | bytes 8224 | tf_op jit(solution)/shard_map/ppermute | solution.py:539
  80.6 0.0 collective-permute-done.1.close_ref
  80.6 3.0 %all-to-all-done.3.modes_ref = f32[16,9,2,256]{3,2,1,0:T(2,128)S(1)} async-done(((f32[16,9,2,256]{3,2,1,0:T(2,128)}), f32[16,9,2,256]{3,2,1,0:T(2,128)S(1)}, u32[]{:S(2)}, u32[]{:S(2)}) %all-to-all-start.3) | async-done | bytes 294944 | tf_op jit(solution)/shard_map/all_to_all | solution.py:538
  83.6 0.0 copy-done.2
  83.6 0.0 copy-done.8
  83.6 2.1 %final.1 = (f32[64,1,256]{2,1,0:T(1,128)}, f32[6,4096]{1,0:T(8,128)}, f32[7,2,256]{2,1,0:T(2,128)}) custom-call(f32[16,9,2,256]{3,2,1,0:T(2,128)S(1)} %all-to-all-done.3.modes_ref, bf16[512,192]{1,0:T(8,128)(2,1)S(1)} %copy-done.8, f32[8,256]{1,0:T(8,128)S(1)} %collective-permute-done.far_ref, f32[8,256]{1,0:T(8,128)S(1)} %collective-permute-done.1.close_ref, ...), custom_call_target="tpu_custom_call" | custom-call | flops 1000000000 | bytes 1048576 | tf_op jit(solution)/shard_map/final/pallas_call | solution.py:541
Async XLA Ops:
  3.0 15.2 %copy-start.11 = (f32[64]{0:T(128)S(1)}, f32[64]{0:T(128)}, u32[]{:S(2)}) copy-start(f32[64]{0:T(128)} %constant.10.clone.eigen_ref) | copy-start | bytes 772
  3.0 28.8 %all-to-all-start = ((f32[16,3,2,256]{3,2,1,0:T(2,128)}), f32[16,3,2,256]{3,2,1,0:T(2,128)S(1)}, u32[]{:S(2)}, u32[]{:S(2)}) async-start(f32[16,3,2,256]{3,2,1,0:T(2,128)} %deposit.1), calls=%async_computation | async-start | bytes 196608 | tf_op jit(solution)/shard_map/all_to_all | solution.py:508
  18.3 1.0 %copy-start = (f32[3,4096]{1,0:T(4,128)S(1)}, f32[3,4096]{1,0:T(4,128)}, u32[]{:S(2)}) copy-start(f32[3,4096]{1,0:T(4,128)} %positions_ref.3) | copy-start | bytes 147460
  18.3 1.0 %copy-start.1 = (f32[3,4096]{1,0:T(4,128)S(1)}, f32[3,4096]{1,0:T(4,128)}, u32[]{:S(2)}) copy-start(f32[3,4096]{1,0:T(4,128)} %velocities_ref.3) | copy-start | bytes 147460
  18.3 1.0 %copy-start.3 = (s32[4096]{0:T(1024)S(1)}, s32[4096]{0:T(1024)}, u32[]{:S(2)}) copy-start(s32[4096]{0:T(1024)} %param.16) | copy-start | bytes 49156
  18.3 1.0 %copy-start.4 = (bf16[4096]{0:T(1024)(128)(2,1)S(1)}, bf16[4096]{0:T(1024)(128)(2,1)}, u32[]{:S(2)}) copy-start(bf16[4096]{0:T(1024)(128)(2,1)} %mass_ref.1) | copy-start | bytes 24580
  19.2 0.7 copy-start.5
  19.2 0.7 copy-start.6
  19.9 11.9 %copy-start.7 = (bf16[1024,256]{1,0:T(8,128)(2,1)S(1)}, bf16[1024,256]{1,0:T(8,128)(2,1)}, u32[]{:S(2)}) copy-start(bf16[1024,256]{1,0:T(8,128)(2,1)} %constant.12.clone.table_ref) | copy-start | bytes 1572868
  19.9 11.9 %copy-start.9 = (f32[128,256]{1,0:T(8,128)S(1)}, f32[128,256]{1,0:T(8,128)}, u32[]{:S(2)}) copy-start(f32[128,256]{1,0:T(8,128)} %constant.11.clone.twist_ref) | copy-start | bytes 393220
  46.0 11.3 %copy-start.10 = (f32[16,16,128]{2,1,0:T(8,128)S(1)}, f32[16,16,128]{2,1,0:T(8,128)}, u32[]{:S(2)}) copy-start(f32[16,16,128]{2,1,0:T(8,128)} %constant.13.clone.weight_ref) | copy-start | bytes 393220
  59.0 24.5 %copy-start.2 = (s32[4096]{0:T(1024)S(1)}, s32[4096]{0:T(1024)}, u32[]{:S(2)}) copy-start(s32[4096]{0:T(1024)} %param.15) | copy-start | bytes 49156
  59.0 24.5 %copy-start.8 = (bf16[512,192]{1,0:T(8,128)(2,1)S(1)}, bf16[512,192]{1,0:T(8,128)(2,1)}, u32[]{:S(2)}) copy-start(bf16[512,192]{1,0:T(8,128)(2,1)} %constant.14.clone.table_ref) | copy-start | bytes 589828
  59.1 24.5 %all-to-all-start.3 = ((f32[16,9,2,256]{3,2,1,0:T(2,128)}), f32[16,9,2,256]{3,2,1,0:T(2,128)S(1)}, u32[]{:S(2)}, u32[]{:S(2)}) async-start(f32[16,9,2,256]{3,2,1,0:T(2,128)} %inverse.1), calls=%async_computation.3 | async-start | bytes 589824 | tf_op jit(solution)/shard_map/all_to_all | solution.py:538
  62.8 17.9 %collective-permute-start = (f32[8,256]{1,0:T(8,128)S(1)}, f32[8,256]{1,0:T(8,128)S(1)}, u32[]{:S(2)}, u32[]{:S(2)}) collective-permute-start(f32[8,256]{1,0:T(8,128)S(1)} %get-tuple-element.42), channel_id=1, source_target_pairs={{0,448},{64,128},{128,64},{192,256},{256,192},{320,384},{384,320},... | collective-permute-start | bytes 24584 | tf_op jit(solution)/shard_map/ppermute | solution.py:539
  73.2 7.4 %collective-permute-start.1 = (f32[8,256]{1,0:T(8,128)S(1)}, f32[8,256]{1,0:T(8,128)S(1)}, u32[]{:S(2)}, u32[]{:S(2)}) collective-permute-start(f32[8,256]{1,0:T(8,128)S(1)} %get-tuple-element.43), channel_id=1, source_target_pairs={{0,64},{64,0},{128,192},{192,128},{256,320},{320,256},{384,448},{4... | collective-permute-start | bytes 24584 | tf_op jit(solution)/shard_map/ppermute | solution.py:540

commit v7 on v6

--- a/solution.py
+++ b/solution.py
@@ -21,6 +21,9 @@
 
 F32 = jnp.float32
 BF16 = jnp.bfloat16
+
+
+PLANE = ("y1", "x1", "c", "y0", "x0")
 
 
 def _split_np(table):
@@ -80,8 +83,11 @@
 
 
 def _row_of(radius):
-    x, zh, y, c = radius >> 4, (radius >> 3) & 1, (radius >> 1) & 3, radius & 1
-    return (((y * 2 + c) * 4 + x) * 2) + zh
+    bits = {name: (radius >> (5 - i)) & 1 for i, name in enumerate(("x1", "x0", "zh", "y1", "y0", "c"))}
+    row = 0
+    for name in PLANE + ("zh",):
+        row = row * 2 + bits[name]
+    return row
 
 
 def _split(value):
@@ -209,7 +215,9 @@
 
 def factor_kernel(eigen_ref, inverse_ref, carry_ref, factor_ref, joint_ref):
     group = lax.axis_index("zh") * 8 + lax.axis_index("az")
-    place = (lax.axis_index("y") * 2 + lax.axis_index("c")) * 4 + lax.axis_index("x")
+    place = 0
+    for name in PLANE:
+        place = place * 2 + lax.axis_index(name)
     level = group * 4 + lax.rem(place, 4)
     residue = lax.div(place, 4)
     eigen = eigen_ref[level]
@@ -416,7 +424,7 @@
 
 
 def final_kernel(
-    modes_ref, table_ref, far_ref, close_ref, positions_ref, velocities_ref, cells_ref, active_ref,
+    modes_ref, table_ref, close_ref, far_ref, positions_ref, velocities_ref, cells_ref, active_ref,
     grid_ref, state_ref, arrive_ref,
 ):
     pieces = [modes_ref[group, part] for group in range(16) for part in range(6)]
@@ -481,7 +489,7 @@
 
 def per_device(positions, velocities, masses, cells, active, send_lists, send_counts):
     shape = functools.partial(jax.ShapeDtypeStruct, dtype=F32)
-    z_axes, plane_axes = ("zh", "az"), ("y", "c", "x")
+    z_axes, plane_axes = ("zh", "az"), PLANE
     exchange = functools.partial(lax.all_to_all, split_axis=0, concat_axis=0, tiled=True)
     table = _split_np(_trig())
     twist = _twist()
@@ -536,21 +544,21 @@
     )
     angles, wrap, near = lax.optimization_barrier((angles, wrap, near))
     modes = exchange(angles, z_axes)
+    close = lax.ppermute(near, "az", [(i, i ^ 1) for i in range(8)])
     far = lax.ppermute(wrap, "az", [(i, (i + 1) % 8 if i % 2 else (i + 7) % 8) for i in range(8)])
-    close = lax.ppermute(near, "az", [(i, i ^ 1) for i in range(8)])
     potential, state, arrivals = _call(
         final_kernel,
         (shape((64, 1, SECTOR)), shape((6, STARS)), shape((7, 2, CAP))),
         "final",
         10**9,
         count=8,
-    )(modes, _split_np(_field_table()), far, close, positions, velocities, cell, live)
+    )(modes, _split_np(_field_table()), close, far, positions, velocities, cell, live)
     return potential, state, arrivals.transpose(1, 0, 2)
 
 
 def solution(mesh):
-    fine = Mesh(mesh.devices.reshape(8, 4, 2, 4, 2), ("az", "x", "zh", "y", "c"))
-    rz = ("x", "zh", "y", "c")
+    fine = Mesh(mesh.devices.reshape(8, 2, 2, 2, 2, 2, 2), ("az", "x1", "x0", "zh", "y1", "y0", "c"))
+    rz = ("x1", "x0", "zh", "y1", "y0", "c")
     every = ("az",) + rz
     return jax.shard_map(
         per_device,

time: 86.2 us -> 85.8 us (level)
  the two profiles are of different devices: /device:TPU:2 before, /device:TPU:34 now
where the time goes in v7:
time: 85.8 us; the launch traced here: 85.3 us
  starting transfers between devices  26.2 us (31%)
  blocking collectives  25.3 us (29%)
  waiting for transfers between devices  23.8 us (28%)
  Pallas kernels  8.49 us (10%)
    all_to_all x1, starting transfers between devices, per_device(): sectors = exchange(layered, z_axes)  15.2 us
    all_to_all x1, blocking collectives, per_device(): columns = exchange(spectrum, plane_axes)  13.9 us
    all_to_all x1, blocking collectives, per_device(): waves = exchange(solved, plane_axes)  11.4 us
    all_to_all x1, waiting for transfers between devices, per_device(): sectors = exchange(layered, z_axes)  10.5 us
    all_to_all x1, waiting for transfers between devices, per_device(): modes = exchange(angles, z_axes)  7.74 us
    ppermute x1, waiting for transfers between devices, per_device(): close = lax.ppermute(near, 'az', [(i, i ^ 1) for i in range(8)])  4.8 us
    ppermute x1, starting transfers between devices, per_device(): lax.ppermute(wrap, 'az', [(i, (i + 1) % 8 if i % 2 else (i + 7) % 8) for...  4.72 us
    all_to_all x1, starting transfers between devices, per_device(): modes = exchange(angles, z_axes)  4.28 us
  transfers between devices with their start and end apart: 4, of which 4 were waited for; matrix products, arithmetic and copies ran while one was open for 0% of the time, Pallas kernels for 2%

profile of v7, /device:TPU:34, one launch (start us, length us, event | category | flops | bytes accessed | tf_op | source)
XLA Modules:
  0.0 85.3 jit_solution(901580413821802608)
XLA Ops:
  0.6 2.4 %deposit.1 = f32[16,3,2,256]{3,2,1,0:T(2,128)} custom-call(s32[1,4096]{1,0:T(1,128)} %bitcast.5, bf16[4096]{0:T(1024)(128)(2,1)} %mass_ref.1, s32[2,256]{1,0:T(2,128)} %lists_ref, s32[32,128]{1,0:T(8,128)} %bitcast.6), custom_call_target="tpu_custom_call" | custom-call | flops 1000000000 | bytes 1048576 | tf_op jit(solution)/shard_map/deposit/pallas_call | solution.py:499
  3.0 0.0 copy-start.11
  3.0 15.2 %all-to-all-start = ((f32[16,3,2,256]{3,2,1,0:T(2,128)}), f32[16,3,2,256]{3,2,1,0:T(2,128)S(1)}, u32[]{:S(2)}, u32[]{:S(2)}) async-start(f32[16,3,2,256]{3,2,1,0:T(2,128)} %deposit.1), calls=%async_computation | async-start | bytes 196608 | tf_op jit(solution)/shard_map/all_to_all | solution.py:516
  18.3 0.0 copy-done.11
  18.3 0.0 copy-start
  18.3 0.0 copy-start.1
  18.3 0.0 copy-start.3
  18.3 0.0 copy-start.4
  18.3 0.9 %factor.1 = (f32[64,256]{1,0:T(8,128)S(1)}, f32[64,256]{1,0:T(8,128)S(1)}, f32[64,256]{1,0:T(8,128)S(1)}, f32[8,256]{1,0:T(8,128)S(1)}) custom-call(f32[64]{0:T(128)S(1)} %copy-done.11), custom_call_target="tpu_custom_call" | custom-call | flops 1000000000 | bytes 1048576 | tf_op jit(solution)/shard_map/factor/pallas_call | solution.py:517
  19.2 0.0 copy-start.5
  19.2 0.0 copy-start.6
  19.2 0.0 copy-done
  19.3 0.0 copy-done.1
  19.3 0.0 copy-done.3
  19.3 0.0 copy-done.4
  19.3 0.6 copy-done.5
  19.9 0.0 copy-done.6
  19.9 0.0 copy-start.7
  19.9 0.0 copy-start.9
  19.9 0.8 pick.1
  20.7 10.5 %all-to-all-done.x_ref.cells_ref = f32[16,3,2,256]{3,2,1,0:T(2,128)S(1)} async-done(((f32[16,3,2,256]{3,2,1,0:T(2,128)}), f32[16,3,2,256]{3,2,1,0:T(2,128)S(1)}, u32[]{:S(2)}, u32[]{:S(2)}) %all-to-all-start) | async-done | bytes 98336 | tf_op jit(solution)/shard_map/all_to_all | solution.py:516
  31.3 0.0 copy-done.7
  31.3 0.0 copy-done.9
  31.3 0.3 forward.1
  31.6 13.9 %all_to_all.20.source_ref = f32[32,2,256]{2,1,0:T(2,128)S(1)} all-to-all(f32[32,2,256]{2,1,0:T(2,128)S(1)} %forward.1), channel_id=1, replica_groups=mesh['az'=8,'x1'=2,'x0'=2,'zh'=2,'y1'=2,'y0'=2,'c'=2] {'y1','x1','c','y0..., dimensions={0} | all-to-all | bytes 131072 | tf_op jit(solution)/shard_map/all_to_all | solution.py:532
  45.5 0.2 solve.1
  45.7 0.0 copy-start.10
  45.7 11.4 %all_to_all.21.x_ref = f32[32,4,256]{2,1,0:T(4,128)S(1)} all-to-all(f32[32,4,256]{2,1,0:T(4,128)S(1)} %solve.1), channel_id=1, replica_groups=mesh['az'=8,'x1'=2,'x0'=2,'zh'=2,'y1'=2,'y0'=2,'c'=2] {'y1','x1','c','y0..., dimensions={0} | all-to-all | bytes 262144 | tf_op jit(solution)/shard_map/all_to_all | solution.py:541
  57.1 0.0 copy-done.10
  57.1 1.8 %inverse.1 = f32[16,9,2,256]{3,2,1,0:T(2,128)} custom-call(f32[32,4,256]{2,1,0:T(4,128)S(1)} %all_to_all.21.x_ref, f32[128,256]{1,0:T(8,128)S(1)} %copy-done.9, bf16[1024,256]{1,0:T(8,128)(2,1)S(1)} %copy-done.7, f32[16,3,2,256]{3,2,1,0:T(2,128)S(1)} %all-to-all-done.x_ref.cells_ref, f32[16,16,128]{2,1,0:T(8,128)S(1)} %copy-done.10), custom_call_target="tpu_custom_call" | custom-call | flops 1000000000 | bytes 1048576 | tf_op jit(solution)/shard_map/inverse/pallas_call | solution.py:542
  58.8 0.0 copy-start.2
  58.9 0.0 copy-start.8
  58.9 4.3 %all-to-all-start.3 = ((f32[16,9,2,256]{3,2,1,0:T(2,128)}), f32[16,9,2,256]{3,2,1,0:T(2,128)S(1)}, u32[]{:S(2)}, u32[]{:S(2)}) async-start(f32[16,9,2,256]{3,2,1,0:T(2,128)} %inverse.1), calls=%async_computation.3 | async-start | bytes 589824 | tf_op jit(solution)/shard_map/all_to_all | solution.py:546
  63.1 2.0 %collective-permute-start = (f32[8,256]{1,0:T(8,128)S(1)}, f32[8,256]{1,0:T(8,128)S(1)}, u32[]{:S(2)}, u32[]{:S(2)}) collective-permute-start(f32[8,256]{1,0:T(8,128)S(1)} %get-tuple-element.42), channel_id=1, source_target_pairs={{0,64},{64,0},{128,192},{192,128},{256,320},{320,256},{384,448},{4... | collective-permute-start | bytes 24584 | tf_op jit(solution)/shard_map/ppermute | solution.py:547
  65.2 4.7 %collective-permute-start.1 = (f32[8,256]{1,0:T(8,128)S(1)}, f32[8,256]{1,0:T(8,128)S(1)}, u32[]{:S(2)}, u32[]{:S(2)}) collective-permute-start(f32[8,256]{1,0:T(8,128)S(1)} %get-tuple-element.43), channel_id=1, source_target_pairs={{0,448},{64,128},{128,64},{192,256},{256,192},{320,384},{384,320},... | collective-permute-start | bytes 24584 | tf_op jit(solution)/shard_map/ppermute | solution.py:548
  69.9 4.8 %collective-permute-done.close_ref = f32[8,256]{1,0:T(8,128)S(1)} collective-permute-done((f32[8,256]{1,0:T(8,128)S(1)}, f32[8,256]{1,0:T(8,128)S(1)}, u32[]{:S(2)}, u32[]{:S(2)}) %collective-permute-start) | collective-permute-done | bytes 8224 | tf_op jit(solution)/shard_map/ppermute | solution.py:547
  74.7 0.7 collective-permute-done.1.far_ref
  75.4 7.7 %all-to-all-done.3.modes_ref = f32[16,9,2,256]{3,2,1,0:T(2,128)S(1)} async-done(((f32[16,9,2,256]{3,2,1,0:T(2,128)}), f32[16,9,2,256]{3,2,1,0:T(2,128)S(1)}, u32[]{:S(2)}, u32[]{:S(2)}) %all-to-all-start.3) | async-done | bytes 294944 | tf_op jit(solution)/shard_map/all_to_all | solution.py:546
  83.2 0.0 copy-done.2
  83.2 0.0 copy-done.8
  83.2 2.1 %final.1 = (f32[64,1,256]{2,1,0:T(1,128)}, f32[6,4096]{1,0:T(8,128)}, f32[7,2,256]{2,1,0:T(2,128)}) custom-call(f32[16,9,2,256]{3,2,1,0:T(2,128)S(1)} %all-to-all-done.3.modes_ref, bf16[512,192]{1,0:T(8,128)(2,1)S(1)} %copy-done.8, f32[8,256]{1,0:T(8,128)S(1)} %collective-permute-done.close_ref, f32[8,256]{1,0:T(8,128)S(1)} %collective-permute-done.1.far_ref, ...), custom_call_target="tpu_custom_call" | custom-call | flops 1000000000 | bytes 1048576 | tf_op jit(solution)/shard_map/final/pallas_call | solution.py:549
Async XLA Ops:
  3.0 15.2 %copy-start.11 = (f32[64]{0:T(128)S(1)}, f32[64]{0:T(128)}, u32[]{:S(2)}) copy-start(f32[64]{0:T(128)} %constant.10.clone.eigen_ref) | copy-start | bytes 772
  3.0 28.2 %all-to-all-start = ((f32[16,3,2,256]{3,2,1,0:T(2,128)}), f32[16,3,2,256]{3,2,1,0:T(2,128)S(1)}, u32[]{:S(2)}, u32[]{:S(2)}) async-start(f32[16,3,2,256]{3,2,1,0:T(2,128)} %deposit.1), calls=%async_computation | async-start | bytes 196608 | tf_op jit(solution)/shard_map/all_to_all | solution.py:516
  18.3 1.0 %copy-start = (f32[3,4096]{1,0:T(4,128)S(1)}, f32[3,4096]{1,0:T(4,128)}, u32[]{:S(2)}) copy-start(f32[3,4096]{1,0:T(4,128)} %positions_ref.3) | copy-start | bytes 147460
  18.3 1.0 %copy-start.1 = (f32[3,4096]{1,0:T(4,128)S(1)}, f32[3,4096]{1,0:T(4,128)}, u32[]{:S(2)}) copy-start(f32[3,4096]{1,0:T(4,128)} %velocities_ref.3) | copy-start | bytes 147460
  18.3 1.0 %copy-start.3 = (s32[4096]{0:T(1024)S(1)}, s32[4096]{0:T(1024)}, u32[]{:S(2)}) copy-start(s32[4096]{0:T(1024)} %param.16) | copy-start | bytes 49156
  18.3 1.0 %copy-start.4 = (bf16[4096]{0:T(1024)(128)(2,1)S(1)}, bf16[4096]{0:T(1024)(128)(2,1)}, u32[]{:S(2)}) copy-start(bf16[4096]{0:T(1024)(128)(2,1)} %mass_ref.1) | copy-start | bytes 24580
  19.2 0.7 copy-start.5
  19.2 0.7 copy-start.6
  19.9 11.4 %copy-start.7 = (bf16[1024,256]{1,0:T(8,128)(2,1)S(1)}, bf16[1024,256]{1,0:T(8,128)(2,1)}, u32[]{:S(2)}) copy-start(bf16[1024,256]{1,0:T(8,128)(2,1)} %constant.12.clone.table_ref) | copy-start | bytes 1572868
  19.9 11.4 %copy-start.9 = (f32[128,256]{1,0:T(8,128)S(1)}, f32[128,256]{1,0:T(8,128)}, u32[]{:S(2)}) copy-start(f32[128,256]{1,0:T(8,128)} %constant.11.clone.twist_ref) | copy-start | bytes 393220
  45.7 11.4 %copy-start.10 = (f32[16,16,128]{2,1,0:T(8,128)S(1)}, f32[16,16,128]{2,1,0:T(8,128)}, u32[]{:S(2)}) copy-start(f32[16,16,128]{2,1,0:T(8,128)} %constant.13.clone.weight_ref) | copy-start | bytes 393220
  58.8 24.3 %copy-start.2 = (s32[4096]{0:T(1024)S(1)}, s32[4096]{0:T(1024)}, u32[]{:S(2)}) copy-start(s32[4096]{0:T(1024)} %param.15) | copy-start | bytes 49156
  58.9 24.3 %copy-start.8 = (bf16[512,192]{1,0:T(8,128)(2,1)S(1)}, bf16[512,192]{1,0:T(8,128)(2,1)}, u32[]{:S(2)}) copy-start(bf16[512,192]{1,0:T(8,128)(2,1)} %constant.14.clone.table_ref) | copy-start | bytes 589828
  58.9 24.3 %all-to-all-start.3 = ((f32[16,9,2,256]{3,2,1,0:T(2,128)}), f32[16,9,2,256]{3,2,1,0:T(2,128)S(1)}, u32[]{:S(2)}, u32[]{:S(2)}) async-start(f32[16,9,2,256]{3,2,1,0:T(2,128)} %inverse.1), calls=%async_computation.3 | async-start | bytes 589824 | tf_op jit(solution)/shard_map/all_to_all | solution.py:546
  63.1 11.5 %collective-permute-start = (f32[8,256]{1,0:T(8,128)S(1)}, f32[8,256]{1,0:T(8,128)S(1)}, u32[]{:S(2)}, u32[]{:S(2)}) collective-permute-start(f32[8,256]{1,0:T(8,128)S(1)} %get-tuple-element.42), channel_id=1, source_target_pairs={{0,64},{64,0},{128,192},{192,128},{256,320},{320,256},{384,448},{4... | collective-permute-start | bytes 24584 | tf_op jit(solution)/shard_map/ppermute | solution.py:547
  65.2 10.3 %collective-permute-start.1 = (f32[8,256]{1,0:T(8,128)S(1)}, f32[8,256]{1,0:T(8,128)S(1)}, u32[]{:S(2)}, u32[]{:S(2)}) collective-permute-start(f32[8,256]{1,0:T(8,128)S(1)} %get-tuple-element.43), channel_id=1, source_target_pairs={{0,448},{64,128},{128,64},{192,256},{256,192},{320,384},{384,320},... | collective-permute-start | bytes 24584 | tf_op jit(solution)/shard_map/ppermute | solution.py:548

commit v8 on v7

--- a/solution.py
+++ b/solution.py
@@ -23,7 +23,24 @@
 BF16 = jnp.bfloat16
 
 
+AZ = ("a2", "a1", "a0")
 PLANE = ("y1", "x1", "c", "y0", "x0")
+ORDER = ("zh", "a2", "a0", "a1")
+
+
+def _group(a, zh):
+    bits = {"zh": zh, "a2": a >> 2, "a1": (a >> 1) & 1, "a0": a & 1}
+    place = 0
+    for name in ORDER:
+        place = place * 2 + bits[name]
+    return place
+
+
+def _own_group():
+    place = 0
+    for name in ORDER:
+        place = place * 2 + lax.axis_index(name)
+    return place
 
 
 def _split_np(table):
@@ -191,7 +208,7 @@
 def forward_kernel(x_ref, twist_ref, table_ref, out_ref):
     tiles = []
     for a in range(8):
-        parts = [x_ref[zh * 8 + a, half] for zh in range(2) for half in range(2)]
+        parts = [x_ref[_group(a, zh), half] for zh in range(2) for half in range(2)]
         tiles.append(jnp.concatenate(parts, axis=0))
     rows = []
     for n2 in range(8):
@@ -214,7 +231,7 @@
 
 
 def factor_kernel(eigen_ref, inverse_ref, carry_ref, factor_ref, joint_ref):
-    group = lax.axis_index("zh") * 8 + lax.axis_index("az")
+    group = _own_group()
     place = 0
     for name in PLANE:
         place = place * 2 + lax.axis_index(name)
@@ -296,7 +313,7 @@
 
 
 def inverse_kernel(x_ref, twist_ref, table_ref, cells_ref, weight_ref, out_ref):
-    group = lax.axis_index("zh") * 8 + lax.axis_index("az")
+    group = _own_group()
     fields = [[], [], []]
     for n2 in range(8):
         pair = []
@@ -332,12 +349,12 @@
             for zh in range(2):
                 for half in range(2):
                     row = zh * 4 + half * 2
-                    out_ref[zh * 8 + a, field * 2 + half] = total[row : row + 2, :]
+                    out_ref[_group(a, zh), field * 2 + half] = total[row : row + 2, :]
             tiles.append(total)
         accel = [[], [], []]
         for quarter in range(4):
             at = 128 * (quarter % 2)
-            cell = [cells_ref[zh * 8 + a, 2, quarter // 2 : quarter // 2 + 1, at : at + 128] for zh in range(2)]
+            cell = [cells_ref[_group(a, zh), 2, quarter // 2 : quarter // 2 + 1, at : at + 128] for zh in range(2)]
             cell = jnp.concatenate([jnp.broadcast_to(part, (4, 128)) for part in cell], axis=0).astype(jnp.int32)
             layer = lax.shift_right_logical(cell, 8)
             lane = cell & 127
@@ -357,7 +374,7 @@
                 row = slot * 3 + field
                 for zh in range(2):
                     spot = 4 * zh + 3
-                    out_ref[zh * 8 + dest, 6 + row // 2, row % 2 : row % 2 + 1, :] = pair[spot : spot + 1, :]
+                    out_ref[_group(dest, zh), 6 + row // 2, row % 2 : row % 2 + 1, :] = pair[spot : spot + 1, :]
 
 
 def pick_kernel(positions_ref, velocities_ref, mass_ref, active_ref, lists_ref, counts_ref, wrap_ref, near_ref):
@@ -391,7 +408,7 @@
     )
     down = rows[:, :CAP]
     up = rows[:, CAP:]
-    odd = lax.rem(lax.axis_index("az"), 2) == 1
+    odd = lax.axis_index("a0") == 1
     wrap_ref[...] = jnp.where(odd, up, down)
     near_ref[...] = jnp.where(odd, down, up)
 
@@ -441,7 +458,7 @@
         for group in range(1, 16):
             total = total + modes_ref[group, part]
         sums += [total[0:1], total[1:2]]
-    odd = lax.rem(lax.axis_index("az"), 2) == 1
+    odd = lax.axis_index("a0") == 1
     far = far_ref[...]
     close = close_ref[...]
     for slot in range(2):
@@ -489,7 +506,7 @@
 
 def per_device(positions, velocities, masses, cells, active, send_lists, send_counts):
     shape = functools.partial(jax.ShapeDtypeStruct, dtype=F32)
-    z_axes, plane_axes = ("zh", "az"), PLANE
+    z_axes, plane_axes = ORDER, PLANE
     exchange = functools.partial(lax.all_to_all, split_axis=0, concat_axis=0, tiled=True)
     table = _split_np(_trig())
     twist = _twist()
@@ -544,8 +561,8 @@
     )
     angles, wrap, near = lax.optimization_barrier((angles, wrap, near))
     modes = exchange(angles, z_axes)
-    close = lax.ppermute(near, "az", [(i, i ^ 1) for i in range(8)])
-    far = lax.ppermute(wrap, "az", [(i, (i + 1) % 8 if i % 2 else (i + 7) % 8) for i in range(8)])
+    close = lax.ppermute(near, AZ, [(i, i ^ 1) for i in range(8)])
+    far = lax.ppermute(wrap, AZ, [(i, (i + 1) % 8 if i % 2 else (i + 7) % 8) for i in range(8)])
     potential, state, arrivals = _call(
         final_kernel,
         (shape((64, 1, SECTOR)), shape((6, STARS)), shape((7, 2, CAP))),
@@ -557,9 +574,9 @@
 
 
 def solution(mesh):
-    fine = Mesh(mesh.devices.reshape(8, 2, 2, 2, 2, 2, 2), ("az", "x1", "x0", "zh", "y1", "y0", "c"))
+    fine = Mesh(mesh.devices.reshape(2, 2, 2, 2, 2, 2, 2, 2, 2), ("a2", "a1", "a0", "x1", "x0", "zh", "y1", "y0", "c"))
     rz = ("x1", "x0", "zh", "y1", "y0", "c")
-    every = ("az",) + rz
+    every = AZ + rz
     return jax.shard_map(
         per_device,
         mesh=fine,
@@ -572,6 +589,6 @@
             P(None, every),
             P(None, every),
         ),
-        out_specs=(P(None, rz, "az"), P(None, every), P(None, None, every)),
+        out_specs=(P(None, rz, AZ), P(None, every), P(None, None, every)),
         check_vma=False,
     )

time: 85.8 us -> 85.5 us (level)
  the two profiles are of different devices: /device:TPU:34 before, /device:TPU:32 now
where the time goes in v8:
time: 85.5 us; the launch traced here: 85 us
  starting transfers between devices  27.1 us (32%)
  blocking collectives  26.2 us (31%)
  waiting for transfers between devices  21.8 us (25%)
  Pallas kernels  8.49 us (10%)
    all_to_all x1, starting transfers between devices, per_device(): sectors = exchange(layered, z_axes)  15.2 us
    all_to_all x1, blocking collectives, per_device(): columns = exchange(spectrum, plane_axes)  14.8 us
    all_to_all x1, blocking collectives, per_device(): waves = exchange(solved, plane_axes)  11.4 us
    all_to_all x1, waiting for transfers between devices, per_device(): sectors = exchange(layered, z_axes)  9.68 us
    all_to_all x1, waiting for transfers between devices, per_device(): modes = exchange(angles, z_axes)  6.41 us
    all_to_all x1, starting transfers between devices, per_device(): modes = exchange(angles, z_axes)  5.11 us
    ppermute x1, waiting for transfers between devices, per_device(): close = lax.ppermute(near, AZ, [(i, i ^ 1) for i in range(8)])  4.77 us
    ppermute x1, starting transfers between devices, per_device(): lax.ppermute(wrap, AZ, [(i, (i + 1) % 8 if i % 2 else (i + 7) % 8) for i...  4.65 us
  transfers between devices with their start and end apart: 4, of which 4 were waited for; matrix products, arithmetic and copies ran while one was open for 0% of the time, Pallas kernels for 2%

profile of v8, /device:TPU:32, one launch (start us, length us, event | category | flops | bytes accessed | tf_op | source)
XLA Modules:
  0.0 85.0 jit_solution(5856374357944727871)
XLA Ops:
  0.6 2.4 %deposit.1 = f32[16,3,2,256]{3,2,1,0:T(2,128)} custom-call(s32[1,4096]{1,0:T(1,128)} %bitcast.5, bf16[4096]{0:T(1024)(128)(2,1)} %mass_ref.1, s32[2,256]{1,0:T(2,128)} %lists_ref, s32[32,128]{1,0:T(8,128)} %bitcast.6), custom_call_target="tpu_custom_call" | custom-call | flops 1000000000 | bytes 1048576 | tf_op jit(solution)/shard_map/deposit/pallas_call | solution.py:516
  3.0 0.0 copy-start.11
  3.0 15.2 %all-to-all-start = ((f32[16,3,2,256]{3,2,1,0:T(2,128)}), f32[16,3,2,256]{3,2,1,0:T(2,128)S(1)}, u32[]{:S(2)}, u32[]{:S(2)}) async-start(f32[16,3,2,256]{3,2,1,0:T(2,128)} %deposit.1), calls=%async_computation | async-start | bytes 196608 | tf_op jit(solution)/shard_map/all_to_all | solution.py:533
  18.3 0.0 copy-done.11
  18.3 0.0 copy-start
  18.3 0.0 copy-start.1
  18.3 0.0 copy-start.3
  18.3 0.0 copy-start.4
  18.3 0.9 %factor.1 = (f32[64,256]{1,0:T(8,128)S(1)}, f32[64,256]{1,0:T(8,128)S(1)}, f32[64,256]{1,0:T(8,128)S(1)}, f32[8,256]{1,0:T(8,128)S(1)}) custom-call(f32[64]{0:T(128)S(1)} %copy-done.11), custom_call_target="tpu_custom_call" | custom-call | flops 1000000000 | bytes 1048576 | tf_op jit(solution)/shard_map/factor/pallas_call | solution.py:534
  19.2 0.0 copy-start.5
  19.2 0.0 copy-start.6
  19.2 0.0 copy-done
  19.3 0.0 copy-done.1
  19.3 0.0 copy-done.3
  19.3 0.0 copy-done.4
  19.3 0.6 copy-done.5
  19.9 0.0 copy-done.6
  19.9 0.0 copy-start.7
  19.9 0.0 copy-start.9
  19.9 0.8 pick.1
  20.7 9.7 %all-to-all-done.x_ref.cells_ref = f32[16,3,2,256]{3,2,1,0:T(2,128)S(1)} async-done(((f32[16,3,2,256]{3,2,1,0:T(2,128)}), f32[16,3,2,256]{3,2,1,0:T(2,128)S(1)}, u32[]{:S(2)}, u32[]{:S(2)}) %all-to-all-start) | async-done | bytes 98336 | tf_op jit(solution)/shard_map/all_to_all | solution.py:533
  30.4 0.0 copy-done.7
  30.4 0.0 copy-done.9
  30.4 0.3 forward.1
  30.8 14.8 %all_to_all.20.source_ref = f32[32,2,256]{2,1,0:T(2,128)S(1)} all-to-all(f32[32,2,256]{2,1,0:T(2,128)S(1)} %forward.1), channel_id=1, replica_groups=mesh['a2'=2,'a1'=2,'a0'=2,'x1'=2,'x0'=2,'zh'=2,'y1'=2,'y0'=2,'c'=2] {'y1..., dimensions={0} | all-to-all | bytes 131072 | tf_op jit(solution)/shard_map/all_to_all | solution.py:549
  45.6 0.2 solve.1
  45.8 0.0 copy-start.10
  45.8 11.4 %all_to_all.21.x_ref = f32[32,4,256]{2,1,0:T(4,128)S(1)} all-to-all(f32[32,4,256]{2,1,0:T(4,128)S(1)} %solve.1), channel_id=1, replica_groups=mesh['a2'=2,'a1'=2,'a0'=2,'x1'=2,'x0'=2,'zh'=2,'y1'=2,'y0'=2,'c'=2] {'y1..., dimensions={0} | all-to-all | bytes 262144 | tf_op jit(solution)/shard_map/all_to_all | solution.py:558
  57.1 0.0 copy-done.10
  57.1 1.8 %inverse.1 = f32[16,9,2,256]{3,2,1,0:T(2,128)} custom-call(f32[32,4,256]{2,1,0:T(4,128)S(1)} %all_to_all.21.x_ref, f32[128,256]{1,0:T(8,128)S(1)} %copy-done.9, bf16[1024,256]{1,0:T(8,128)(2,1)S(1)} %copy-done.7, f32[16,3,2,256]{3,2,1,0:T(2,128)S(1)} %all-to-all-done.x_ref.cells_ref, f32[16,16,128]{2,1,0:T(8,128)S(1)} %copy-done.10), custom_call_target="tpu_custom_call" | custom-call | flops 1000000000 | bytes 1048576 | tf_op jit(solution)/shard_map/inverse/pallas_call | solution.py:559
  58.9 0.0 copy-start.2
  58.9 0.0 copy-start.8
  58.9 5.1 %all-to-all-start.3 = ((f32[16,9,2,256]{3,2,1,0:T(2,128)}), f32[16,9,2,256]{3,2,1,0:T(2,128)S(1)}, u32[]{:S(2)}, u32[]{:S(2)}) async-start(f32[16,9,2,256]{3,2,1,0:T(2,128)} %inverse.1), calls=%async_computation.3 | async-start | bytes 589824 | tf_op jit(solution)/shard_map/all_to_all | solution.py:563
  64.1 2.1 %collective-permute-start = (f32[8,256]{1,0:T(8,128)S(1)}, f32[8,256]{1,0:T(8,128)S(1)}, u32[]{:S(2)}, u32[]{:S(2)}) collective-permute-start(f32[8,256]{1,0:T(8,128)S(1)} %get-tuple-element.42), channel_id=1, source_target_pairs={{0,64},{64,0},{128,192},{192,128},{256,320},{320,256},{384,448},{4... | collective-permute-start | bytes 24584 | tf_op jit(solution)/shard_map/ppermute | solution.py:564
  66.1 4.7 %collective-permute-start.1 = (f32[8,256]{1,0:T(8,128)S(1)}, f32[8,256]{1,0:T(8,128)S(1)}, u32[]{:S(2)}, u32[]{:S(2)}) collective-permute-start(f32[8,256]{1,0:T(8,128)S(1)} %get-tuple-element.43), channel_id=1, source_target_pairs={{0,448},{64,128},{128,64},{192,256},{256,192},{320,384},{384,320},... | collective-permute-start | bytes 24584 | tf_op jit(solution)/shard_map/ppermute | solution.py:565
  70.8 4.8 %collective-permute-done.close_ref = f32[8,256]{1,0:T(8,128)S(1)} collective-permute-done((f32[8,256]{1,0:T(8,128)S(1)}, f32[8,256]{1,0:T(8,128)S(1)}, u32[]{:S(2)}, u32[]{:S(2)}) %collective-permute-start) | collective-permute-done | bytes 8224 | tf_op jit(solution)/shard_map/ppermute | solution.py:564
  75.6 0.9 %collective-permute-done.1.far_ref = f32[8,256]{1,0:T(8,128)S(1)} collective-permute-done((f32[8,256]{1,0:T(8,128)S(1)}, f32[8,256]{1,0:T(8,128)S(1)}, u32[]{:S(2)}, u32[]{:S(2)}) %collective-permute-start.1) | collective-permute-done | bytes 8224 | tf_op jit(solution)/shard_map/ppermute | solution.py:565
  76.5 6.4 %all-to-all-done.3.modes_ref = f32[16,9,2,256]{3,2,1,0:T(2,128)S(1)} async-done(((f32[16,9,2,256]{3,2,1,0:T(2,128)}), f32[16,9,2,256]{3,2,1,0:T(2,128)S(1)}, u32[]{:S(2)}, u32[]{:S(2)}) %all-to-all-start.3) | async-done | bytes 294944 | tf_op jit(solution)/shard_map/all_to_all | solution.py:563
  82.9 0.0 copy-done.2
  82.9 0.0 copy-done.8
  82.9 2.1 %final.1 = (f32[64,1,256]{2,1,0:T(1,128)}, f32[6,4096]{1,0:T(8,128)}, f32[7,2,256]{2,1,0:T(2,128)}) custom-call(f32[16,9,2,256]{3,2,1,0:T(2,128)S(1)} %all-to-all-done.3.modes_ref, bf16[512,192]{1,0:T(8,128)(2,1)S(1)} %copy-done.8, f32[8,256]{1,0:T(8,128)S(1)} %collective-permute-done.close_ref, f32[8,256]{1,0:T(8,128)S(1)} %collective-permute-done.1.far_ref, ...), custom_call_target="tpu_custom_call" | custom-call | flops 1000000000 | bytes 1048576 | tf_op jit(solution)/shard_map/final/pallas_call | solution.py:566
Async XLA Ops:
  3.0 15.2 %copy-start.11 = (f32[64]{0:T(128)S(1)}, f32[64]{0:T(128)}, u32[]{:S(2)}) copy-start(f32[64]{0:T(128)} %constant.10.clone.eigen_ref) | copy-start | bytes 772
  3.0 27.4 %all-to-all-start = ((f32[16,3,2,256]{3,2,1,0:T(2,128)}), f32[16,3,2,256]{3,2,1,0:T(2,128)S(1)}, u32[]{:S(2)}, u32[]{:S(2)}) async-start(f32[16,3,2,256]{3,2,1,0:T(2,128)} %deposit.1), calls=%async_computation | async-start | bytes 196608 | tf_op jit(solution)/shard_map/all_to_all | solution.py:533
  18.3 1.0 %copy-start = (f32[3,4096]{1,0:T(4,128)S(1)}, f32[3,4096]{1,0:T(4,128)}, u32[]{:S(2)}) copy-start(f32[3,4096]{1,0:T(4,128)} %positions_ref.3) | copy-start | bytes 147460
  18.3 1.0 %copy-start.1 = (f32[3,4096]{1,0:T(4,128)S(1)}, f32[3,4096]{1,0:T(4,128)}, u32[]{:S(2)}) copy-start(f32[3,4096]{1,0:T(4,128)} %velocities_ref.3) | copy-start | bytes 147460
  18.3 1.0 %copy-start.3 = (s32[4096]{0:T(1024)S(1)}, s32[4096]{0:T(1024)}, u32[]{:S(2)}) copy-start(s32[4096]{0:T(1024)} %param.16) | copy-start | bytes 49156
  18.3 1.0 %copy-start.4 = (bf16[4096]{0:T(1024)(128)(2,1)S(1)}, bf16[4096]{0:T(1024)(128)(2,1)}, u32[]{:S(2)}) copy-start(bf16[4096]{0:T(1024)(128)(2,1)} %mass_ref.1) | copy-start | bytes 24580
  19.2 0.7 copy-start.5
  19.2 0.7 copy-start.6
  19.9 10.5 %copy-start.7 = (bf16[1024,256]{1,0:T(8,128)(2,1)S(1)}, bf16[1024,256]{1,0:T(8,128)(2,1)}, u32[]{:S(2)}) copy-start(bf16[1024,256]{1,0:T(8,128)(2,1)} %constant.12.clone.table_ref) | copy-start | bytes 1572868
  19.9 10.5 %copy-start.9 = (f32[128,256]{1,0:T(8,128)S(1)}, f32[128,256]{1,0:T(8,128)}, u32[]{:S(2)}) copy-start(f32[128,256]{1,0:T(8,128)} %constant.11.clone.twist_ref) | copy-start | bytes 393220
  45.8 11.4 %copy-start.10 = (f32[16,16,128]{2,1,0:T(8,128)S(1)}, f32[16,16,128]{2,1,0:T(8,128)}, u32[]{:S(2)}) copy-start(f32[16,16,128]{2,1,0:T(8,128)} %constant.13.clone.weight_ref) | copy-start | bytes 393220
  58.9 23.9 %copy-start.2 = (s32[4096]{0:T(1024)S(1)}, s32[4096]{0:T(1024)}, u32[]{:S(2)}) copy-start(s32[4096]{0:T(1024)} %param.15) | copy-start | bytes 49156
  58.9 23.9 %copy-start.8 = (bf16[512,192]{1,0:T(8,128)(2,1)S(1)}, bf16[512,192]{1,0:T(8,128)(2,1)}, u32[]{:S(2)}) copy-start(bf16[512,192]{1,0:T(8,128)(2,1)} %constant.14.clone.table_ref) | copy-start | bytes 589828
  58.9 23.9 %all-to-all-start.3 = ((f32[16,9,2,256]{3,2,1,0:T(2,128)}), f32[16,9,2,256]{3,2,1,0:T(2,128)S(1)}, u32[]{:S(2)}, u32[]{:S(2)}) async-start(f32[16,9,2,256]{3,2,1,0:T(2,128)} %inverse.1), calls=%async_computation.3 | async-start | bytes 589824 | tf_op jit(solution)/shard_map/all_to_all | solution.py:563
  64.1 11.5 %collective-permute-start = (f32[8,256]{1,0:T(8,128)S(1)}, f32[8,256]{1,0:T(8,128)S(1)}, u32[]{:S(2)}, u32[]{:S(2)}) collective-permute-start(f32[8,256]{1,0:T(8,128)S(1)} %get-tuple-element.42), channel_id=1, source_target_pairs={{0,64},{64,0},{128,192},{192,128},{256,320},{320,256},{384,448},{4... | collective-permute-start | bytes 24584 | tf_op jit(solution)/shard_map/ppermute | solution.py:564
  66.1 10.3 %collective-permute-start.1 = (f32[8,256]{1,0:T(8,128)S(1)}, f32[8,256]{1,0:T(8,128)S(1)}, u32[]{:S(2)}, u32[]{:S(2)}) collective-permute-start(f32[8,256]{1,0:T(8,128)S(1)} %get-tuple-element.43), channel_id=1, source_target_pairs={{0,448},{64,128},{128,64},{192,256},{256,192},{320,384},{384,320},... | collective-permute-start | bytes 24584 | tf_op jit(solution)/shard_map/ppermute | solution.py:565
